TPU v7x, 32 devices: a whole 2x2x4 slice. The times are simulated.
32 devices in a mesh: dp: 8 (over y, x, core), tensor: 4 (over z).
Axes of the slice: x: 2, y: 2, z: 4, core: 2. Of those that a mesh axis runs over, the one named last changes fastest.
Arguments:
- hidden: bfloat16 [1536, 16384], P('dp', 'tensor'), may hold values from -6 to 6
- cotangent: bfloat16 [1536, 16384], P('dp', 'tensor'), may hold values from -6 to 6
- blocks: bfloat16 [7, 64, 256, 256], P(None, 'tensor', 'dp'), may hold values from -0.125 to 0.125
- low_left: bfloat16 [16384, 128], P('tensor'), may hold values from -0.046875 to 0.046875
- low_right: bfloat16 [128, 16384], P(None, 'tensor'), may hold values from -0.5 to 0.5
Outputs:
- mixed_rows: bfloat16 [1536, 16384], P('dp', 'tensor')
- grad_hidden: bfloat16 [1536, 16384], P('dp', 'tensor')
- grad_blocks: float32 [7, 64, 256, 256], P(None, 'tensor', 'dp')
- grad_left: float32 [16384, 128], P('tensor')
- grad_right: float32 [128, 16384], P(None, 'tensor')
All inputs are finite; a program needn't handle non-finite values.
Results may differ from a plain program's by a relative error of at most 0.0095.
Values may be sent and summed in bfloat16 or wider, within the bound.
No kernel may reach another device: no remote copies, remote signals or barrier semaphores. Data moves between devices by JAX's collectives and lax.ppermute only.
A program may use at most 256 MiB of HBM per device.

v0:
```python
import jax
import jax.numpy as jnp
from jax import lax
from jax.sharding import PartitionSpec as P


def partner(value, axis, bit):
    return lax.ppermute(value, axis, [(i, i ^ 1 << bit) for i in range(lax.axis_size(axis))])


def flip_blocks(values, distance):
    array_shape = values.shape
    grouped = values.reshape(
        array_shape[:-2] + (array_shape[-2] // (2 * distance), 2, distance, array_shape[-1])
    )
    return grouped[..., ::-1, :, :].reshape(array_shape)


def per_device(hidden, cotangent, blocks, low_left, low_right):
    tok_rows, ff_local = hidden.shape
    blocks_here = blocks.shape[1]
    block_size = blocks.shape[3]
    local_bits = blocks_here.bit_length() - 1
    cross_bits = lax.axis_size("tensor").bit_length() - 1
    grad_scale = jnp.float32(1.0) / jnp.sqrt(jnp.float32(tok_rows * lax.axis_size("dp")))
    weights = lax.all_gather(blocks, "dp", axis=2, tiled=True)
    inputs_b = hidden.reshape(tok_rows, blocks_here, block_size)
    local_inputs = [inputs_b] + [
        flip_blocks(inputs_b, 2**level_idx) for level_idx in range(local_bits)
    ]
    remote_inputs = [partner(inputs_b, "tensor", bit_idx) for bit_idx in range(cross_bits)]
    stacked_in = jnp.stack(local_inputs + remote_inputs)
    mixed_blocks = jnp.einsum(
        "ktnb,knbc->tnc", stacked_in, weights, preferred_element_type=jnp.float32
    )
    partial_in = jnp.dot(hidden, low_left, preferred_element_type=jnp.float32)
    factor_b = lax.psum(partial_in, "tensor").astype(jnp.bfloat16)
    low_term = jnp.dot(factor_b, low_right, preferred_element_type=jnp.float32)
    mixed_rows = (mixed_blocks.reshape(tok_rows, ff_local) + low_term).astype(jnp.bfloat16)
    cot_b = cotangent.reshape(tok_rows, blocks_here, block_size)
    block_terms = (
        jnp.einsum("ktnb,tnc->knbc", stacked_in, cot_b, preferred_element_type=jnp.float32)
        * grad_scale
    )
    grad_blocks = lax.psum_scatter(
        block_terms.astype(jnp.bfloat16), "dp", scatter_dimension=2, tiled=True
    ).astype(jnp.float32)
    products = jnp.einsum("tnc,knbc->ktnb", cot_b, weights, preferred_element_type=jnp.float32)
    grad_in = products[0]
    for level_idx in range(local_bits):
        grad_in = grad_in + flip_blocks(products[1 + level_idx], 2**level_idx)
    for bit_idx in range(cross_bits):
        sent_terms = products[1 + local_bits + bit_idx]
        grad_in = grad_in + partner(sent_terms, "tensor", bit_idx)
    partial_back = jnp.einsum("tf,rf->tr", cotangent, low_right, preferred_element_type=jnp.float32)
    back_b = lax.psum(partial_back, "tensor").astype(jnp.bfloat16)
    low_back = jnp.einsum("tr,fr->tf", back_b, low_left, preferred_element_type=jnp.float32)
    grad_hidden = (grad_in.reshape(tok_rows, ff_local) + low_back).astype(jnp.bfloat16)
    part_left = (
        jnp.einsum("tf,tr->fr", hidden, back_b, preferred_element_type=jnp.float32) * grad_scale
    )
    part_right = (
        jnp.einsum("tr,tf->rf", factor_b, cotangent, preferred_element_type=jnp.float32)
        * grad_scale
    )
    grad_left, grad_right = lax.psum((part_left, part_right), "dp")
    return (mixed_rows, grad_hidden, grad_blocks, grad_left, grad_right)


def solution(mesh):
    placed = (
        P("dp", "tensor"),
        P("dp", "tensor"),
        P(None, "tensor", "dp", None),
        P("tensor", None),
        P(None, "tensor"),
    )
    return jax.shard_map(
        per_device,
        mesh=mesh,
        in_specs=placed,
        out_specs=(
            P("dp", "tensor"),
            P("dp", "tensor"),
            P(None, "tensor", "dp", None),
            P("tensor", None),
            P(None, "tensor"),
        ),
        check_vma=False,
    )
```

profile of v0, /device:TPU:0, one launch (start us, length us, event | category | flops | bytes accessed | tf_op | source)
XLA Modules:
  0.0 353.8 jit_solution(5965905838084927043)
XLA Ops:
  7.2 3.0 copy.29
  10.4 1.3 copy.59
  11.7 4.1 %collective-permute-start.1 = (bf16[192,16,256]{2,0,1:T(8,128)(2,1)}, bf16[192,16,256]{2,0,1:T(8,128)(2,1)}, u32[]{:S(2)}, u32[]{:S(2)}) collective-permute-start(bf16[192,16,256]{2,0,1:T(8,128)(2,1)} %bitcast.91), channel_id=1, source_target_pairs={{0,2},{1,3},{2,0},{3,1},{4,6},{5,7},{6,4},{7,5},{8,10},{9,11},{10,... | collective-permute-start | bytes 4718600 | tf_op jit(solution)/shard_map/ppermute | solution.py:8
  15.7 1.6 collective-permute-start
  17.3 0.6 fusion.18
  17.9 0.6 fusion.19
  18.4 82.4 %all-reduce.6 = (bf16[192,128]{1,0:T(8,128)(2,1)S(1)}, bf16[192,128]{1,0:T(8,128)(2,1)S(1)}) all-reduce(f32[192,128]{1,0:T(8,128)S(1)} %fusion.18, f32[192,128]{1,0:T(8,128)S(1)} %fusion.19), channel_id=1, replica_groups=mesh['dp'=8,'tensor'=4] {'tensor'}, use_global_device_ids=true, to_apply=%region_0.0 | all-reduce | flops 49152 | bytes 294912 | tf_op jit(solution)/shard_map/psum | solution.py:37
  100.9 3.2 convolution_multiply_fusion
  104.1 1.8 fusion.2
  106.1 2.4 reshape_reshape.14
  108.5 2.4 reshape_reshape.13
  110.9 2.4 reshape_reshape.12
  113.7 1.1 copy-done.4
  114.8 0.6 copy.25
  115.4 1.3 rev.27
  116.7 3.2 copy.24
  119.9 2.8 rev.26
  122.7 1.7 copy.23
  124.4 2.7 rev.25
  127.1 3.3 copy.22
  130.3 2.7 rev.24
  133.0 1.7 copy_dynamic-update-slice_fusion
  134.7 1.3 constant_dynamic-update-slice_fusion.3
  136.0 1.2 constant_dynamic-update-slice_fusion.2
  137.3 1.3 constant_dynamic-update-slice_fusion.1
  138.5 1.3 constant_dynamic-update-slice_fusion
  140.3 2.8 bitcast_dynamic-update-slice_fusion.1
  143.1 2.7 bitcast_dynamic-update-slice_fusion
  145.8 11.5 %fusion = bf16[7,16,256,256]{3,2,0,1:T(8,128)(2,1)} fusion(bf16[7,192,16,256]{3,1,0,2:T(8,128)(2,1)} %bitcast_dynamic-update-slice_fusion, bf16[192,16,256,1]{2,1,0,3:T(8,128)(2,1)S(1)} %bitcast.103), kind=kOutput, calls=%fused_computation.1 | convolution fusion | flops 2833252352 | bytes 27262976 | tf_op jit(solution)/shard_map/ktnb,tnc->knbc/dot_general | solution.py:42
  157.4 13.9 %convolution_bitcast_fusion = f32[7,192,16,256]{3,1,0,2:T(8,128)} fusion(bf16[7,16,256,256]{3,2,0,1:T(8,128)(2,1)} %all-gather.2.cloned.1.call-done, bf16[192,16,256,1]{2,1,0,3:T(8,128)(2,1)S(1)} %bitcast.104), kind=kOutput, calls=%fused_computation.2 | convolution fusion | flops 2818572288 | bytes 38273024 | tf_op jit(solution)/shard_map/tnc,knbc->ktnb/dot_general | solution.py:48
  171.2 13.8 %fusion.17 = (f32[1,192,16,256]{3,1,0,2:T(8,128)}, f32[192,16,256]{2,0,1:T(8,128)}, f32[1,192,16,256]{3,1,0,2:T(8,128)}, f32[1,192,16,256]{3,1,0,2:T(8,128)}, f3...) fusion(f32[7,192,16,256]{3,1,0,2:T(8,128)} %convolution_bitcast_fusion), kind=kLoop, calls=%fused_computation.35 | loop fusion | bytes 37748736 | tf_op jit(solution)/shard_map/slice | solution.py:51
  185.0 0.8 collective-permute-start.3
  185.8 2.2 fusion.20
  188.1 2.9 copy.37
  190.9 102.4 %reduce-scatter.2.cloned.1.call-done = bf16[7,16,32,256]{3,2,0,1:T(8,128)(2,1)} async-done(((bf16[7,16,256,256]{3,2,0,1:T(8,128)(2,1)}), bf16[7,16,32,256]{3,2,0,1:T(8,128)(2,1)}) %reduce-scatter.2.cloned.1.call-update) | async-done | bytes 1835024 | tf_op jit(solution)/shard_map/reduce_scatter | solution.py:45
  293.3 3.8 %copy.36 = f32[7,16,32,256]{3,2,1,0:T(8,128)} copy(bf16[7,16,32,256]{3,2,0,1:T(8,128)(2,1)} %reduce-scatter.2.cloned.1.call-done) | data formatting | bytes 5505024
  297.1 12.5 %convolution_bitcast_fusion.1 = f32[16,24,8,256]{3,2,1,0:T(8,128)S(1)} fusion(bf16[7,192,16,256]{3,1,0,2:T(8,128)(2,1)} %bitcast_dynamic-update-slice_fusion, bf16[7,16,256,256]{3,2,0,1:T(8,128)(2,1)} %all-gather.2.cloned.1.call-done), kind=kOutput, calls=%fused_computation.19 | convolution fusion | flops 2818572288 | bytes 28835840 | tf_op jit(solution)/shard_map/ktnb,knbc->tnc/dot_general | solution.py:33
  309.6 2.1 copy.48
  311.7 3.8 %rev.28 = f32[192,8,2,1,256]{4,0,2,1,3:T(8,128)} reverse(f32[192,8,2,1,256]{4,0,2,1,3:T(8,128)} %bitcast.100), dimensions={2} | reverse | bytes 6291456 | tf_op jit(solution)/shard_map/rev | solution.py:16
  315.5 3.9 %rev.31 = f32[192,1,2,8,256]{4,0,3,2,1:T(8,128)} reverse(f32[192,1,2,8,256]{4,0,3,2,1:T(8,128)} %bitcast.99), dimensions={2} | reverse | bytes 6291456 | tf_op jit(solution)/shard_map/rev | solution.py:16
  319.3 3.9 %rev.30 = f32[192,2,2,4,256]{4,0,3,2,1:T(8,128)} reverse(f32[192,2,2,4,256]{4,0,3,2,1:T(8,128)} %bitcast.98), dimensions={2} | reverse | bytes 6291456 | tf_op jit(solution)/shard_map/rev | solution.py:16
  323.2 4.0 %rev.29 = f32[192,4,2,2,256]{4,0,3,2,1:T(8,128)} reverse(f32[192,4,2,2,256]{4,0,3,2,1:T(8,128)} %bitcast.97), dimensions={2} | reverse | bytes 6291456 | tf_op jit(solution)/shard_map/rev | solution.py:16
  327.2 3.7 %fusion.1 = bf16[192,4096]{1,0:T(8,128)(2,1)} fusion(f32[192,4096]{1,0:T(8,128)} %bitcast.101, bf16[128,4096]{1,0:T(8,128)(2,1)S(1)} %copy-done.14, bf16[192,128]{1,0:T(8,128)(2,1)S(1)} %get-tuple-element.17), kind=kOutput, calls=%fused_computation.4 | convolution fusion | flops 202899456 | bytes 5816320 | tf_op jit(solution)/shard_map/dot_general | solution.py:38
  331.0 10.0 %fusion.9 = f32[16,24,8,256]{3,2,1,0:T(8,128)} fusion(f32[192,16,256]{2,0,1:T(8,128)} %collective-permute-done.3, f32[192,16,256]{2,0,1:T(8,128)} %collective-permute-done.2, f32[7,192,16,256]{3,1,0,2:T(8,128)} %convolution_bitcast_fusion, f32[192,1,2,8,256]{4,0,3,2,1:T(8,128)} %rev.31, f32[192,2,2,4,256]{4,0,3,2,1:T(8,128)} %rev.30, ...), kind=kLoop, calls=%fused_computation.17 | loop fusion | flops 4718592 | bytes 25165824
  340.9 2.4 copy.49
  343.8 1.5 add_convert_fusion
  345.3 0.6 copy-done.15
  345.9 1.3 copy.72
  (45 shorter events, 1.7 us)
Async XLA Ops:
  7.2 10.1 %copy-start = (bf16[4096,128]{1,0:T(8,128)(2,1)S(1)}, bf16[4096,128]{1,0:T(8,128)(2,1)}, u32[]{:S(2)}) copy-start(bf16[4096,128]{1,0:T(8,128)(2,1)} %param.8) | copy-start | bytes 3145732
  7.2 3.2 copy-start.1
  7.2 150.2 %all-gather.2.cloned.1.call-start = ((), (), s32[]{:S(2)}) async-start(), calls=%async_computation.1 | async-start | bytes 16515072 | tf_op jit(solution)/shard_map/all_gather | solution.py:26
  10.3 177.8 %all-reduce.5.cloned.1.call-start = ((), (), s32[]{:S(2)}) async-start(), calls=%async_computation.3 | async-start | bytes 8388608 | tf_op jit(solution)/shard_map/psum | solution.py:66
  10.3 7.5 %copy-start.2 = (bf16[192,4096]{1,0:T(8,128)(2,1)S(1)}, bf16[192,4096]{1,0:T(8,128)(2,1)}, u32[]{:S(2)}) copy-start(bf16[192,4096]{1,0:T(8,128)(2,1)} %param.6) | copy-start | bytes 4718596
  10.4 7.5 %copy-start.13 = (bf16[128,4096]{1,0:T(8,128)(2,1)S(1)}, bf16[128,4096]{1,0:T(8,128)(2,1)}, u32[]{:S(2)}) copy-start(bf16[128,4096]{1,0:T(8,128)(2,1)} %param.9) | copy-start | bytes 3145732
  11.7 131.4 %collective-permute-start.1 = (bf16[192,16,256]{2,0,1:T(8,128)(2,1)}, bf16[192,16,256]{2,0,1:T(8,128)(2,1)}, u32[]{:S(2)}, u32[]{:S(2)}) collective-permute-start(bf16[192,16,256]{2,0,1:T(8,128)(2,1)} %bitcast.91), channel_id=1, source_target_pairs={{0,2},{1,3},{2,0},{3,1},{4,6},{5,7},{6,4},{7,5},{8,10},{9,11},{10,... | collective-permute-start | bytes 4718600 | tf_op jit(solution)/shard_map/ppermute | solution.py:8
  15.7 124.6 %collective-permute-start = (bf16[192,16,256]{2,0,1:T(8,128)(2,1)}, bf16[192,16,256]{2,0,1:T(8,128)(2,1)}, u32[]{:S(2)}, u32[]{:S(2)}) collective-permute-start(bf16[192,16,256]{2,0,1:T(8,128)(2,1)} %bitcast.91), channel_id=1, source_target_pairs={{0,1},{1,0},{2,3},{3,2},{4,5},{5,4},{6,7},{7,6},{8,9},{9,8},{10,11... | collective-permute-start | bytes 4718600 | tf_op jit(solution)/shard_map/ppermute | solution.py:8
  105.9 187.4 %reduce-scatter.2.cloned.1.call-start = ((), (), s32[]{:S(2)}) async-start(), calls=%async_computation.2 | async-start | bytes 16515072 | tf_op jit(solution)/shard_map/reduce_scatter | solution.py:45
  113.7 1.1 copy-start.4
  116.7 6.0 %copy-start.11 = (bf16[192,4,2,2,256]{4,3,2,1,0:T(2,128)(2,1)S(1)}, bf16[192,4,2,2,256]{4,3,2,1,0:T(2,128)(2,1)}, u32[]{:S(2)}) copy-start(bf16[192,4,2,2,256]{4,3,2,1,0:T(2,128)(2,1)} %reshape_reshape.13) | copy-start | bytes 4718596
  127.1 6.0 %copy-start.5 = (bf16[24,8,16,256]{3,2,1,0:T(8,128)(2,1)S(1)}, bf16[24,8,16,256]{3,2,1,0:T(8,128)(2,1)}, u32[]{:S(2)}) copy-start(bf16[24,8,16,256]{3,2,1,0:T(8,128)(2,1)} %copy-done.4) | copy-start | bytes 4718596
  133.0 1.7 copy-start.12
  133.0 3.0 copy-start.10
  134.7 2.5 copy-start.9
  136.0 2.5 copy-start.8
  137.3 2.6 copy-start.3
  185.0 146.0 %collective-permute-start.3 = (f32[192,16,256]{2,0,1:T(8,128)}, f32[192,16,256]{2,0,1:T(8,128)}, u32[]{:S(2)}, u32[]{:S(2)}) collective-permute-start(f32[192,16,256]{2,0,1:T(8,128)} %get-tuple-element.20), channel_id=1, source_target_pairs={{0,2},{1,3},{2,0},{3,1},{4,6},{5,7},{6,4},{7,5},{8,10},{9,11},{10,... | collective-permute-start | bytes 9437192 | tf_op jit(solution)/shard_map/ppermute | solution.py:8
  185.8 145.1 %collective-permute-start.2 = (f32[192,16,256]{2,0,1:T(8,128)}, f32[192,16,256]{2,0,1:T(8,128)}, u32[]{:S(2)}, u32[]{:S(2)}) collective-permute-start(f32[192,16,256]{2,0,1:T(8,128)} %get-tuple-element.24), channel_id=1, source_target_pairs={{0,1},{1,0},{2,3},{3,2},{4,5},{5,4},{6,7},{7,6},{8,9},{9,8},{10,11... | collective-permute-start | bytes 9437192 | tf_op jit(solution)/shard_map/ppermute | solution.py:8
  323.2 4.0 %copy-start.14 = (bf16[128,4096]{1,0:T(8,128)(2,1)S(1)}, bf16[128,4096]{1,0:T(8,128)(2,1)}, u32[]{:S(2)}) copy-start(bf16[128,4096]{1,0:T(8,128)(2,1)} %param.9) | copy-start | bytes 3145732
  327.2 3.8 %copy-start.6 = (f32[192,8,2,1,256]{4,0,2,1,3:T(8,128)S(1)}, f32[192,8,2,1,256]{4,0,2,1,3:T(8,128)}, u32[]{:S(2)}) copy-start(f32[192,8,2,1,256]{4,0,2,1,3:T(8,128)} %rev.28) | copy-start | bytes 9437188
  340.9 2.8 copy-start.7
  343.8 2.2 copy-start.15
Sparse Core Ops, SparseCore 0:
  10.5 83.6 all-gather.1
  106.0 79.6 all-reduce.4
  189.7 103.6 reduce-scatter.1
where the time goes:
time: 354 us
  waiting for transfers between devices  102 us (29%)
  local copies, waits for them, and re-layouts  86.7 us (24%)
  blocking collectives  82.4 us (23%)
  matrix products  50 us (14%)
  between operations  13.9 us (4%)
  other arithmetic  11.5 us (3%)
  starting transfers between devices  6.77 us (2%)
    reduce_scatter x1, waiting for transfers between devices, per_device(): lax.psum_scatter(block_terms.astype(jnp.bfloat16), 'dp', scatter_dimensio...  102 us
    psum x1, blocking collectives, per_device(): factor_b = lax.psum(partial_in, 'tensor').astype(jnp.bfloat16)  82.4 us
    rev x8, local copies, waits for them, and re-layouts, flip_blocks(): return grouped[..., ::-1, :, :].reshape(array_shape)  24.9 us
    unnamed x44, local copies, waits for them, and re-layouts  23.7 us
    another operation x7, local copies, waits for them, and re-layouts, flip_blocks(): values.reshape(array_shape[:-2] + (array_shape[-2] // (2 * distance), 2,...  15.8 us
    dot_general x1, matrix products, per_device(): jnp.einsum('tnc,knbc->ktnb', cot_b, weights, preferred_element_type=jnp.f...  13.9 us
    slice x1, local copies, waits for them, and re-layouts, per_device(): grad_in = grad_in + flip_blocks(products[1 + level_idx], 2 ** level_idx)  13.8 us
    dot_general x1, matrix products, per_device(): jnp.einsum('ktnb,knbc->tnc', stacked_in, weights, preferred_element_type=...  12.5 us
  transfers between devices with their start and end apart: 7, of which 1 were waited for; matrix products, arithmetic and copies ran while one was open for 36% of the time, Pallas kernels for 0%

commit v1 on v0

v1 whole, which is shorter than its diff:
```python
import functools

import jax
import jax.numpy as jnp
from jax import lax
from jax.experimental import pallas as pl
from jax.experimental.pallas import tpu as pltpu
from jax.sharding import PartitionSpec as P

F32 = jnp.float32
BF16 = jnp.bfloat16
VMEM_LIMIT = 40 * 1024 * 1024


def swap(value, axis, mask):
    return lax.ppermute(value, axis, [(i, i ^ mask) for i in range(lax.axis_size(axis))])


def params():
    return pltpu.CompilerParams(
        dimension_semantics=("arbitrary",), vmem_limit_bytes=VMEM_LIMIT
    )


def aligned(index, size):
    return pl.ds(pl.multiple_of(index * size, size), size)


def grads_kernel(levels, shards, scale, pos_ref, cot_ref, *refs):
    n_src = 1 + max(src for src, _ in levels)
    sources, (keep_ref, send_ref, tmp_ref) = refs[:n_src], refs[n_src:]
    block = cot_ref.shape[1]
    rows = block // shards
    j = pl.program_id(0)
    pos = pos_ref[0]
    cot = cot_ref[...]
    for k, (src, distance) in enumerate(levels):
        values = sources[src][:, aligned(j ^ distance, block)]
        term = lax.dot_general(
            values, cot, (((0,), (0,)), ((), ())), preferred_element_type=F32
        )
        tmp_ref[k] = term * scale
        for m in range(shards):
            part = tmp_ref[k, aligned(pos ^ m, rows), :].astype(BF16)
            (send_ref if m & 1 else keep_ref)[m >> 1, k, 0] = part


def block_grads(pos, cot, sources, levels, n_blocks, shards, scale):
    tok, ff = cot.shape
    block = ff // n_blocks
    rows = block // shards
    part = jax.ShapeDtypeStruct((shards // 2, len(levels), n_blocks, rows, block), BF16)
    part_spec = pl.BlockSpec(
        (shards // 2, len(levels), 1, rows, block), lambda j, *_: (0, 0, j, 0, 0)
    )
    return pl.pallas_call(
        functools.partial(grads_kernel, levels, shards, scale),
        grid_spec=pltpu.PrefetchScalarGridSpec(
            num_scalar_prefetch=1,
            grid=(n_blocks,),
            in_specs=[pl.BlockSpec((tok, block), lambda j, *_: (0, j))]
            + [pl.BlockSpec((tok, ff), lambda j, *_: (0, 0)) for _ in sources],
            out_specs=[part_spec, part_spec],
            scratch_shapes=[pltpu.VMEM((len(levels), block, block), F32)],
        ),
        out_shape=[part, part],
        compiler_params=params(),
        cost_estimate=pl.CostEstimate(
            flops=2 * tok * ff * block * len(levels),
            bytes_accessed=2 * tok * ff * (1 + len(sources)) + 2 * len(levels) * ff * block,
            transcendentals=0,
        ),
    )(pos, cot, *sources)


def assemble(pos, pieces, refs, w_ref, k):
    for (m, columns, _), ref in zip(pieces, refs):
        w_ref[k, pos ^ m, :, columns] = ref[k, 0]
    shards, rows, block = w_ref.shape[1:]
    return w_ref[k].reshape(shards * rows, block)


def piece_specs(pieces):
    return [
        pl.BlockSpec((p.shape[0], 1) + p.shape[2:], lambda j, *_: (0, j, 0, 0))
        for _, _, p in pieces
    ]


def w_scratch(pieces, n_levels, shards):
    own = pieces[0][2]
    return pltpu.VMEM((n_levels, shards, own.shape[2], own.shape[3]), BF16)


NT = (((1,), (1,)), ((), ()))


def local_kernel(
    pieces, distances, pos_ref, hid_ref, cot_ref, fac_ref, back_ref, left_ref, right_ref, *refs
):
    w_refs, (mixed_ref, grad_ref, w_ref) = refs[: len(pieces)], refs[len(pieces) :]
    block = cot_ref.shape[1]
    j = pl.program_id(0)
    pos = pos_ref[0]

    @pl.when(j == 0)
    def _():
        grad_ref[...] = jnp.zeros_like(grad_ref)

    cot = cot_ref[...]
    mixed = jnp.dot(fac_ref[...], right_ref[...], preferred_element_type=F32)
    for k, distance in enumerate(distances):
        weight = assemble(pos, pieces, w_refs, w_ref, k)
        there = aligned(j ^ distance, block)
        mixed += jnp.dot(hid_ref[:, there], weight, preferred_element_type=F32)
        term = lax.dot_general(cot, weight, NT, preferred_element_type=F32)
        if distance == 0:
            term += lax.dot_general(back_ref[...], left_ref[...], NT, preferred_element_type=F32)
        grad_ref[:, there] += term
    mixed_ref[...] = mixed


def local_terms(pos, hidden, cot, factor, back, low_left, low_right, pieces, distances, n_blocks, shards):
    tok, ff = hidden.shape
    block = ff // n_blocks
    rank = factor.shape[1]
    column = pl.BlockSpec((tok, block), lambda j, *_: (0, j))
    whole = pl.BlockSpec((tok, ff), lambda j, *_: (0, 0))
    low = pl.BlockSpec((tok, rank), lambda j, *_: (0, 0))
    out = jax.ShapeDtypeStruct((tok, ff), F32)
    return pl.pallas_call(
        functools.partial(local_kernel, pieces, distances),
        grid_spec=pltpu.PrefetchScalarGridSpec(
            num_scalar_prefetch=1,
            grid=(n_blocks,),
            in_specs=[
                whole,
                column,
                low,
                low,
                pl.BlockSpec((block, rank), lambda j, *_: (j, 0)),
                pl.BlockSpec((rank, block), lambda j, *_: (0, j)),
            ]
            + piece_specs(pieces),
            out_specs=[column, whole],
            scratch_shapes=[w_scratch(pieces, len(distances), shards)],
        ),
        out_shape=[out, out],
        compiler_params=params(),
        cost_estimate=pl.CostEstimate(
            flops=4 * tok * ff * block * len(distances),
            bytes_accessed=12 * tok * ff + 2 * len(distances) * ff * block,
            transcendentals=0,
        ),
    )(pos, hidden, cot, factor, back, low_left, low_right, *[p for _, _, p in pieces])


def back_kernel(pieces, n_levels, pos_ref, cot_ref, *refs):
    w_refs, (out_refs, w_ref) = refs[: len(pieces)], (refs[len(pieces) : -1], refs[-1])
    for k in range(n_levels):
        weight = assemble(pos_ref[0], pieces, w_refs, w_ref, k)
        term = lax.dot_general(cot_ref[...], weight, NT, preferred_element_type=F32)
        out_refs[k][...] = term.astype(BF16)


def back_terms(pos, cot, pieces, n_levels, n_blocks, shards):
    tok, ff = cot.shape
    block = ff // n_blocks
    column = pl.BlockSpec((tok, block), lambda j, *_: (0, j))
    return pl.pallas_call(
        functools.partial(back_kernel, pieces, n_levels),
        grid_spec=pltpu.PrefetchScalarGridSpec(
            num_scalar_prefetch=1,
            grid=(n_blocks,),
            in_specs=[column] + piece_specs(pieces),
            out_specs=[column] * n_levels,
            scratch_shapes=[w_scratch(pieces, n_levels, shards)],
        ),
        out_shape=[jax.ShapeDtypeStruct((tok, ff), BF16)] * n_levels,
        compiler_params=params(),
        cost_estimate=pl.CostEstimate(
            flops=2 * tok * ff * block * n_levels,
            bytes_accessed=2 * tok * ff * (1 + n_levels) + 2 * n_levels * ff * block,
            transcendentals=0,
        ),
    )(pos, cot, *[p for _, _, p in pieces])


def cross_kernel(pieces, n_levels, pos_ref, mixed_ref, *refs):
    sources = refs[:n_levels]
    w_refs, (out_ref, w_ref) = refs[n_levels:-2], refs[-2:]
    mixed = mixed_ref[...]
    for k in range(n_levels):
        weight = assemble(pos_ref[0], pieces, w_refs, w_ref, k)
        mixed += jnp.dot(sources[k][...], weight, preferred_element_type=F32)
    out_ref[...] = mixed.astype(BF16)


def cross_terms(pos, mixed, sources, pieces, n_blocks, shards):
    tok, ff = mixed.shape
    block = ff // n_blocks
    n_levels = len(sources)
    column = pl.BlockSpec((tok, block), lambda j, *_: (0, j))
    return pl.pallas_call(
        functools.partial(cross_kernel, pieces, n_levels),
        grid_spec=pltpu.PrefetchScalarGridSpec(
            num_scalar_prefetch=1,
            grid=(n_blocks,),
            in_specs=[column] * (1 + n_levels) + piece_specs(pieces),
            out_specs=column,
            scratch_shapes=[w_scratch(pieces, n_levels, shards)],
        ),
        out_shape=jax.ShapeDtypeStruct((tok, ff), BF16),
        compiler_params=params(),
        cost_estimate=pl.CostEstimate(
            flops=2 * tok * ff * block * n_levels,
            bytes_accessed=2 * tok * ff * (3 + n_levels) + 2 * n_levels * ff * block,
            transcendentals=0,
        ),
    )(pos, mixed, *sources, *[p for _, _, p in pieces])


def highest(mask):
    return 1 << mask.bit_length() - 1


def gather_pieces(own, shards):
    half = own.shape[-1] // 2
    low, high, full = slice(0, half), slice(half, None), slice(None)
    far = {0: [(full, own)]}
    for mask in range(2, shards, 2):
        last_a, last_b = highest(mask), mask & -mask
        if last_a == last_b:
            far[mask] = [(full, swap(own, "dp", mask))]
            continue
        far[mask] = []
        for last, columns in ((last_a, low), (last_b, high)):
            for held, value in far[mask ^ last]:
                if held == full:
                    value = value[..., columns]
                elif held != columns:
                    continue
                far[mask].append((columns, swap(value, "dp", last)))
    pieces = [(mask, columns, value) for mask in far for columns, value in far[mask]]
    return pieces + [(mask | 1, columns, swap(value, "dp", 1)) for mask, columns, value in pieces]


def scatter_sum(keep, send, shards):
    arrived = swap(send, "dp", 1)
    half = keep.shape[-1] // 2
    bits = [bit for bit in range(shards.bit_length() - 2)]
    totals = []
    for columns, order in ((slice(0, half), bits), (slice(half, None), bits[::-1])):
        terms = {
            q: [keep[q][..., columns], arrived[q][..., columns]] for q in range(shards // 2)
        }
        for bit in order:
            got = {}
            for q in sorted(terms):
                if q >> bit & 1:
                    total = sum(t.astype(F32) for t in terms[q]).astype(BF16)
                    got[q ^ 1 << bit] = swap(total, "dp", 2 << bit)
            terms = {q: terms[q] + [got[q]] for q in terms if not q >> bit & 1}
        totals.append(sum(t.astype(F32) for t in terms[0]))
    return jnp.concatenate(totals, axis=-1)


def per_device(hidden, cotangent, blocks, low_left, low_right):
    tok, ff = hidden.shape
    n_blocks = blocks.shape[1]
    shards = lax.axis_size("dp")
    local_bits = n_blocks.bit_length() - 1
    cross_bits = lax.axis_size("tensor").bit_length() - 1
    n_local = 1 + local_bits
    scale = 1.0 / (tok * shards) ** 0.5
    pos = lax.axis_index("dp").astype(jnp.int32).reshape(1)

    factors = jnp.concatenate(
        [
            jnp.dot(hidden, low_left, preferred_element_type=F32),
            lax.dot_general(cotangent, low_right, NT, preferred_element_type=F32),
        ],
        axis=1,
    )
    for bit in range(cross_bits):
        factors = factors + swap(factors, "tensor", 1 << bit)
    factors = factors.astype(BF16)
    rank = low_left.shape[1]
    factor, back = factors[:, :rank], factors[:, rank:]

    remote = [swap(hidden, "tensor", 1 << bit) for bit in range(cross_bits)]
    cross_pieces = gather_pieces(blocks[n_local:], shards)
    local_pieces = gather_pieces(blocks[:n_local], shards)

    distances = [0] + [1 << level for level in range(local_bits)]
    keep, send = block_grads(
        pos, cotangent, [hidden], [(0, d) for d in distances], n_blocks, shards, scale
    )
    grads_local = scatter_sum(keep, send, shards)

    sent = back_terms(pos, cotangent, cross_pieces, cross_bits, n_blocks, shards)
    returned = [swap(term, "tensor", 1 << bit) for bit, term in enumerate(sent)]

    mixed, grad_in = local_terms(
        pos, hidden, cotangent, factor, back, low_left, low_right,
        local_pieces, distances, n_blocks, shards,
    )
    mixed_rows = cross_terms(pos, mixed, remote, cross_pieces, n_blocks, shards)

    keep, send = block_grads(
        pos, cotangent, remote, [(bit, 0) for bit in range(cross_bits)], n_blocks, shards, scale
    )
    grads_cross = scatter_sum(keep, send, shards)
    grad_blocks = jnp.concatenate([grads_local, grads_cross], axis=0)

    part_left = jnp.einsum("tf,tr->fr", hidden, back, preferred_element_type=F32) * scale
    part_right = jnp.einsum("tr,tf->rf", factor, cotangent, preferred_element_type=F32) * scale
    grad_left, grad_right = lax.psum((part_left, part_right), "dp")

    grad_hidden = (grad_in + sum(term.astype(F32) for term in returned)).astype(BF16)
    return (mixed_rows, grad_hidden, grad_blocks, grad_left, grad_right)


def solution(mesh):
    placed = (
        P("dp", "tensor"),
        P("dp", "tensor"),
        P(None, "tensor", "dp", None),
        P("tensor", None),
        P(None, "tensor"),
    )
    return jax.shard_map(
        per_device, mesh=mesh, in_specs=placed, out_specs=placed, check_vma=False
    )
```

time: 354 us -> 387 us (1.093)
  waiting for transfers between devices: 102 us -> 222 us
  blocking collectives: 82.4 us -> 0 us
  Pallas kernels: 0 us -> 54.5 us
  local copies, waits for them, and re-layouts: 86.7 us -> 34.1 us
  matrix products: 50 us -> 4.79 us
  starting transfers between devices: 6.77 us -> 41.2 us
    ppermute x4 -> x38, waiting for transfers between devices: 0.01 us -> 192 us  [swap(): lax.ppermute(value, axis, [(i, i ^ mask) for i in range(lax.axis_size(axi...]
    reduce_scatter x1 -> x0, waiting for transfers between devices: 102 us -> none  [per_device(): lax.psum_scatter(block_terms.astype(jnp.bfloat16), 'dp', scatter_dimensio...]
    psum x1 -> x0, blocking collectives: 82.4 us -> none  [per_device(): factor_b = lax.psum(partial_in, 'tensor').astype(jnp.bfloat16)]
    pallas_call x0 -> x5, Pallas kernels: none -> 54.5 us  [the longest x2 18.6 us: block_grads(): pl.pallas_call(functools.partial(grads_kernel, levels, shards, scale), gr...]
    dot_general x9 -> x4, matrix products: 50 us -> 4.79 us  [the longest x1 1.87 us: per_device(): jnp.einsum('tr,tf->rf', factor, cotangent, preferred_element_type=F32)]
    ppermute x4 -> x38, starting transfers between devices: 6.46 us -> 41.1 us  [swap(): lax.ppermute(value, axis, [(i, i ^ mask) for i in range(lax.axis_size(axi...]
    psum x1, waiting for transfers between devices: 0.01 us -> 29.6 us  [per_device(): grad_left, grad_right = lax.psum((part_left, part_right), 'dp')]
    rev x8 -> x0, local copies, waits for them, and re-layouts: 24.9 us -> none  [flip_blocks(): return grouped[..., ::-1, :, :].reshape(array_shape)]
  transfers between devices with their start and end apart: 7 -> 39, of which waited for: 1 -> 13; matrix products, arithmetic and copies ran while one was open for 36% -> 10% of each run, Pallas kernels for 0% -> 11%
where the time goes in v1:
time: 387 us; the launch traced here: 385 us
  waiting for transfers between devices  222 us (57%)
  Pallas kernels  54.5 us (14%)
  starting transfers between devices  41.2 us (11%)
  local copies, waits for them, and re-layouts  34.1 us (9%)
  between operations  14.6 us (4%)
  other arithmetic  13.7 us (4%)
  matrix products  4.79 us (1%)
    ppermute x38, waiting for transfers between devices, swap(): lax.ppermute(value, axis, [(i, i ^ mask) for i in range(lax.axis_size(axi...  192 us
    ppermute x38, starting transfers between devices, swap(): lax.ppermute(value, axis, [(i, i ^ mask) for i in range(lax.axis_size(axi...  41.1 us
    psum x1, waiting for transfers between devices, per_device(): grad_left, grad_right = lax.psum((part_left, part_right), 'dp')  29.6 us
    pallas_call x2, Pallas kernels, block_grads(): pl.pallas_call(functools.partial(grads_kernel, levels, shards, scale), gr...  18.6 us
    pallas_call x1, Pallas kernels, local_terms(): pl.pallas_call(functools.partial(local_kernel, pieces, distances), grid_s...  16.8 us
    unnamed x110, local copies, waits for them, and re-layouts  15.3 us
    pallas_call x1, Pallas kernels, cross_terms(): pl.pallas_call(functools.partial(cross_kernel, pieces, n_levels), grid_sp...  10.2 us
    pallas_call x1, Pallas kernels, back_terms(): pl.pallas_call(functools.partial(back_kernel, pieces, n_levels), grid_spe...  9.04 us
  transfers between devices with their start and end apart: 39, of which 13 were waited for; matrix products, arithmetic and copies ran while one was open for 10% of the time, Pallas kernels for 11%

profile of v1, /device:TPU:0, one launch (start us, length us, event | category | flops | bytes accessed | tf_op | source)
XLA Modules:
  0.0 384.9 jit_solution(5318354328697278878)
XLA Ops:
  7.2 1.4 copy-done
  8.6 1.4 copy-done.2
  10.0 10.3 %shard_map.95 = (bf16[4,5,16,32,256]{4,3,2,1,0:T(8,128)(2,1)S(1)}, bf16[4,5,16,32,256]{4,3,2,1,0:T(8,128)(2,1)}) custom-call(s32[1]{0:T(128)} %bitcast.pos_ref, bf16[192,4096]{1,0:T(8,128)(2,1)S(1)} %copy-done, bf16[192,4096]{1,0:T(8,128)(2,1)S(1)} %copy-done.2), custom_call_target="tpu_custom_call" | custom-call | flops 2013265920 | bytes 13631488 | tf_op jit(solution)/shard_map/pallas_call | solution.py:56
  20.4 2.3 copy-done.6
  23.1 2.6 collective-permute-start.11
  25.7 2.6 collective-permute-start.12
  30.4 1.5 collective-permute-start.13
  31.9 66.7 %collective-permute-done = f32[192,256]{1,0:T(8,128)S(1)} collective-permute-done((f32[192,256]{1,0:T(8,128)S(1)}, f32[192,256]{1,0:T(8,128)S(1)}, u32[]{:S(2)}, u32[]{:S(2)}) %collective-permute-start) | collective-permute-done | bytes 196640 | tf_op jit(solution)/shard_map/ppermute | solution.py:16
  98.7 2.9 collective-permute-start.1
  101.5 9.0 %collective-permute-done.1 = f32[192,256]{1,0:T(8,128)S(1)} collective-permute-done((f32[192,256]{1,0:T(8,128)S(1)}, f32[192,256]{1,0:T(8,128)S(1)}, u32[]{:S(2)}, u32[]{:S(2)}) %collective-permute-start.1) | collective-permute-done | bytes 196640 | tf_op jit(solution)/shard_map/ppermute | solution.py:16
  110.6 1.5 collective-permute-start.14
  112.1 1.2 slice.186.refs_0_
  113.4 10.1 %collective-permute-done.14.refs_4_.refs_2_ = bf16[2,16,32,256]{3,2,1,0:T(8,128)(2,1)S(1)} collective-permute-done((bf16[2,16,32,256]{3,2,1,0:T(8,128)(2,1)S(1)}, bf16[2,16,32,256]{3,2,1,0:T(8,128)(2,1)S(1)}, u32[]{:S(2)}, u32[]{:S(2)}) %collective-permute-start.14) | collective-permute-done | bytes 524320 | tf_op jit(solution)/shard_map/ppermute | solution.py:16
  123.5 1.3 collective-permute-start.2
  124.8 1.8 fusion
  128.1 1.6 collective-permute-start.15
  130.2 8.2 %shard_map.96 = (bf16[4,2,16,32,256]{4,3,2,1,0:T(8,128)(2,1)S(1)}, bf16[4,2,16,32,256]{4,3,2,1,0:T(8,128)(2,1)}) custom-call(s32[1]{0:T(128)} %bitcast.pos_ref, bf16[192,4096]{1,0:T(8,128)(2,1)S(1)} %copy-done.1, bf16[192,4096]{1,0:T(8,128)(2,1)S(1)} %collective-permute-done.11.refs_0_, bf16[192,4096]{1,0:T(8,128)(2,1)S(1)} %collective-permute-done.12.refs_1_), custom_call_target="tpu_custom_call" | custom-call | flops 805306368 | bytes 8912896 | tf_op jit(solution)/shard_map/pallas_call | solution.py:56
  138.4 1.3 copy-done.28
  140.5 1.9 convolution_multiply_fusion
  143.0 24.6 %collective-permute-done.16.refs_6_.refs_4_ = bf16[2,16,32,128]{3,2,1,0:T(8,128)(2,1)} collective-permute-done((bf16[2,16,32,128]{3,2,1,0:T(8,128)(2,1)}, bf16[2,16,32,128]{3,2,1,0:T(8,128)(2,1)}, u32[]{:S(2)}, u32[]{:S(2)}) %collective-permute-start.16) | collective-permute-done | bytes 262176 | tf_op jit(solution)/shard_map/ppermute | solution.py:16
  172.0 5.3 %slice_bitcast_fusion.7 = (bf16[5,16,32,256]{3,2,1,0:T(8,128)(2,1)}, bf16[5,16,32,256]{3,2,1,0:T(8,128)(2,1)}, bf16[5,16,32,256]{3,2,1,0:T(8,128)(2,1)}, bf16[5,16,32,256]{3,2,1,0:T(8,128)(2,1)}) fusion(bf16[4,5,16,32,256]{4,3,2,1,0:T(8,128)(2,1)} %copy-done.6), kind=kLoop, calls=%fused_computation.20 | loop fusion | bytes 10485760 | tf_op jit(solution)/shard_map/squeeze | solution.py:255
  177.5 30.5 %collective-permute-done.3.refs_2_ = bf16[5,16,32,256]{3,2,1,0:T(8,128)(2,1)} collective-permute-done((bf16[5,16,32,256]{3,2,1,0:T(8,128)(2,1)}, bf16[5,16,32,256]{3,2,1,0:T(8,128)(2,1)}, u32[]{:S(2)}, u32[]{:S(2)}) %collective-permute-start.3) | collective-permute-done | bytes 1310752 | tf_op jit(solution)/shard_map/ppermute | solution.py:16
  208.1 9.0 %shard_map.94 = (bf16[192,4096]{1,0:T(8,128)(2,1)S(1)}, bf16[192,4096]{1,0:T(8,128)(2,1)S(1)}) custom-call(s32[1]{0:T(128)} %bitcast.pos_ref, bf16[192,4096]{1,0:T(8,128)(2,1)S(1)} %copy-done.1, bf16[2,16,32,256]{3,2,1,0:T(8,128)(2,1)S(1)} %copy-done.8, bf16[2,16,32,256]{3,2,1,0:T(8,128)(2,1)S(1)} %copy-done.15, bf16[2,16,32,256]{3,2,1,0:T(8,128)(2,1)S(1)} %copy-done.18, ...), custom_call_target="tpu_custom_call" | custom-call | flops 805306368 | bytes 8912896 | tf_op jit(solution)/shard_map/pallas_call | solution.py:170
  217.2 1.2 copy-done.36
  219.5 2.0 slice.243
  221.5 2.2 collective-permute-done.4.refs_3_
  223.7 1.6 collective-permute-start.5
  225.3 1.4 slice_bitcast_fusion.15
  226.7 29.6 %all-reduce.3.cloned.1.call-done = (f32[4096,128]{0,1:T(8,128)}, f32[128,4096]{1,0:T(8,128)}) async-done(((f32[4096,128]{0,1:T(8,128)}, f32[128,4096]{1,0:T(8,128)}), (f32[4096,128]{0,1:T(8,128)}, f32[128,4096]{1,0:T(8,128)})) %all-reduce.3.cloned.1.call-update) | async-done | bytes 4194320 | tf_op jit(solution)/shard_map/psum | solution.py:318
  256.4 2.9 copy.10
  259.2 2.5 slice_bitcast_fusion.11
  263.5 3.6 slice_bitcast_fusion.3
  267.2 7.9 %collective-permute-start.22 = (bf16[192,4096]{1,0:T(8,128)(2,1)S(1)}, bf16[192,4096]{1,0:T(8,128)(2,1)}, u32[]{:S(2)}, u32[]{:S(2)}) collective-permute-start(bf16[192,4096]{1,0:T(8,128)(2,1)S(1)} %copy-done.37), channel_id=1, source_target_pairs={{0,1},{1,0},{2,3},{3,2},{4,5},{5,4},{6,7},{7,6},{8,9},{9,8},{10,11... | collective-permute-start | bytes 4718600 | tf_op jit(solution)/shard_map/ppermute | solution.py:16
  275.1 1.4 add_convert_fusion.5
  277.1 1.5 collective-permute-start.36
  279.8 16.8 %shard_map.92 = (f32[192,4096]{1,0:T(8,128)}, f32[192,4096]{1,0:T(8,128)}) custom-call(s32[1]{0:T(128)} %bitcast.pos_ref, bf16[192,4096]{1,0:T(8,128)(2,1)S(1)} %copy-done.3, bf16[192,4096]{1,0:T(8,128)(2,1)} %cot_ref.7, bf16[192,128]{1,0:T(8,128)(2,1)S(1)} %get-tuple-element.61.fac_ref, bf16[192,128]{1,0:T(8,128)(2,1)S(1)} %get-tuple-element.60.back_ref, ...), custom_call_target="tpu_custom_call" | custom-call | flops 4026531840 | bytes 19922944 | tf_op jit(solution)/shard_map/pallas_call | solution.py:131
  298.6 1.3 collective-permute-start.34
  302.0 1.6 add_convert_fusion.4
  303.6 10.9 %collective-permute-done.29 = bf16[5,16,32,128]{3,2,1,0:T(8,128)(2,1)S(1)} collective-permute-done((bf16[5,16,32,128]{3,2,1,0:T(8,128)(2,1)}, bf16[5,16,32,128]{3,2,1,0:T(8,128)(2,1)S(1)}, u32[]{:S(2)}, u32[]{:S(2)}) %collective-permute-start.29) | collective-permute-done | bytes 655392 | tf_op jit(solution)/shard_map/ppermute | solution.py:16
  315.8 22.5 %collective-permute-done.23 = bf16[192,4096]{1,0:T(8,128)(2,1)} collective-permute-done((bf16[192,4096]{1,0:T(8,128)(2,1)S(1)}, bf16[192,4096]{1,0:T(8,128)(2,1)}, u32[]{:S(2)}, u32[]{:S(2)}) %collective-permute-start.23) | collective-permute-done | bytes 1572896 | tf_op jit(solution)/shard_map/ppermute | solution.py:16
  340.4 1.4 collective-permute-start.25
  343.5 3.8 add_convert_fusion
  348.1 10.2 %shard_map.93 = bf16[192,4096]{1,0:T(8,128)(2,1)} custom-call(s32[1]{0:T(128)} %bitcast.pos_ref, f32[192,4096]{1,0:T(8,128)S(1)} %copy-done.20, bf16[192,4096]{1,0:T(8,128)(2,1)S(1)} %collective-permute-done.11.refs_0_, bf16[192,4096]{1,0:T(8,128)(2,1)S(1)} %copy-done.5, bf16[2,16,32,256]{3,2,1,0:T(8,128)(2,1)S(1)} %copy-done.9, ...), custom_call_target="tpu_custom_call" | custom-call | flops 805306368 | bytes 12058624 | tf_op jit(solution)/shard_map/pallas_call | solution.py:204
  358.6 3.1 collective-permute-done.27
  361.6 8.0 %collective-permute-done.30 = bf16[5,16,32,128]{3,2,1,0:T(8,128)(2,1)S(1)} collective-permute-done((bf16[5,16,32,128]{3,2,1,0:T(8,128)(2,1)S(1)}, bf16[5,16,32,128]{3,2,1,0:T(8,128)(2,1)S(1)}, u32[]{:S(2)}, u32[]{:S(2)}) %collective-permute-start.30) | collective-permute-done | bytes 655392 | tf_op jit(solution)/shard_map/ppermute | solution.py:16
  369.7 4.1 %collective-permute-done.28 = bf16[5,16,32,128]{3,2,1,0:T(8,128)(2,1)S(1)} collective-permute-done((bf16[5,16,32,128]{3,2,1,0:T(8,128)(2,1)S(1)}, bf16[5,16,32,128]{3,2,1,0:T(8,128)(2,1)S(1)}, u32[]{:S(2)}, u32[]{:S(2)}) %collective-permute-start.28) | collective-permute-done | bytes 655392 | tf_op jit(solution)/shard_map/ppermute | solution.py:16
  374.5 2.2 maximum_maximum_fusion
  376.7 1.3 copy.13
  (174 shorter events, 26.1 us)
Async XLA Ops:
  7.2 249.2 %all-reduce.3.cloned.1.call-start = ((), (), s32[]{:S(2)}) async-start(), calls=%async_computation | async-start | bytes 8388608 | tf_op jit(solution)/shard_map/psum | solution.py:318
  22.6 240.4 %collective-permute-start.24 = (bf16[4,5,16,32,256]{4,3,2,1,0:T(8,128)(2,1)}, bf16[4,5,16,32,256]{4,3,2,1,0:T(8,128)(2,1)}, u32[]{:S(2)}, u32[]{:S(2)}) collective-permute-start(bf16[4,5,16,32,256]{4,3,2,1,0:T(8,128)(2,1)} %get-tuple-element.18), channel_id=1, source_target_pairs={{0,4},{4,0},{8,12},{12,8},{16,20},{20,16},{24,28},{28,24},{1,5},{5... | collective-permute-start | bytes 15728648 | tf_op jit(solution)/shard_map/ppermute | solution.py:16
  23.1 105.0 %collective-permute-start.11 = (bf16[192,4096]{1,0:T(8,128)(2,1)S(1)}, bf16[192,4096]{1,0:T(8,128)(2,1)S(1)}, u32[]{:S(2)}, u32[]{:S(2)}) collective-permute-start(bf16[192,4096]{1,0:T(8,128)(2,1)S(1)} %copy-done.2), channel_id=1, source_target_pairs={{0,1},{1,0},{2,3},{3,2},{4,5},{5,4},{6,7},{7,6},{8,9},{9,8},{10,11... | collective-permute-start | bytes 4718600 | tf_op jit(solution)/shard_map/ppermute | solution.py:16
  25.7 104.0 %collective-permute-start.12 = (bf16[192,4096]{1,0:T(8,128)(2,1)S(1)}, bf16[192,4096]{1,0:T(8,128)(2,1)S(1)}, u32[]{:S(2)}, u32[]{:S(2)}) collective-permute-start(bf16[192,4096]{1,0:T(8,128)(2,1)S(1)} %copy-done.2), channel_id=1, source_target_pairs={{0,2},{1,3},{2,0},{3,1},{4,6},{5,7},{6,4},{7,5},{8,10},{9,11},{10,... | collective-permute-start | bytes 4718600 | tf_op jit(solution)/shard_map/ppermute | solution.py:16
  29.4 69.2 %collective-permute-start = (f32[192,256]{1,0:T(8,128)S(1)}, f32[192,256]{1,0:T(8,128)S(1)}, u32[]{:S(2)}, u32[]{:S(2)}) collective-permute-start(f32[192,256]{1,0:T(8,128)S(1)} %pad_maximum_fusion), channel_id=1, source_target_pairs={{0,1},{1,0},{2,3},{3,2},{4,5},{5,4},{6,7},{7,6},{8,9},{9,8},{10,11... | collective-permute-start | bytes 589832 | tf_op jit(solution)/shard_map/ppermute | solution.py:16
  30.4 82.9 %copy-start.7 = (bf16[2,16,32,256]{3,2,1,0:T(8,128)(2,1)}, bf16[2,16,32,256]{3,2,1,0:T(8,128)(2,1)S(1)}, u32[]{:S(2)}) copy-start(bf16[2,16,32,256]{3,2,1,0:T(8,128)(2,1)S(1)} %slice.189.refs_2_.refs_0_) | copy-start | bytes 1572868
  30.4 82.8 %collective-permute-start.13 = (bf16[2,16,32,256]{3,2,1,0:T(8,128)(2,1)S(1)}, bf16[2,16,32,256]{3,2,1,0:T(8,128)(2,1)S(1)}, u32[]{:S(2)}, u32[]{:S(2)}) collective-permute-start(bf16[2,16,32,256]{3,2,1,0:T(8,128)(2,1)S(1)} %slice.189.refs_2_.refs_0_), channel_id=1, source_target_pairs={{0,8},{4,12},{8,0},{12,4},{16,24},{20,28},{24,16},{28,20},{1,9},{5... | collective-permute-start | bytes 1572872 | tf_op jit(solution)/shard_map/ppermute | solution.py:16
  98.7 11.9 %collective-permute-start.1 = (f32[192,256]{1,0:T(8,128)S(1)}, f32[192,256]{1,0:T(8,128)S(1)}, u32[]{:S(2)}, u32[]{:S(2)}) collective-permute-start(f32[192,256]{1,0:T(8,128)S(1)} %fusion.3), channel_id=1, source_target_pairs={{0,2},{1,3},{2,0},{3,1},{4,6},{5,7},{6,4},{7,5},{8,10},{9,11},{10,... | collective-permute-start | bytes 589832 | tf_op jit(solution)/shard_map/ppermute | solution.py:16
  110.6 12.9 %collective-permute-start.14 = (bf16[2,16,32,256]{3,2,1,0:T(8,128)(2,1)S(1)}, bf16[2,16,32,256]{3,2,1,0:T(8,128)(2,1)S(1)}, u32[]{:S(2)}, u32[]{:S(2)}) collective-permute-start(bf16[2,16,32,256]{3,2,1,0:T(8,128)(2,1)S(1)} %slice.189.refs_2_.refs_0_), channel_id=1, source_target_pairs={{0,16},{4,20},{8,24},{12,28},{16,0},{20,4},{24,8},{28,12},{1,17},{... | collective-permute-start | bytes 1572872 | tf_op jit(solution)/shard_map/ppermute | solution.py:16
  113.2 26.5 %collective-permute-start.17 = (bf16[2,16,32,256]{3,2,1,0:T(8,128)(2,1)S(1)}, bf16[2,16,32,256]{3,2,1,0:T(8,128)(2,1)S(1)}, u32[]{:S(2)}, u32[]{:S(2)}) collective-permute-start(bf16[2,16,32,256]{3,2,1,0:T(8,128)(2,1)S(1)} %slice.189.refs_2_.refs_0_), channel_id=1, source_target_pairs={{0,4},{4,0},{8,12},{12,8},{16,20},{20,16},{24,28},{28,24},{1,5},{5... | collective-permute-start | bytes 1572872 | tf_op jit(solution)/shard_map/ppermute | solution.py:16
  123.5 45.2 %collective-permute-start.2 = (bf16[5,16,32,256]{3,2,1,0:T(8,128)(2,1)}, bf16[5,16,32,256]{3,2,1,0:T(8,128)(2,1)}, u32[]{:S(2)}, u32[]{:S(2)}) collective-permute-start(bf16[5,16,32,256]{3,2,1,0:T(8,128)(2,1)} %slice.186.refs_0_), channel_id=1, source_target_pairs={{0,8},{4,12},{8,0},{12,4},{16,24},{20,28},{24,16},{28,20},{1,9},{5... | collective-permute-start | bytes 3932168 | tf_op jit(solution)/shard_map/ppermute | solution.py:16
  128.1 14.3 %collective-permute-start.15 = (bf16[2,16,32,128]{3,2,1,0:T(8,128)(2,1)}, bf16[2,16,32,128]{3,2,1,0:T(8,128)(2,1)S(1)}, u32[]{:S(2)}, u32[]{:S(2)}) collective-permute-start(bf16[2,16,32,128]{3,2,1,0:T(8,128)(2,1)} %slice.244), channel_id=1, source_target_pairs={{0,16},{4,20},{8,24},{12,28},{16,0},{20,4},{24,8},{28,12},{1,17},{... | collective-permute-start | bytes 786440 | tf_op jit(solution)/shard_map/ppermute | solution.py:16
  129.7 38.0 %collective-permute-start.16 = (bf16[2,16,32,128]{3,2,1,0:T(8,128)(2,1)}, bf16[2,16,32,128]{3,2,1,0:T(8,128)(2,1)}, u32[]{:S(2)}, u32[]{:S(2)}) collective-permute-start(bf16[2,16,32,128]{3,2,1,0:T(8,128)(2,1)} %slice.245), channel_id=1, source_target_pairs={{0,8},{4,12},{8,0},{12,4},{16,24},{20,28},{24,16},{28,20},{1,9},{5... | collective-permute-start | bytes 786440 | tf_op jit(solution)/shard_map/ppermute | solution.py:16
  140.5 84.8 %collective-permute-start.31 = (bf16[4,2,16,32,256]{4,3,2,1,0:T(8,128)(2,1)}, bf16[4,2,16,32,256]{4,3,2,1,0:T(8,128)(2,1)}, u32[]{:S(2)}, u32[]{:S(2)}) collective-permute-start(bf16[4,2,16,32,256]{4,3,2,1,0:T(8,128)(2,1)} %get-tuple-element.20), channel_id=1, source_target_pairs={{0,4},{4,0},{8,12},{12,8},{16,20},{20,16},{24,28},{28,24},{1,5},{5... | collective-permute-start | bytes 6291464 | tf_op jit(solution)/shard_map/ppermute | solution.py:16
  142.4 26.3 %collective-permute-start.18 = (bf16[2,16,32,256]{3,2,1,0:T(8,128)(2,1)}, bf16[2,16,32,256]{3,2,1,0:T(8,128)(2,1)S(1)}, u32[]{:S(2)}, u32[]{:S(2)}) collective-permute-start(bf16[2,16,32,256]{3,2,1,0:T(8,128)(2,1)} %copy-done.14), channel_id=1, source_target_pairs={{0,4},{4,0},{8,12},{12,8},{16,20},{20,16},{24,28},{28,24},{1,5},{5... | collective-permute-start | bytes 1572872 | tf_op jit(solution)/shard_map/ppermute | solution.py:16
  167.7 40.3 %collective-permute-start.3 = (bf16[5,16,32,256]{3,2,1,0:T(8,128)(2,1)}, bf16[5,16,32,256]{3,2,1,0:T(8,128)(2,1)}, u32[]{:S(2)}, u32[]{:S(2)}) collective-permute-start(bf16[5,16,32,256]{3,2,1,0:T(8,128)(2,1)} %slice.186.refs_0_), channel_id=1, source_target_pairs={{0,16},{4,20},{8,24},{12,28},{16,0},{20,4},{24,8},{28,12},{1,17},{... | collective-permute-start | bytes 3932168 | tf_op jit(solution)/shard_map/ppermute | solution.py:16
  168.7 39.3 %copy-start.24 = (bf16[2,16,32,256]{3,2,1,0:T(8,128)(2,1)}, bf16[2,16,32,256]{3,2,1,0:T(8,128)(2,1)S(1)}, u32[]{:S(2)}) copy-start(bf16[2,16,32,256]{3,2,1,0:T(8,128)(2,1)S(1)} %collective-permute-done.18.refs_8_.refs_6_) | copy-start | bytes 1572868
  168.7 2.1 collective-permute-start.19
  168.7 2.3 collective-permute-start.20
  170.8 37.2 %copy-start.26 = (bf16[2,16,32,256]{3,2,1,0:T(8,128)(2,1)}, bf16[2,16,32,256]{3,2,1,0:T(8,128)(2,1)S(1)}, u32[]{:S(2)}) copy-start(bf16[2,16,32,256]{3,2,1,0:T(8,128)(2,1)S(1)} %collective-permute-done.19.refs_9_.refs_7_) | copy-start | bytes 1572868
  170.8 6.5 %collective-permute-start.21 = (bf16[2,16,32,128]{3,2,1,0:T(8,128)(2,1)}, bf16[2,16,32,128]{3,2,1,0:T(8,128)(2,1)S(1)}, u32[]{:S(2)}, u32[]{:S(2)}) collective-permute-start(bf16[2,16,32,128]{3,2,1,0:T(8,128)(2,1)} %collective-permute-done.16.refs_6_.refs_4_), channel_id=1, source_target_pairs={{0,4},{4,0},{8,12},{12,8},{16,20},{20,16},{24,28},{28,24},{1,5},{5... | collective-permute-start | bytes 786440 | tf_op jit(solution)/shard_map/ppermute | solution.py:16
  171.0 37.0 %copy-start.30 = (bf16[2,16,32,128]{3,2,1,0:T(8,128)(2,1)}, bf16[2,16,32,128]{3,2,1,0:T(8,128)(2,1)S(1)}, u32[]{:S(2)}) copy-start(bf16[2,16,32,128]{3,2,1,0:T(8,128)(2,1)S(1)} %collective-permute-done.20.refs_10_.refs_8_) | copy-start | bytes 786436
  171.0 52.7 %collective-permute-start.4 = (bf16[5,16,32,128]{3,2,1,0:T(8,128)(2,1)S(1)}, bf16[5,16,32,128]{3,2,1,0:T(8,128)(2,1)S(1)}, u32[]{:S(2)}, u32[]{:S(2)}) collective-permute-start(bf16[5,16,32,128]{3,2,1,0:T(8,128)(2,1)S(1)} %slice.242), channel_id=1, source_target_pairs={{0,16},{4,20},{8,24},{12,28},{16,0},{20,4},{24,8},{28,12},{1,17},{... | collective-permute-start | bytes 1966088 | tf_op jit(solution)/shard_map/ppermute | solution.py:16
  172.0 36.1 %copy-start.8 = (bf16[2,16,32,256]{3,2,1,0:T(8,128)(2,1)S(1)}, bf16[2,16,32,256]{3,2,1,0:T(8,128)(2,1)}, u32[]{:S(2)}) copy-start(bf16[2,16,32,256]{3,2,1,0:T(8,128)(2,1)} %copy-done.7) | copy-start | bytes 1572868
  172.0 36.1 %copy-start.15 = (bf16[2,16,32,256]{3,2,1,0:T(8,128)(2,1)S(1)}, bf16[2,16,32,256]{3,2,1,0:T(8,128)(2,1)}, u32[]{:S(2)}) copy-start(bf16[2,16,32,256]{3,2,1,0:T(8,128)(2,1)} %copy-done.14) | copy-start | bytes 1572868
  172.0 36.1 %copy-start.18 = (bf16[2,16,32,256]{3,2,1,0:T(8,128)(2,1)S(1)}, bf16[2,16,32,256]{3,2,1,0:T(8,128)(2,1)}, u32[]{:S(2)}) copy-start(bf16[2,16,32,256]{3,2,1,0:T(8,128)(2,1)} %copy-done.17) | copy-start | bytes 1572868
  172.0 36.1 %copy-start.22 = (bf16[2,16,32,256]{3,2,1,0:T(8,128)(2,1)S(1)}, bf16[2,16,32,256]{3,2,1,0:T(8,128)(2,1)}, u32[]{:S(2)}) copy-start(bf16[2,16,32,256]{3,2,1,0:T(8,128)(2,1)} %copy-done.21) | copy-start | bytes 1572868
  177.3 39.8 %copy-start.32 = (bf16[2,16,32,128]{3,2,1,0:T(8,128)(2,1)}, bf16[2,16,32,128]{3,2,1,0:T(8,128)(2,1)S(1)}, u32[]{:S(2)}) copy-start(bf16[2,16,32,128]{3,2,1,0:T(8,128)(2,1)S(1)} %collective-permute-done.21.refs_11_.refs_9_) | copy-start | bytes 786436
  177.3 89.7 %collective-permute-start.6 = (bf16[5,16,32,256]{3,2,1,0:T(8,128)(2,1)}, bf16[5,16,32,256]{3,2,1,0:T(8,128)(2,1)}, u32[]{:S(2)}, u32[]{:S(2)}) collective-permute-start(bf16[5,16,32,256]{3,2,1,0:T(8,128)(2,1)} %slice.186.refs_0_), channel_id=1, source_target_pairs={{0,4},{4,0},{8,12},{12,8},{16,20},{20,16},{24,28},{28,24},{1,5},{5... | collective-permute-start | bytes 3932168 | tf_op jit(solution)/shard_map/ppermute | solution.py:16
  208.0 59.2 %collective-permute-start.7 = (bf16[5,16,32,256]{3,2,1,0:T(8,128)(2,1)}, bf16[5,16,32,256]{3,2,1,0:T(8,128)(2,1)}, u32[]{:S(2)}, u32[]{:S(2)}) collective-permute-start(bf16[5,16,32,256]{3,2,1,0:T(8,128)(2,1)} %collective-permute-done.2.refs_1_), channel_id=1, source_target_pairs={{0,4},{4,0},{8,12},{12,8},{16,20},{20,16},{24,28},{28,24},{1,5},{5... | collective-permute-start | bytes 3932168 | tf_op jit(solution)/shard_map/ppermute | solution.py:16
  223.7 39.0 %collective-permute-start.5 = (bf16[5,16,32,128]{3,2,1,0:T(8,128)(2,1)}, bf16[5,16,32,128]{3,2,1,0:T(8,128)(2,1)}, u32[]{:S(2)}, u32[]{:S(2)}) collective-permute-start(bf16[5,16,32,128]{3,2,1,0:T(8,128)(2,1)} %slice.243), channel_id=1, source_target_pairs={{0,8},{4,12},{8,0},{12,4},{16,24},{20,28},{24,16},{28,20},{1,9},{5... | collective-permute-start | bytes 1966088 | tf_op jit(solution)/shard_map/ppermute | solution.py:16
  225.3 51.2 %collective-permute-start.8 = (bf16[5,16,32,256]{3,2,1,0:T(8,128)(2,1)}, bf16[5,16,32,256]{3,2,1,0:T(8,128)(2,1)S(1)}, u32[]{:S(2)}, u32[]{:S(2)}) collective-permute-start(bf16[5,16,32,256]{3,2,1,0:T(8,128)(2,1)} %collective-permute-done.3.refs_2_), channel_id=1, source_target_pairs={{0,4},{4,0},{8,12},{12,8},{16,20},{20,16},{24,28},{28,24},{1,5},{5... | collective-permute-start | bytes 3932168 | tf_op jit(solution)/shard_map/ppermute | solution.py:16
  263.0 14.2 %collective-permute-start.9 = (bf16[5,16,32,128]{3,2,1,0:T(8,128)(2,1)S(1)}, bf16[5,16,32,128]{3,2,1,0:T(8,128)(2,1)S(1)}, u32[]{:S(2)}, u32[]{:S(2)}) collective-permute-start(bf16[5,16,32,128]{3,2,1,0:T(8,128)(2,1)S(1)} %copy-done.35), channel_id=1, source_target_pairs={{0,4},{4,0},{8,12},{12,8},{16,20},{20,16},{24,28},{28,24},{1,5},{5... | collective-permute-start | bytes 1966088 | tf_op jit(solution)/shard_map/ppermute | solution.py:16
  263.0 15.6 %collective-permute-start.10 = (bf16[5,16,32,128]{3,2,1,0:T(8,128)(2,1)}, bf16[5,16,32,128]{3,2,1,0:T(8,128)(2,1)S(1)}, u32[]{:S(2)}, u32[]{:S(2)}) collective-permute-start(bf16[5,16,32,128]{3,2,1,0:T(8,128)(2,1)} %collective-permute-done.5.refs_4_), channel_id=1, source_target_pairs={{0,4},{4,0},{8,12},{12,8},{16,20},{20,16},{24,28},{28,24},{1,5},{5... | collective-permute-start | bytes 1966088 | tf_op jit(solution)/shard_map/ppermute | solution.py:16
  267.1 71.2 %collective-permute-start.23 = (bf16[192,4096]{1,0:T(8,128)(2,1)S(1)}, bf16[192,4096]{1,0:T(8,128)(2,1)}, u32[]{:S(2)}, u32[]{:S(2)}) collective-permute-start(bf16[192,4096]{1,0:T(8,128)(2,1)S(1)} %copy-done.39), channel_id=1, source_target_pairs={{0,2},{1,3},{2,0},{3,1},{4,6},{5,7},{6,4},{7,5},{8,10},{9,11},{10,... | collective-permute-start | bytes 4718600 | tf_op jit(solution)/shard_map/ppermute | solution.py:16
  267.2 72.1 %collective-permute-start.22 = (bf16[192,4096]{1,0:T(8,128)(2,1)S(1)}, bf16[192,4096]{1,0:T(8,128)(2,1)}, u32[]{:S(2)}, u32[]{:S(2)}) collective-permute-start(bf16[192,4096]{1,0:T(8,128)(2,1)S(1)} %copy-done.37), channel_id=1, source_target_pairs={{0,1},{1,0},{2,3},{3,2},{4,5},{5,4},{6,7},{7,6},{8,9},{9,8},{10,11... | collective-permute-start | bytes 4718600 | tf_op jit(solution)/shard_map/ppermute | solution.py:16
  276.5 20.1 %collective-permute-start.33 = (bf16[2,16,32,128]{3,2,1,0:T(8,128)(2,1)}, bf16[2,16,32,128]{3,2,1,0:T(8,128)(2,1)}, u32[]{:S(2)}, u32[]{:S(2)}) collective-permute-start(bf16[2,16,32,128]{3,2,1,0:T(8,128)(2,1)} %get-tuple-element.58), channel_id=1, source_target_pairs={{0,8},{4,12},{8,0},{12,4},{16,24},{20,28},{24,16},{28,20},{1,9},{5... | collective-permute-start | bytes 786440 | tf_op jit(solution)/shard_map/ppermute | solution.py:16
  277.1 21.4 %collective-permute-start.36 = (bf16[2,16,32,128]{3,2,1,0:T(8,128)(2,1)}, bf16[2,16,32,128]{3,2,1,0:T(8,128)(2,1)}, u32[]{:S(2)}, u32[]{:S(2)}) collective-permute-start(bf16[2,16,32,128]{3,2,1,0:T(8,128)(2,1)} %get-tuple-element.59), channel_id=1, source_target_pairs={{0,16},{4,20},{8,24},{12,28},{16,0},{20,4},{24,8},{28,12},{1,17},{... | collective-permute-start | bytes 786440 | tf_op jit(solution)/shard_map/ppermute | solution.py:16
  278.6 22.4 %collective-permute-start.26 = (bf16[5,16,32,128]{3,2,1,0:T(8,128)(2,1)}, bf16[5,16,32,128]{3,2,1,0:T(8,128)(2,1)}, u32[]{:S(2)}, u32[]{:S(2)}) collective-permute-start(bf16[5,16,32,128]{3,2,1,0:T(8,128)(2,1)} %get-tuple-element.42), channel_id=1, source_target_pairs={{0,8},{4,12},{8,0},{12,4},{16,24},{20,28},{24,16},{28,20},{1,9},{5... | collective-permute-start | bytes 1966088 | tf_op jit(solution)/shard_map/ppermute | solution.py:16
  296.6 17.9 %collective-permute-start.29 = (bf16[5,16,32,128]{3,2,1,0:T(8,128)(2,1)}, bf16[5,16,32,128]{3,2,1,0:T(8,128)(2,1)S(1)}, u32[]{:S(2)}, u32[]{:S(2)}) collective-permute-start(bf16[5,16,32,128]{3,2,1,0:T(8,128)(2,1)} %get-tuple-element.43), channel_id=1, source_target_pairs={{0,16},{4,20},{8,24},{12,28},{16,0},{20,4},{24,8},{28,12},{1,17},{... | collective-permute-start | bytes 1966088 | tf_op jit(solution)/shard_map/ppermute | solution.py:16
  298.6 41.8 %collective-permute-start.34 = (bf16[2,16,32,128]{3,2,1,0:T(8,128)(2,1)S(1)}, bf16[2,16,32,128]{3,2,1,0:T(8,128)(2,1)S(1)}, u32[]{:S(2)}, u32[]{:S(2)}) collective-permute-start(bf16[2,16,32,128]{3,2,1,0:T(8,128)(2,1)S(1)} %get-tuple-element.56), channel_id=1, source_target_pairs={{0,16},{4,20},{8,24},{12,28},{16,0},{20,4},{24,8},{28,12},{1,17},{... | collective-permute-start | bytes 786440 | tf_op jit(solution)/shard_map/ppermute | solution.py:16
  301.0 40.8 %collective-permute-start.32 = (bf16[2,16,32,128]{3,2,1,0:T(8,128)(2,1)S(1)}, bf16[2,16,32,128]{3,2,1,0:T(8,128)(2,1)S(1)}, u32[]{:S(2)}, u32[]{:S(2)}) collective-permute-start(bf16[2,16,32,128]{3,2,1,0:T(8,128)(2,1)S(1)} %get-tuple-element.54), channel_id=1, source_target_pairs={{0,8},{4,12},{8,0},{12,4},{16,24},{20,28},{24,16},{28,20},{1,9},{5... | collective-permute-start | bytes 786440 | tf_op jit(solution)/shard_map/ppermute | solution.py:16
  314.5 27.9 %collective-permute-start.37 = (bf16[2,16,32,128]{3,2,1,0:T(8,128)(2,1)S(1)}, bf16[2,16,32,128]{3,2,1,0:T(8,128)(2,1)S(1)}, u32[]{:S(2)}, u32[]{:S(2)}) collective-permute-start(bf16[2,16,32,128]{3,2,1,0:T(8,128)(2,1)S(1)} %get-tuple-element.55), channel_id=1, source_target_pairs={{0,8},{4,12},{8,0},{12,4},{16,24},{20,28},{24,16},{28,20},{1,9},{5... | collective-permute-start | bytes 786440 | tf_op jit(solution)/shard_map/ppermute | solution.py:16
  338.3 19.9 %collective-permute-start.35 = (bf16[2,16,32,128]{3,2,1,0:T(8,128)(2,1)S(1)}, bf16[2,16,32,128]{3,2,1,0:T(8,128)(2,1)S(1)}, u32[]{:S(2)}, u32[]{:S(2)}) collective-permute-start(bf16[2,16,32,128]{3,2,1,0:T(8,128)(2,1)S(1)} %get-tuple-element.57), channel_id=1, source_target_pairs={{0,16},{4,20},{8,24},{12,28},{16,0},{20,4},{24,8},{28,12},{1,17},{... | collective-permute-start | bytes 786440 | tf_op jit(solution)/shard_map/ppermute | solution.py:16
  339.3 22.3 %collective-permute-start.27 = (bf16[5,16,32,128]{3,2,1,0:T(8,128)(2,1)S(1)}, bf16[5,16,32,128]{3,2,1,0:T(8,128)(2,1)S(1)}, u32[]{:S(2)}, u32[]{:S(2)}) collective-permute-start(bf16[5,16,32,128]{3,2,1,0:T(8,128)(2,1)S(1)} %get-tuple-element.40), channel_id=1, source_target_pairs={{0,16},{4,20},{8,24},{12,28},{16,0},{20,4},{24,8},{28,12},{1,17},{... | collective-permute-start | bytes 1966088 | tf_op jit(solution)/shard_map/ppermute | solution.py:16
  340.4 21.3 %collective-permute-start.25 = (bf16[5,16,32,128]{3,2,1,0:T(8,128)(2,1)S(1)}, bf16[5,16,32,128]{3,2,1,0:T(8,128)(2,1)S(1)}, u32[]{:S(2)}, u32[]{:S(2)}) collective-permute-start(bf16[5,16,32,128]{3,2,1,0:T(8,128)(2,1)S(1)} %get-tuple-element.38), channel_id=1, source_target_pairs={{0,8},{4,12},{8,0},{12,4},{16,24},{20,28},{24,16},{28,20},{1,9},{5... | collective-permute-start | bytes 1966088 | tf_op jit(solution)/shard_map/ppermute | solution.py:16
  341.8 27.9 %collective-permute-start.30 = (bf16[5,16,32,128]{3,2,1,0:T(8,128)(2,1)S(1)}, bf16[5,16,32,128]{3,2,1,0:T(8,128)(2,1)S(1)}, u32[]{:S(2)}, u32[]{:S(2)}) collective-permute-start(bf16[5,16,32,128]{3,2,1,0:T(8,128)(2,1)S(1)} %get-tuple-element.39), channel_id=1, source_target_pairs={{0,8},{4,12},{8,0},{12,4},{16,24},{20,28},{24,16},{28,20},{1,9},{5... | collective-permute-start | bytes 1966088 | tf_op jit(solution)/shard_map/ppermute | solution.py:16
  342.4 31.4 %collective-permute-start.28 = (bf16[5,16,32,128]{3,2,1,0:T(8,128)(2,1)S(1)}, bf16[5,16,32,128]{3,2,1,0:T(8,128)(2,1)S(1)}, u32[]{:S(2)}, u32[]{:S(2)}) collective-permute-start(bf16[5,16,32,128]{3,2,1,0:T(8,128)(2,1)S(1)} %get-tuple-element.41), channel_id=1, source_target_pairs={{0,16},{4,20},{8,24},{12,28},{16,0},{20,4},{24,8},{28,12},{1,17},{... | collective-permute-start | bytes 1966088 | tf_op jit(solution)/shard_map/ppermute | solution.py:16
  (45 other events, 388.4 us)
Sparse Core Ops, SparseCore 0:
  142.5 113.7 all-reduce.2

commit v2 on v1

v2 whole, which is shorter than its diff:
```python
import functools

import jax
import jax.numpy as jnp
from jax import lax
from jax.experimental import pallas as pl
from jax.experimental.pallas import tpu as pltpu
from jax.sharding import PartitionSpec as P

F32 = jnp.float32
BF16 = jnp.bfloat16
COST = pl.CostEstimate(flops=1, bytes_accessed=1, transcendentals=0)
VMEM_LIMIT = 28 * 1024 * 1024


def swap(value, axis, mask):
    return lax.ppermute(value, axis, [(i, i ^ mask) for i in range(lax.axis_size(axis))])


def params():
    return pltpu.CompilerParams(
        dimension_semantics=("arbitrary",), vmem_limit_bytes=VMEM_LIMIT
    )


def aligned(index, size):
    return pl.ds(pl.multiple_of(index * size, size), size)


TN = (((0,), (0,)), ((), ()))
NT = (((1,), (1,)), ((), ()))


def after(value, *others):
    return lax.optimization_barrier((value, *others))[0]


def join(j, parts, refs, joined):
    @pl.when(j == 0)
    def _():
        places = iter(refs)
        start = 0
        for width, _ in parts:
            for to in joined:
                to[:, start : start + width] = next(places)[:, :width]
            start += width

    return joined


def grads_kernel(levels, parts, shards, scale, pos_ref, cot_ref, *refs):
    joined = len(parts[0][1])
    sources = join(pl.program_id(0), parts, refs[: len(refs) - 3 - joined], refs[len(refs) - joined :])
    keep_ref, send_ref, tmp_ref = refs[len(refs) - 3 - joined : len(refs) - joined]
    block = cot_ref.shape[1]
    rows = block // shards
    j = pl.program_id(0)
    pos = pos_ref[0]
    cot = cot_ref[...]
    for k in range(levels):
        values = sources[k][:, aligned(j, block)]
        tmp_ref[k] = lax.dot_general(values, cot, TN, preferred_element_type=F32) * scale
        for m in range(shards):
            part = tmp_ref[k, aligned(pos ^ m, rows), :].astype(BF16)
            (send_ref if m & 1 else keep_ref)[m >> 1, k, 0] = part


def block_grads(pos, cot, parts, n_blocks, shards, scale):
    tok, ff = cot.shape
    block = ff // n_blocks
    rows = block // shards
    n_levels = len(parts[0][1])
    sources = [value for _, part in parts for value in part]
    part = jax.ShapeDtypeStruct((shards // 2, n_levels, n_blocks, rows, block), BF16)
    part_spec = pl.BlockSpec(
        (shards // 2, n_levels, 1, rows, block), lambda j, *_: (0, 0, j, 0, 0)
    )
    return pl.pallas_call(
        functools.partial(grads_kernel, n_levels, parts, shards, scale),
        grid_spec=pltpu.PrefetchScalarGridSpec(
            num_scalar_prefetch=1,
            grid=(n_blocks,),
            in_specs=[pl.BlockSpec((tok, block), lambda j, *_: (0, j))]
            + [pl.BlockSpec(s.shape, lambda j, *_: (0, 0)) for s in sources],
            out_specs=[part_spec, part_spec],
            scratch_shapes=[pltpu.VMEM((n_levels, block, block), F32)]
            + [pltpu.VMEM((tok, ff), BF16)] * n_levels,
        ),
        out_shape=[part, part],
        compiler_params=params(),
        cost_estimate=COST,
    )(pos, cot, *sources)


def pair_kernel(distances, shards, scale, pos_ref, *refs):
    ins, (keep_ref, tmp_ref) = refs[:-2], refs[-2:]
    pair = ins[: len(ins) // 2], ins[len(ins) // 2 :]
    block = ins[1].shape[1]
    rows = block // shards
    j = pl.program_id(0)
    pos = pos_ref[0]

    def product(left, right):
        return lax.dot_general(left, right, TN, preferred_element_type=F32)

    for k, distance in enumerate((*distances, None)):
        if distance is None:
            rank = ins[2].shape[1] // 2
            tmp_ref[k, :, :rank] = scale * sum(
                product(hid[:, aligned(j, block)], fac[:, rank:]) for hid, _, fac in pair
            )
            tmp_ref[k, :, rank:] = scale * sum(
                product(cot[...], fac[:, :rank]) for _, cot, fac in pair
            )
        else:
            there = aligned(j ^ distance, block)
            tmp_ref[k] = scale * sum(product(hid[:, there], cot[...]) for hid, cot, _ in pair)
        for m in range(0, shards, 2):
            keep_ref[m >> 1, k, 0] = tmp_ref[k, aligned(pos ^ m, rows), :].astype(BF16)


def pair_grads(pos, mine, other, distances, n_blocks, shards, scale):
    tok, ff = mine[0].shape
    block = ff // n_blocks
    shape = (shards // 2, len(distances) + 1, n_blocks, block // shards, block)
    specs = [
        pl.BlockSpec((tok, ff), lambda j, *_: (0, 0)),
        pl.BlockSpec((tok, block), lambda j, *_: (0, j)),
        pl.BlockSpec(mine[2].shape, lambda j, *_: (0, 0)),
    ]
    return pl.pallas_call(
        functools.partial(pair_kernel, distances, shards, scale),
        grid_spec=pltpu.PrefetchScalarGridSpec(
            num_scalar_prefetch=1,
            grid=(n_blocks,),
            in_specs=specs
            + [
                pl.BlockSpec((None, tok, ff), lambda j, *_: (0, 0, 0)),
                pl.BlockSpec((None, tok, block), lambda j, *_: (1, 0, j)),
                specs[2],
            ],
            out_specs=pl.BlockSpec(shape[:2] + (1,) + shape[3:], lambda j, *_: (0, 0, j, 0, 0)),
            scratch_shapes=[pltpu.VMEM((shape[1], block, block), F32)],
        ),
        out_shape=jax.ShapeDtypeStruct(shape, BF16),
        compiler_params=params(),
        cost_estimate=COST,
    )(pos, *mine, *other)


def assemble(pos, pieces, refs, w_ref, k):
    for (masks, _), ref in zip(pieces, refs):
        for i, m in enumerate(masks):
            w_ref[k, pos ^ m] = ref[i, k, 0]
    shards, rows, block = w_ref.shape[1:]
    return w_ref[k].reshape(shards * rows, block)


def piece_specs(pieces, first, n_levels, start=0):
    return [
        pl.BlockSpec(
            tuple(map(pl.Element, (p.shape[0], n_levels, 1, p.shape[3], p.shape[4]))),
            lambda j, *_: (0, first, j + start, 0, 0),
        )
        for _, p in pieces
    ]


def w_scratch(pieces, n_levels, shards):
    return pltpu.VMEM((n_levels, shards) + pieces[0][1].shape[3:], BF16)


def rows_kernel(
    pieces, distances, parts, pos_ref, hid_ref, cot_ref, fac_ref, back_ref, left_ref, right_ref,
    *refs
):
    n_cross = len(parts[0][1])
    n_src = n_cross * len(parts)
    w_refs = refs[n_src : n_src + len(pieces)]
    mixed_ref, grad_ref, w_ref = refs[n_src + len(pieces) :][:3]
    block = cot_ref.shape[1]
    j = pl.program_id(0)
    pos = pos_ref[0]
    sources = join(j, parts, refs[:n_src], refs[-n_cross:])

    @pl.when(j == 0)
    def _():
        grad_ref[...] = jnp.zeros_like(grad_ref)

    cot = cot_ref[...]
    mixed = jnp.dot(fac_ref[...], right_ref[...], preferred_element_type=F32)
    for k, distance in enumerate(distances):
        weight = assemble(pos, pieces, w_refs, w_ref, k)
        there = aligned(j ^ distance, block)
        mixed += jnp.dot(hid_ref[:, there], weight, preferred_element_type=F32)
        term = lax.dot_general(cot, weight, NT, preferred_element_type=F32)
        if distance == 0:
            term += lax.dot_general(back_ref[...], left_ref[...], NT, preferred_element_type=F32)
        grad_ref[:, there] += term
    for k, source in enumerate(sources, len(distances)):
        weight = assemble(pos, pieces, w_refs, w_ref, k)
        mixed += jnp.dot(source[:, aligned(j, block)], weight, preferred_element_type=F32)
    mixed_ref[...] = mixed.astype(BF16)


def rows_terms(pos, hidden, cot, factor, back, low_left, low_right, parts, pieces, distances, n_blocks, shards):
    tok, ff = hidden.shape
    block = ff // n_blocks
    rank = factor.shape[1]
    n_cross = len(parts[0][1])
    n_levels = len(distances) + n_cross
    column = pl.BlockSpec((tok, block), lambda j, *_: (0, j))
    whole = pl.BlockSpec((tok, ff), lambda j, *_: (0, 0))
    low = pl.BlockSpec((tok, rank), lambda j, *_: (0, 0))
    sources = [value for _, part in parts for value in part]
    return pl.pallas_call(
        functools.partial(rows_kernel, pieces, distances, parts),
        grid_spec=pltpu.PrefetchScalarGridSpec(
            num_scalar_prefetch=1,
            grid=(n_blocks,),
            in_specs=[
                whole,
                column,
                low,
                low,
                pl.BlockSpec((block, rank), lambda j, *_: (j, 0)),
                pl.BlockSpec((rank, block), lambda j, *_: (0, j)),
            ]
            + [pl.BlockSpec(s.shape, lambda j, *_: (0, 0)) for s in sources]
            + piece_specs(pieces, 0, n_levels),
            out_specs=[column, whole],
            scratch_shapes=[w_scratch(pieces, n_levels, shards)]
            + [pltpu.VMEM((tok, ff), BF16)] * n_cross,
        ),
        out_shape=[jax.ShapeDtypeStruct((tok, ff), BF16), jax.ShapeDtypeStruct((tok, ff), F32)],
        compiler_params=params(),
        cost_estimate=COST,
    )(pos, hidden, cot, factor, back, low_left, low_right, *sources, *[p for _, p in pieces])


def back_kernel(pieces, n_levels, pos_ref, cot_ref, *refs):
    w_refs, (out_refs, w_ref) = refs[: len(pieces)], (refs[len(pieces) : -1], refs[-1])
    for k in range(n_levels):
        weight = assemble(pos_ref[0], pieces, w_refs, w_ref, k)
        term = lax.dot_general(cot_ref[...], weight, NT, preferred_element_type=F32)
        out_refs[k][...] = term.astype(BF16)


def back_terms(pos, cot, pieces, first, n_levels, shards, start, count):
    tok = cot.shape[0]
    block = pieces[0][1].shape[-1]
    column = pl.BlockSpec((tok, block), lambda j, *_: (0, j))
    return pl.pallas_call(
        functools.partial(back_kernel, pieces, n_levels),
        grid_spec=pltpu.PrefetchScalarGridSpec(
            num_scalar_prefetch=1,
            grid=(count,),
            in_specs=[pl.BlockSpec((tok, block), lambda j, *_: (0, j + start))]
            + piece_specs(pieces, first, n_levels, start),
            out_specs=[column] * n_levels,
            scratch_shapes=[w_scratch(pieces, n_levels, shards)],
        ),
        out_shape=[jax.ShapeDtypeStruct((tok, count * block), BF16)] * n_levels,
        compiler_params=params(),
        cost_estimate=COST,
    )(pos, cot, *[p for _, p in pieces])


def highest(mask):
    return 1 << mask.bit_length() - 1


def gather_pieces(own, shards, tie):
    half = own.shape[-1] // 2
    low, high, full = slice(0, half), slice(half, None), slice(None)
    far = {0: [(full, own)]}
    for mask in range(2, shards, 2):
        last_a, last_b = highest(mask), mask & -mask
        if last_a == last_b:
            far[mask] = [(full, swap(own, "dp", mask))]
            continue
        far[mask] = []
        for last, columns in ((last_a, low), (last_b, high)):
            for held, value in far[mask ^ last]:
                if held == full:
                    value = value[..., columns]
                elif held != columns:
                    continue
                far[mask].append((columns, swap(after(value, *tie), "dp", last)))
    near = [mask for mask in far if len(far[mask]) == 1]
    rest = [mask for mask in far if mask not in near]
    pieces = [(near, jnp.stack([far[mask][0][1] for mask in near]))]
    if rest:
        joined = [jnp.concatenate([value for _, value in far[mask]], axis=-1) for mask in rest]
        pieces.append((rest, jnp.stack(joined)))
    return pieces, [value for mask in far for _, value in far[mask]]


def with_pair(pieces, tie):
    return pieces + [
        ([mask | 1 for mask in masks], swap(after(value, *tie), "dp", 1))
        for masks, value in pieces
    ]


def scatter_sum(parts, shards, *ties):
    half = parts[0].shape[-1] // 2
    bits = list(range(shards.bit_length() - 2))
    totals, received = [], []
    for columns, order in ((slice(0, half), bits), (slice(half, None), bits[::-1])):
        terms = {
            q: [part[q][..., columns] for part in parts] for q in range(shards // 2)
        }
        for step, bit in enumerate(order):
            going = [q for q in sorted(terms) if q >> bit & 1]
            total = jnp.stack([sum(t.astype(F32) for t in terms[q]).astype(BF16) for q in going])
            if step < len(ties):
                total = after(total, *ties[step])
            got = swap(total, "dp", 2 << bit)
            terms = {q: terms[q] for q in terms if not q >> bit & 1}
            for place, q in enumerate(going):
                terms[q ^ 1 << bit] = terms[q ^ 1 << bit] + [got[place]]
        received.append(terms[0][-1])
        totals.append(sum(t.astype(F32) for t in terms[0]))
    return totals, received


def gather_rows(value, shards):
    pos = lax.axis_index("dp")
    for bit in range(shards.bit_length() - 1)[::-1]:
        other = swap(value, "dp", 1 << bit)
        first = pos >> bit & 1 == 0
        pair = jnp.where(first, value, other), jnp.where(first, other, value)
        value = jnp.stack(pair, axis=shards.bit_length() - 1 - bit)
    return value


def per_device(hidden, cotangent, blocks, low_left, low_right):
    tok, ff = hidden.shape
    n_blocks, block = blocks.shape[1], blocks.shape[3]
    shards = lax.axis_size("dp")
    local_bits = n_blocks.bit_length() - 1
    cross_bits = lax.axis_size("tensor").bit_length() - 1
    n_local = 1 + local_bits
    scale = 1.0 / (tok * shards) ** 0.5
    pos = lax.axis_index("dp").astype(jnp.int32).reshape(1)

    factors = jnp.concatenate(
        [
            jnp.dot(hidden, low_left, preferred_element_type=F32),
            lax.dot_general(cotangent, low_right, NT, preferred_element_type=F32),
        ],
        axis=1,
    ).astype(BF16)
    rank = low_left.shape[1]

    def add(value, other):
        return (value.astype(F32) + other.astype(F32)).astype(BF16)

    cuts = [0, max(1, n_blocks // 4) * block, max(2, n_blocks // 2) * block, ff]
    both = swap(jnp.stack([hidden, cotangent]), "dp", 1)
    remote, ready = [], []
    for number, (start, stop) in enumerate(zip(cuts, cuts[1:])):
        part = after(hidden[:, start:stop], *ready, *([both] if ready else []))
        ready = [
            swap(
                jnp.concatenate([part, factors], axis=1) if bit == number < 2 else part,
                "tensor",
                1 << bit,
            )
            for bit in range(cross_bits)
        ]
        remote.append((stop - start, ready))
        if number < 2:
            factors = add(factors, ready[number][:, stop - start :])
        if number == 1:
            for bit in range(2, cross_bits):
                factors = add(factors, swap(factors, "tensor", 1 << bit))
    factor, back = factors[:, :rank], factors[:, rank:]

    pieces, gathered = gather_pieces(blocks, shards, remote[0][1] + remote[1][1])
    direct = gathered[1:3]
    distances = [0] + [1 << level for level in range(local_bits)]
    their_factors = swap(after(factors, *direct, *remote[1][1]), "dp", 1)
    kept = pair_grads(
        pos, (hidden, cotangent, factors), (both, both, their_factors), distances, n_blocks,
        shards, scale,
    )

    pieces = with_pair(pieces, [their_factors])
    cuts = [0, max(1, n_blocks * 7 // 16), max(2, n_blocks * 3 // 4), n_blocks]
    sent, returned, ready = [], [], remote[-1][1]
    for number, (start, stop) in enumerate(zip(cuts, cuts[1:])):
        terms = back_terms(
            pos, after(cotangent, *(returned[0] if number > 1 else ())), pieces, n_local,
            cross_bits, shards, start, stop - start,
        )
        ready = [swap(after(t, *ready), "tensor", 1 << bit) for bit, t in enumerate(terms)]
        sent.append(list(terms))
        returned.append(ready)
    keep, send = block_grads(pos, after(cotangent, *sent[0]), remote, n_blocks, shards, scale)
    crossed = swap(send, "dp", 1)
    grads_local, received = scatter_sum(
        [kept], shards, gathered + remote[2][1], returned[0] + sent[1] + [keep]
    )
    mixed_rows, grad_in = rows_terms(
        pos, hidden, after(cotangent, crossed), factor, back, low_left, low_right, remote,
        pieces, distances, n_blocks, shards,
    )

    low = jnp.concatenate([part[n_local] for part in grads_local], axis=-1).astype(BF16)
    low = gather_rows(low, shards).reshape(ff, 2 * rank).astype(F32)
    grad_left, grad_right = low[:, :rank], low[:, rank:].T

    grads_cross, _ = scatter_sum(
        [keep, crossed], shards, received + returned[1] + sent[2] + [mixed_rows]
    )
    grad_blocks = jnp.concatenate(
        [
            jnp.concatenate([a[:n_local], b], axis=0)
            for a, b in zip(grads_local, grads_cross)
        ],
        axis=-1,
    )

    returned = [jnp.concatenate(pair, axis=1) for pair in zip(*returned)]
    grad_hidden = (grad_in + sum(term.astype(F32) for term in returned)).astype(BF16)
    return (mixed_rows, grad_hidden, grad_blocks, grad_left, grad_right)


def solution(mesh):
    placed = (
        P("dp", "tensor"),
        P("dp", "tensor"),
        P(None, "tensor", "dp", None),
        P("tensor", None),
        P(None, "tensor"),
    )
    return jax.shard_map(
        per_device, mesh=mesh, in_specs=placed, out_specs=placed, check_vma=False
    )
```

time: 387 us -> 250 us (0.65)
  waiting for transfers between devices: 222 us -> 101 us
  between operations: 14.6 us -> 1.45 us
  other arithmetic: 13.7 us -> 22.5 us
  Pallas kernels: 54.5 us -> 50.4 us
    ppermute x38 -> x32, waiting for transfers between devices: 192 us -> 101 us  [swap(): lax.ppermute(value, axis, [(i, i ^ mask) for i in range(lax.axis_size(axi...]
    psum x1 -> x0, waiting for transfers between devices: 29.6 us -> none  [per_device(): grad_left, grad_right = lax.psum((part_left, part_right), 'dp')]
    another operation x0 -> x17, other arithmetic: none -> 13.6 us  [the longest x9 4.11 us: scatter_sum(): jnp.stack([sum((t.astype(F32) for t in terms[q])).astype(BF16) for q in g...]
    pallas_call x4 -> x3, Pallas kernels: 45.5 us -> 38.3 us  [the longest x1 16.1 us: rows_terms(): pl.pallas_call(functools.partial(rows_kernel, pieces, distances, parts),...]
    squeeze x4 -> x5, local copies, waits for them, and re-layouts: 12.9 us -> 6.37 us  [the longest x3 6.33 us: scatter_sum(): part[q][..., columns]]
    convert_element_type x7 -> x3, other arithmetic: 6.67 us -> 0.33 us  [the longest x1 0.27 us: per_device(): low = gather_rows(low, shards).reshape(ff, 2 * rank).astype(F32)]
    pallas_call x1 -> x3, Pallas kernels: 9.04 us -> 12.1 us  [back_terms(): pl.pallas_call(functools.partial(back_kernel, pieces, n_levels), grid_spe...]
    unnamed x110 -> x139, local copies, waits for them, and re-layouts: 15.3 us -> 17.9 us
  transfers between devices with their start and end apart: 39 -> 32, of which waited for: 13 -> 13; matrix products, arithmetic and copies ran while one was open for 10% -> 14% of each run, Pallas kernels for 11% -> 20%
where the time goes in v2:
time: 250 us; the launch traced here: 249 us
  waiting for transfers between devices  101 us (40%)
  Pallas kernels  50.4 us (20%)
  starting transfers between devices  38.9 us (16%)
  local copies, waits for them, and re-layouts  34 us (14%)
  other arithmetic  22.5 us (9%)
    ppermute x32, waiting for transfers between devices, swap(): lax.ppermute(value, axis, [(i, i ^ mask) for i in range(lax.axis_size(axi...  101 us
    ppermute x32, starting transfers between devices, swap(): lax.ppermute(value, axis, [(i, i ^ mask) for i in range(lax.axis_size(axi...  38.9 us
    unnamed x139, local copies, waits for them, and re-layouts  17.9 us
    pallas_call x1, Pallas kernels, rows_terms(): pl.pallas_call(functools.partial(rows_kernel, pieces, distances, parts),...  16.1 us
    pallas_call x1, Pallas kernels, pair_grads(): pl.pallas_call(functools.partial(pair_kernel, distances, shards, scale),...  13.6 us
    pallas_call x3, Pallas kernels, back_terms(): pl.pallas_call(functools.partial(back_kernel, pieces, n_levels), grid_spe...  12.1 us
    pallas_call x1, Pallas kernels, block_grads(): pl.pallas_call(functools.partial(grads_kernel, n_levels, parts, shards, s...  8.51 us
    squeeze x3, local copies, waits for them, and re-layouts, scatter_sum(): part[q][..., columns]  6.33 us
  transfers between devices with their start and end apart: 32, of which 13 were waited for; matrix products, arithmetic and copies ran while one was open for 14% of the time, Pallas kernels for 20%

profile of v2, /device:TPU:0, one launch (start us, length us, event | category | flops | bytes accessed | tf_op | source)
XLA Modules:
  0.0 249.0 jit_solution(2172240678625814847)
XLA Ops:
  0.7 2.3 pad_maximum_fusion.1
  3.5 2.6 %collective-permute-start.1 = (bf16[7,16,32,256]{3,2,1,0:T(8,128)(2,1)S(1)}, bf16[7,16,32,256]{3,2,1,0:T(8,128)(2,1)S(1)}, u32[]{:S(2)}, u32[]{:S(2)}) collective-permute-start(bf16[7,16,32,256]{3,2,1,0:T(8,128)(2,1)S(1)} %copy-done.56), channel_id=1, source_target_pairs={{0,16},{4,20},{8,24},{12,28},{16,0},{20,4},{24,8},{28,12},{1,17},{... | collective-permute-start | bytes 5505032 | tf_op jit(solution)/shard_map/ppermute | solution.py:17
  6.1 1.5 collective-permute-start
  9.5 1.6 collective-permute-start.2
  11.2 2.6 %collective-permute-start.3 = (bf16[192,1024]{1,0:T(8,128)(2,1)S(1)}, bf16[192,1024]{1,0:T(8,128)(2,1)S(1)}, u32[]{:S(2)}, u32[]{:S(2)}) collective-permute-start(bf16[192,1024]{1,0:T(8,128)(2,1)S(1)} %get-tuple-element.100), channel_id=1, source_target_pairs={{0,2},{1,3},{2,0},{3,1},{4,6},{5,7},{6,4},{7,5},{8,10},{9,11},{10,... | collective-permute-start | bytes 1179656 | tf_op jit(solution)/shard_map/ppermute | solution.py:17
  13.7 17.3 %collective-permute-done.2.refs_0_ = bf16[192,1280]{1,0:T(8,128)(2,1)S(1)} collective-permute-done((bf16[192,1280]{1,0:T(8,128)(2,1)S(1)}, bf16[192,1280]{1,0:T(8,128)(2,1)S(1)}, u32[]{:S(2)}, u32[]{:S(2)}) %collective-permute-start.2) | collective-permute-done | bytes 491552 | tf_op jit(solution)/shard_map/ppermute | solution.py:17
  32.6 1.7 copy-done.5
  34.3 1.7 collective-permute-start.6
  36.0 2.5 collective-permute-start.5
  38.5 19.4 %collective-permute-done.6.refs_3_ = bf16[192,1280]{1,0:T(8,128)(2,1)S(1)} collective-permute-done((bf16[192,1280]{1,0:T(8,128)(2,1)S(1)}, bf16[192,1280]{1,0:T(8,128)(2,1)S(1)}, u32[]{:S(2)}, u32[]{:S(2)}) %collective-permute-start.6) | collective-permute-done | bytes 491552 | tf_op jit(solution)/shard_map/ppermute | solution.py:17
  59.6 3.0 %pad_maximum_fusion.refs_0_.refs_6_ = bf16[3,7,16,32,256]{4,3,2,1,0:T(8,128)(2,1)} fusion(bf16[1,7,16,32,256]{4,3,2,1,0:T(8,128)(2,1)S(1)} %bitcast.132, bf16[1,7,16,32,256]{4,3,2,1,0:T(8,128)(2,1)S(1)} %bitcast.133, bf16[1,7,16,32,256]{4,3,2,1,0:T(8,128)(2,1)S(1)} %bitcast.134), kind=kLoop, calls=%fused_computation | loop fusion | flops 5505024 | bytes 11010048 | tf_op jit(solution)/shard_map/stack | solution.py:292
  67.4 3.1 %collective-permute-start.13 = (bf16[192,2048]{1,0:T(8,128)(2,1)}, bf16[192,2048]{1,0:T(8,128)(2,1)S(1)}, u32[]{:S(2)}, u32[]{:S(2)}) collective-permute-start(bf16[192,2048]{1,0:T(8,128)(2,1)} %slice.197), channel_id=1, source_target_pairs={{0,2},{1,3},{2,0},{3,1},{4,6},{5,7},{6,4},{7,5},{8,10},{9,11},{10,... | collective-permute-start | bytes 2359304 | tf_op jit(solution)/shard_map/ppermute | solution.py:17
  70.5 1.9 copy-done.6
  72.4 13.6 %shard_map.97 = bf16[4,6,16,32,256]{4,3,2,1,0:T(8,128)(2,1)S(1)} custom-call(s32[1]{0:T(128)} %bitcast.pos_ref, bf16[192,4096]{1,0:T(8,128)(2,1)S(1)} %copy-done.1, bf16[192,4096]{1,0:T(8,128)(2,1)S(1)} %copy-done, bf16[192,256]{1,0:T(8,128)(2,1)S(1)} %add_convert_fusion.5.refs_2_, bf16[2,192,4096]{2,1,0:T(8,128)(2,1)S(1)} %copy-done.6, ...), custom_call_target="tpu_custom_call" | custom-call | flops 1 | bytes 1 | tf_op jit(solution)/shard_map/pallas_call | solution.py:131
  86.0 2.0 slice_bitcast_fusion.4
  88.4 1.8 maximum_bitcast_fusion.refs_1_.refs_7_
  90.9 12.2 %collective-permute-done.12.refs_4_ = bf16[192,2048]{1,0:T(8,128)(2,1)S(1)} collective-permute-done((bf16[192,2048]{1,0:T(8,128)(2,1)}, bf16[192,2048]{1,0:T(8,128)(2,1)S(1)}, u32[]{:S(2)}, u32[]{:S(2)}) %collective-permute-start.12) | collective-permute-done | bytes 786464 | tf_op jit(solution)/shard_map/ppermute | solution.py:17
  103.1 1.4 collective-permute-done.13.refs_5_
  104.5 1.4 collective-permute-start.21
  105.9 1.5 collective-permute-start.23
  107.4 5.3 %shard_map.92 = (bf16[192,1792]{1,0:T(8,128)(2,1)S(1)}, bf16[192,1792]{1,0:T(8,128)(2,1)S(1)}) custom-call(s32[1]{0:T(128)} %bitcast.pos_ref, bf16[192,4096]{1,0:T(8,128)(2,1)S(1)} %copy-done, bf16[3,7,16,32,256]{4,3,2,1,0:T(8,128)(2,1)} %pad_maximum_fusion.refs_0_.refs_6_, bf16[1,7,16,32,256]{4,3,2,1,0:T(8,128)(2,1)S(1)} %maximum_bitcast_fusion.refs_1_.refs_7_, ...), custom_call_target="tpu_custom_call" | custom-call | flops 1 | bytes 1 | tf_op jit(solution)/shard_map/pallas_call | solution.py:253
  113.1 2.6 %collective-permute-start.16 = (bf16[192,1792]{1,0:T(8,128)(2,1)S(1)}, bf16[192,1792]{1,0:T(8,128)(2,1)S(1)}, u32[]{:S(2)}, u32[]{:S(2)}) collective-permute-start(bf16[192,1792]{1,0:T(8,128)(2,1)S(1)} %get-tuple-element.53), channel_id=1, source_target_pairs={{0,2},{1,3},{2,0},{3,1},{4,6},{5,7},{6,4},{7,5},{8,10},{9,11},{10,... | collective-permute-start | bytes 2064392 | tf_op jit(solution)/shard_map/ppermute | solution.py:17
  115.7 22.6 %collective-permute-done.21 = bf16[2,6,16,32,128]{4,3,2,1,0:T(8,128)(2,1)S(1)} collective-permute-done((bf16[2,6,16,32,128]{4,3,2,1,0:T(8,128)(2,1)S(1)}, bf16[2,6,16,32,128]{4,3,2,1,0:T(8,128)(2,1)S(1)}, u32[]{:S(2)}, u32[]{:S(2)}) %collective-permute-start.21) | collective-permute-done | bytes 1572896 | tf_op jit(solution)/shard_map/ppermute | solution.py:17
  139.3 1.7 fusion.4
  141.0 3.9 %shard_map.95 = (bf16[192,1280]{1,0:T(8,128)(2,1)S(1)}, bf16[192,1280]{1,0:T(8,128)(2,1)S(1)}) custom-call(s32[1]{0:T(128)} %bitcast.pos_ref, bf16[192,4096]{1,0:T(8,128)(2,1)S(1)} %copy-done, bf16[3,7,16,32,256]{4,3,2,1,0:T(8,128)(2,1)} %pad_maximum_fusion.refs_0_.refs_6_, bf16[1,7,16,32,256]{4,3,2,1,0:T(8,128)(2,1)S(1)} %maximum_bitcast_fusion.refs_1_.refs_7_, ...), custom_call_target="tpu_custom_call" | custom-call | flops 1 | bytes 1 | tf_op jit(solution)/shard_map/pallas_call | solution.py:253
  145.0 8.5 %shard_map.93 = (bf16[4,2,16,32,256]{4,3,2,1,0:T(8,128)(2,1)S(1)}, bf16[4,2,16,32,256]{4,3,2,1,0:T(8,128)(2,1)}) custom-call(s32[1]{0:T(128)} %bitcast.pos_ref, bf16[192,4096]{1,0:T(8,128)(2,1)S(1)} %copy-done, bf16[192,1280]{1,0:T(8,128)(2,1)S(1)} %copy-done.18, bf16[192,1024]{1,0:T(8,128)(2,1)S(1)} %copy-done.26, bf16[192,1024]{1,0:T(8,128)(2,1)S(1)} %copy-done.29, ...), custom_call_target="tpu_custom_call" | custom-call | flops 1 | bytes 1 | tf_op jit(solution)/shard_map/pallas_call | solution.py:78
  153.5 1.3 copy-done.23
  156.6 1.5 collective-permute-start.22
  159.0 13.5 %collective-permute-done.22 = bf16[1,6,16,32,128]{4,3,2,1,0:T(8,128)(2,1)} collective-permute-done((bf16[1,6,16,32,128]{4,3,2,1,0:T(8,128)(2,1)}, bf16[1,6,16,32,128]{4,3,2,1,0:T(8,128)(2,1)}, u32[]{:S(2)}, u32[]{:S(2)}) %collective-permute-start.22) | collective-permute-done | bytes 786464 | tf_op jit(solution)/shard_map/ppermute | solution.py:17
  172.5 1.3 collective-permute-done.24
  173.8 3.2 %fusion.3 = (f32[6,16,32,128]{3,2,1,0:T(8,128)S(1)}, f32[6,16,32,128]{3,2,1,0:T(8,128)S(1)}) fusion(bf16[2,6,16,32,128]{4,3,2,1,0:T(8,128)(2,1)} %copy-done.57, bf16[6,16,32,256]{3,2,1,0:T(8,128)(2,1)} %get-tuple-element.79, bf16[1,6,16,32,128]{4,3,2,1,0:T(8,128)(2,1)} %collective-permute-done.22, bf16[1,6,16,32,128]{4,3,2,1,0:T(8,128)(2,1)} %collective-permute-done.24, ...), kind=kLoop, calls=%fused_computation.20 | loop fusion | flops 3932160 | bytes 7864320 | tf_op jit(solution)/shard_map/add | solution.py:324
  179.9 3.2 %collective-permute-start.17 = (bf16[192,1280]{1,0:T(8,128)(2,1)S(1)}, bf16[192,1280]{1,0:T(8,128)(2,1)S(1)}, u32[]{:S(2)}, u32[]{:S(2)}) collective-permute-start(bf16[192,1280]{1,0:T(8,128)(2,1)S(1)} %copy-done.34), channel_id=1, source_target_pairs={{0,1},{1,0},{2,3},{3,2},{4,5},{5,4},{6,7},{7,6},{8,9},{9,8},{10,11... | collective-permute-start | bytes 1474568 | tf_op jit(solution)/shard_map/ppermute | solution.py:17
  183.1 2.9 %shard_map.96 = (bf16[192,1024]{1,0:T(8,128)(2,1)S(1)}, bf16[192,1024]{1,0:T(8,128)(2,1)S(1)}) custom-call(s32[1]{0:T(128)} %bitcast.pos_ref, bf16[192,4096]{1,0:T(8,128)(2,1)S(1)} %copy-done, bf16[3,7,16,32,256]{4,3,2,1,0:T(8,128)(2,1)} %pad_maximum_fusion.refs_0_.refs_6_, bf16[1,7,16,32,256]{4,3,2,1,0:T(8,128)(2,1)S(1)} %maximum_bitcast_fusion.refs_1_.refs_7_, ...), custom_call_target="tpu_custom_call" | custom-call | flops 1 | bytes 1 | tf_op jit(solution)/shard_map/pallas_call | solution.py:253
  188.8 3.1 %slice_bitcast_fusion.15 = (bf16[2,16,32,256]{3,2,1,0:T(8,128)(2,1)S(1)}, bf16[2,16,32,256]{3,2,1,0:T(8,128)(2,1)}, bf16[2,16,32,256]{3,2,1,0:T(8,128)(2,1)S(1)}, bf16[2,16,32,256]{3,2,1,0:T(8,128)(2,1)}) fusion(bf16[4,2,16,32,256]{4,3,2,1,0:T(8,128)(2,1)} %collective-permute-done.14), kind=kLoop, calls=%fused_computation.38 | loop fusion | bytes 4194304 | tf_op jit(solution)/shard_map/squeeze | solution.py:312
  192.1 16.1 %shard_map.94 = (bf16[192,4096]{1,0:T(8,128)(2,1)}, f32[192,4096]{1,0:T(8,128)S(1)}) custom-call(s32[1]{0:T(128)} %bitcast.pos_ref, bf16[192,4096]{1,0:T(8,128)(2,1)S(1)} %copy-done.2, bf16[192,4096]{1,0:T(8,128)(2,1)S(1)} %copy-done, bf16[192,128]{1,0:T(8,128)(2,1)S(1)} %get-tuple-element.112.fac_ref, bf16[192,128]{1,0:T(8,128)(2,1)S(1)} %get-tuple-element.111.back_ref, ...), custom_call_target="tpu_custom_call" | custom-call | flops 1 | bytes 1 | tf_op jit(solution)/shard_map/pallas_call | solution.py:216
  208.2 1.7 copy-done.15
  212.8 1.9 collective-permute-start.19
  215.8 2.5 %slice.287 = f32[5,16,32,128]{3,2,1,0:T(8,128)} slice(f32[6,16,32,128]{3,2,1,0:T(8,128)} %copy-done.41), slice={[0:5], [0:16], [0:32], [0:128]} | slice | bytes 2621440 | tf_op jit(solution)/shard_map/slice | solution.py:420
  222.2 1.6 collective-permute-start.27
  223.8 3.9 %collective-permute-done.19 = bf16[192,1024]{1,0:T(8,128)(2,1)S(1)} collective-permute-done((bf16[192,1024]{1,0:T(8,128)(2,1)S(1)}, bf16[192,1024]{1,0:T(8,128)(2,1)S(1)}, u32[]{:S(2)}, u32[]{:S(2)}) %collective-permute-start.19) | collective-permute-done | bytes 393248 | tf_op jit(solution)/shard_map/ppermute | solution.py:17
  227.8 2.4 collective-permute-done.20
  230.2 1.4 add_convert_fusion
  231.7 1.5 collective-permute-start.26
  233.1 4.0 %collective-permute-done.27 = bf16[2,2,16,32,128]{4,3,2,1,0:T(8,128)(2,1)S(1)} collective-permute-done((bf16[2,2,16,32,128]{4,3,2,1,0:T(8,128)(2,1)S(1)}, bf16[2,2,16,32,128]{4,3,2,1,0:T(8,128)(2,1)S(1)}, u32[]{:S(2)}, u32[]{:S(2)}) %collective-permute-start.27) | collective-permute-done | bytes 524320 | tf_op jit(solution)/shard_map/ppermute | solution.py:17
  240.1 1.6 slice_bitcast_fusion
  241.7 1.8 copy.12
  244.7 1.6 convert_add_fusion.7
  246.7 2.2 maximum_maximum_fusion
  (207 shorter events, 33.5 us)
Async XLA Ops:
  0.7 7.0 %copy-start.7 = (bf16[128,4096]{1,0:T(8,128)(2,1)S(1)}, bf16[128,4096]{1,0:T(8,128)(2,1)}, u32[]{:S(2)}) copy-start(bf16[128,4096]{1,0:T(8,128)(2,1)} %right_ref.1) | copy-start | bytes 3145732
  3.0 29.6 %collective-permute-start.4 = (bf16[2,192,4096]{2,1,0:T(8,128)(2,1)S(1)}, bf16[2,192,4096]{2,1,0:T(8,128)(2,1)S(1)}, u32[]{:S(2)}, u32[]{:S(2)}) collective-permute-start(bf16[2,192,4096]{2,1,0:T(8,128)(2,1)S(1)} %pad_maximum_fusion.1), channel_id=1, source_target_pairs={{0,4},{4,0},{8,12},{12,8},{16,20},{20,16},{24,28},{28,24},{1,5},{5... | collective-permute-start | bytes 9437192 | tf_op jit(solution)/shard_map/ppermute | solution.py:17
  3.5 55.2 %collective-permute-start.1 = (bf16[7,16,32,256]{3,2,1,0:T(8,128)(2,1)S(1)}, bf16[7,16,32,256]{3,2,1,0:T(8,128)(2,1)S(1)}, u32[]{:S(2)}, u32[]{:S(2)}) collective-permute-start(bf16[7,16,32,256]{3,2,1,0:T(8,128)(2,1)S(1)} %copy-done.56), channel_id=1, source_target_pairs={{0,16},{4,20},{8,24},{12,28},{16,0},{20,4},{24,8},{28,12},{1,17},{... | collective-permute-start | bytes 5505032 | tf_op jit(solution)/shard_map/ppermute | solution.py:17
  6.1 52.6 %collective-permute-start = (bf16[7,16,32,256]{3,2,1,0:T(8,128)(2,1)S(1)}, bf16[7,16,32,256]{3,2,1,0:T(8,128)(2,1)S(1)}, u32[]{:S(2)}, u32[]{:S(2)}) collective-permute-start(bf16[7,16,32,256]{3,2,1,0:T(8,128)(2,1)S(1)} %copy-done.56), channel_id=1, source_target_pairs={{0,8},{4,12},{8,0},{12,4},{16,24},{20,28},{24,16},{28,20},{1,9},{5... | collective-permute-start | bytes 5505032 | tf_op jit(solution)/shard_map/ppermute | solution.py:17
  9.5 21.5 %collective-permute-start.2 = (bf16[192,1280]{1,0:T(8,128)(2,1)S(1)}, bf16[192,1280]{1,0:T(8,128)(2,1)S(1)}, u32[]{:S(2)}, u32[]{:S(2)}) collective-permute-start(bf16[192,1280]{1,0:T(8,128)(2,1)S(1)} %pad_maximum_fusion.8), channel_id=1, source_target_pairs={{0,1},{1,0},{2,3},{3,2},{4,5},{5,4},{6,7},{7,6},{8,9},{9,8},{10,11... | collective-permute-start | bytes 1474568 | tf_op jit(solution)/shard_map/ppermute | solution.py:17
  11.2 20.7 %collective-permute-start.3 = (bf16[192,1024]{1,0:T(8,128)(2,1)S(1)}, bf16[192,1024]{1,0:T(8,128)(2,1)S(1)}, u32[]{:S(2)}, u32[]{:S(2)}) collective-permute-start(bf16[192,1024]{1,0:T(8,128)(2,1)S(1)} %get-tuple-element.100), channel_id=1, source_target_pairs={{0,2},{1,3},{2,0},{3,1},{4,6},{5,7},{6,4},{7,5},{8,10},{9,11},{10,... | collective-permute-start | bytes 1179656 | tf_op jit(solution)/shard_map/ppermute | solution.py:17
  34.3 23.6 %collective-permute-start.6 = (bf16[192,1280]{1,0:T(8,128)(2,1)S(1)}, bf16[192,1280]{1,0:T(8,128)(2,1)S(1)}, u32[]{:S(2)}, u32[]{:S(2)}) collective-permute-start(bf16[192,1280]{1,0:T(8,128)(2,1)S(1)} %pad_maximum_fusion.9), channel_id=1, source_target_pairs={{0,2},{1,3},{2,0},{3,1},{4,6},{5,7},{6,4},{7,5},{8,10},{9,11},{10,... | collective-permute-start | bytes 1474568 | tf_op jit(solution)/shard_map/ppermute | solution.py:17
  36.0 22.7 %collective-permute-start.5 = (bf16[192,1024]{1,0:T(8,128)(2,1)S(1)}, bf16[192,1024]{1,0:T(8,128)(2,1)S(1)}, u32[]{:S(2)}, u32[]{:S(2)}) collective-permute-start(bf16[192,1024]{1,0:T(8,128)(2,1)S(1)} %get-tuple-element.37), channel_id=1, source_target_pairs={{0,1},{1,0},{2,3},{3,2},{4,5},{5,4},{6,7},{7,6},{8,9},{9,8},{10,11... | collective-permute-start | bytes 1179656 | tf_op jit(solution)/shard_map/ppermute | solution.py:17
  59.5 3.0 %collective-permute-start.9 = (bf16[192,256]{1,0:T(8,128)(2,1)S(1)}, bf16[192,256]{1,0:T(8,128)(2,1)S(1)}, u32[]{:S(2)}, u32[]{:S(2)}) collective-permute-start(bf16[192,256]{1,0:T(8,128)(2,1)S(1)} %add_convert_fusion.5.refs_2_), channel_id=1, source_target_pairs={{0,4},{4,0},{8,12},{12,8},{16,20},{20,16},{24,28},{28,24},{1,5},{5... | collective-permute-start | bytes 294920 | tf_op jit(solution)/shard_map/ppermute | solution.py:17
  62.5 44.9 %collective-permute-start.10 = (bf16[3,7,16,32,256]{4,3,2,1,0:T(8,128)(2,1)}, bf16[3,7,16,32,256]{4,3,2,1,0:T(8,128)(2,1)}, u32[]{:S(2)}, u32[]{:S(2)}) collective-permute-start(bf16[3,7,16,32,256]{4,3,2,1,0:T(8,128)(2,1)} %pad_maximum_fusion.refs_0_.refs_6_), channel_id=1, source_target_pairs={{0,4},{4,0},{8,12},{12,8},{16,20},{20,16},{24,28},{28,24},{1,5},{5... | collective-permute-start | bytes 16515080 | tf_op jit(solution)/shard_map/ppermute | solution.py:17
  65.3 23.1 %collective-permute-start.8 = (bf16[7,16,32,128]{3,2,1,0:T(8,128)(2,1)}, bf16[7,16,32,128]{3,2,1,0:T(8,128)(2,1)}, u32[]{:S(2)}, u32[]{:S(2)}) collective-permute-start(bf16[7,16,32,128]{3,2,1,0:T(8,128)(2,1)} %slice.252), channel_id=1, source_target_pairs={{0,8},{4,12},{8,0},{12,4},{16,24},{20,28},{24,16},{28,20},{1,9},{5... | collective-permute-start | bytes 2752520 | tf_op jit(solution)/shard_map/ppermute | solution.py:17
  65.8 22.6 %collective-permute-start.7 = (bf16[7,16,32,128]{3,2,1,0:T(8,128)(2,1)}, bf16[7,16,32,128]{3,2,1,0:T(8,128)(2,1)}, u32[]{:S(2)}, u32[]{:S(2)}) collective-permute-start(bf16[7,16,32,128]{3,2,1,0:T(8,128)(2,1)} %slice.250), channel_id=1, source_target_pairs={{0,16},{4,20},{8,24},{12,28},{16,0},{20,4},{24,8},{28,12},{1,17},{... | collective-permute-start | bytes 2752520 | tf_op jit(solution)/shard_map/ppermute | solution.py:17
  67.4 35.7 %collective-permute-start.12 = (bf16[192,2048]{1,0:T(8,128)(2,1)}, bf16[192,2048]{1,0:T(8,128)(2,1)S(1)}, u32[]{:S(2)}, u32[]{:S(2)}) collective-permute-start(bf16[192,2048]{1,0:T(8,128)(2,1)} %slice.197), channel_id=1, source_target_pairs={{0,1},{1,0},{2,3},{3,2},{4,5},{5,4},{6,7},{7,6},{8,9},{9,8},{10,11... | collective-permute-start | bytes 2359304 | tf_op jit(solution)/shard_map/ppermute | solution.py:17
  67.4 37.1 %collective-permute-start.13 = (bf16[192,2048]{1,0:T(8,128)(2,1)}, bf16[192,2048]{1,0:T(8,128)(2,1)S(1)}, u32[]{:S(2)}, u32[]{:S(2)}) collective-permute-start(bf16[192,2048]{1,0:T(8,128)(2,1)} %slice.197), channel_id=1, source_target_pairs={{0,2},{1,3},{2,0},{3,1},{4,6},{5,7},{6,4},{7,5},{8,10},{9,11},{10,... | collective-permute-start | bytes 2359304 | tf_op jit(solution)/shard_map/ppermute | solution.py:17
  90.2 17.3 %collective-permute-start.11 = (bf16[1,7,16,32,256]{4,3,2,1,0:T(8,128)(2,1)S(1)}, bf16[1,7,16,32,256]{4,3,2,1,0:T(8,128)(2,1)S(1)}, u32[]{:S(2)}, u32[]{:S(2)}) collective-permute-start(bf16[1,7,16,32,256]{4,3,2,1,0:T(8,128)(2,1)S(1)} %maximum_bitcast_fusion.refs_1_.refs_7_), channel_id=1, source_target_pairs={{0,4},{4,0},{8,12},{12,8},{16,20},{20,16},{24,28},{28,24},{1,5},{5... | collective-permute-start | bytes 5505032 | tf_op jit(solution)/shard_map/ppermute | solution.py:17
  103.1 41.8 %copy-start.11 = (bf16[192,2048]{1,0:T(8,128)(2,1)}, bf16[192,2048]{1,0:T(8,128)(2,1)S(1)}, u32[]{:S(2)}) copy-start(bf16[192,2048]{1,0:T(8,128)(2,1)S(1)} %collective-permute-done.12.refs_4_) | copy-start | bytes 2359300
  104.5 40.4 %copy-start.13 = (bf16[192,2048]{1,0:T(8,128)(2,1)}, bf16[192,2048]{1,0:T(8,128)(2,1)S(1)}, u32[]{:S(2)}) copy-start(bf16[192,2048]{1,0:T(8,128)(2,1)S(1)} %collective-permute-done.13.refs_5_) | copy-start | bytes 2359300
  104.5 33.8 %collective-permute-start.21 = (bf16[2,6,16,32,128]{4,3,2,1,0:T(8,128)(2,1)S(1)}, bf16[2,6,16,32,128]{4,3,2,1,0:T(8,128)(2,1)S(1)}, u32[]{:S(2)}, u32[]{:S(2)}) collective-permute-start(bf16[2,6,16,32,128]{4,3,2,1,0:T(8,128)(2,1)S(1)} %pad_maximum_fusion.2), channel_id=1, source_target_pairs={{0,8},{4,12},{8,0},{12,4},{16,24},{20,28},{24,16},{28,20},{1,9},{5... | collective-permute-start | bytes 4718600 | tf_op jit(solution)/shard_map/ppermute | solution.py:17
  105.9 33.4 %collective-permute-start.23 = (bf16[2,6,16,32,128]{4,3,2,1,0:T(8,128)(2,1)S(1)}, bf16[2,6,16,32,128]{4,3,2,1,0:T(8,128)(2,1)S(1)}, u32[]{:S(2)}, u32[]{:S(2)}) collective-permute-start(bf16[2,6,16,32,128]{4,3,2,1,0:T(8,128)(2,1)S(1)} %pad_maximum_fusion.3), channel_id=1, source_target_pairs={{0,16},{4,20},{8,24},{12,28},{16,0},{20,4},{24,8},{28,12},{1,17},{... | collective-permute-start | bytes 4718600 | tf_op jit(solution)/shard_map/ppermute | solution.py:17
  107.4 33.5 %copy-start.3 = (bf16[1,7,16,32,256]{4,3,2,1,0:T(8,128)(2,1)}, bf16[1,7,16,32,256]{4,3,2,1,0:T(8,128)(2,1)S(1)}, u32[]{:S(2)}) copy-start(bf16[1,7,16,32,256]{4,3,2,1,0:T(8,128)(2,1)S(1)} %collective-permute-done.11.refs_3_.refs_9_) | copy-start | bytes 5505028
  112.7 42.1 %collective-permute-start.15 = (bf16[192,1792]{1,0:T(8,128)(2,1)S(1)}, bf16[192,1792]{1,0:T(8,128)(2,1)S(1)}, u32[]{:S(2)}, u32[]{:S(2)}) collective-permute-start(bf16[192,1792]{1,0:T(8,128)(2,1)S(1)} %get-tuple-element.51), channel_id=1, source_target_pairs={{0,1},{1,0},{2,3},{3,2},{4,5},{5,4},{6,7},{7,6},{8,9},{9,8},{10,11... | collective-permute-start | bytes 2064392 | tf_op jit(solution)/shard_map/ppermute | solution.py:17
  113.1 41.7 %collective-permute-start.16 = (bf16[192,1792]{1,0:T(8,128)(2,1)S(1)}, bf16[192,1792]{1,0:T(8,128)(2,1)S(1)}, u32[]{:S(2)}, u32[]{:S(2)}) collective-permute-start(bf16[192,1792]{1,0:T(8,128)(2,1)S(1)} %get-tuple-element.53), channel_id=1, source_target_pairs={{0,2},{1,3},{2,0},{3,1},{4,6},{5,7},{6,4},{7,5},{8,10},{9,11},{10,... | collective-permute-start | bytes 2064392 | tf_op jit(solution)/shard_map/ppermute | solution.py:17
  145.0 8.5 %copy-start.31 = (bf16[192,1280]{1,0:T(8,128)(2,1)}, bf16[192,1280]{1,0:T(8,128)(2,1)S(1)}, u32[]{:S(2)}) copy-start(bf16[192,1280]{1,0:T(8,128)(2,1)S(1)} %get-tuple-element.58) | copy-start | bytes 1474564
  145.0 8.5 %copy-start.33 = (bf16[192,1280]{1,0:T(8,128)(2,1)}, bf16[192,1280]{1,0:T(8,128)(2,1)S(1)}, u32[]{:S(2)}) copy-start(bf16[192,1280]{1,0:T(8,128)(2,1)S(1)} %get-tuple-element.54) | copy-start | bytes 1474564
  156.6 15.9 %collective-permute-start.22 = (bf16[1,6,16,32,128]{4,3,2,1,0:T(8,128)(2,1)}, bf16[1,6,16,32,128]{4,3,2,1,0:T(8,128)(2,1)}, u32[]{:S(2)}, u32[]{:S(2)}) collective-permute-start(bf16[1,6,16,32,128]{4,3,2,1,0:T(8,128)(2,1)} %get-tuple-element.64), channel_id=1, source_target_pairs={{0,16},{4,20},{8,24},{12,28},{16,0},{20,4},{24,8},{28,12},{1,17},{... | collective-permute-start | bytes 2359304 | tf_op jit(solution)/shard_map/ppermute | solution.py:17
  158.1 15.7 %collective-permute-start.24 = (bf16[1,6,16,32,128]{4,3,2,1,0:T(8,128)(2,1)}, bf16[1,6,16,32,128]{4,3,2,1,0:T(8,128)(2,1)}, u32[]{:S(2)}, u32[]{:S(2)}) collective-permute-start(bf16[1,6,16,32,128]{4,3,2,1,0:T(8,128)(2,1)} %get-tuple-element.66), channel_id=1, source_target_pairs={{0,8},{4,12},{8,0},{12,4},{16,24},{20,28},{24,16},{28,20},{1,9},{5... | collective-permute-start | bytes 2359304 | tf_op jit(solution)/shard_map/ppermute | solution.py:17
  158.9 29.8 %collective-permute-start.14 = (bf16[4,2,16,32,256]{4,3,2,1,0:T(8,128)(2,1)}, bf16[4,2,16,32,256]{4,3,2,1,0:T(8,128)(2,1)}, u32[]{:S(2)}, u32[]{:S(2)}) collective-permute-start(bf16[4,2,16,32,256]{4,3,2,1,0:T(8,128)(2,1)} %get-tuple-element.47), channel_id=1, source_target_pairs={{0,4},{4,0},{8,12},{12,8},{16,20},{20,16},{24,28},{28,24},{1,5},{5... | collective-permute-start | bytes 6291464 | tf_op jit(solution)/shard_map/ppermute | solution.py:17
  177.0 9.1 %copy-start.41 = (f32[6,16,32,128]{3,2,1,0:T(8,128)}, f32[6,16,32,128]{3,2,1,0:T(8,128)S(1)}, u32[]{:S(2)}) copy-start(f32[6,16,32,128]{3,2,1,0:T(8,128)S(1)} %get-tuple-element.96) | copy-start | bytes 4718596
  178.2 7.9 %collective-permute-start.29 = (bf16[16,32,256]{2,1,0:T(8,128)(2,1)S(1)}, bf16[16,32,256]{2,1,0:T(8,128)(2,1)S(1)}, u32[]{:S(2)}, u32[]{:S(2)}) collective-permute-start(bf16[16,32,256]{2,1,0:T(8,128)(2,1)S(1)} %pad_maximum_fusion.10), channel_id=1, source_target_pairs={{0,16},{4,20},{8,24},{12,28},{16,0},{20,4},{24,8},{28,12},{1,17},{... | collective-permute-start | bytes 786440 | tf_op jit(solution)/shard_map/ppermute | solution.py:17
  179.9 12.0 %copy-start.50 = (bf16[2,16,32,256]{3,2,1,0:T(8,128)(2,1)}, bf16[2,16,32,256]{3,2,1,0:T(8,128)(2,1)S(1)}, u32[]{:S(2)}) copy-start(bf16[2,16,32,256]{3,2,1,0:T(8,128)(2,1)S(1)} %get-tuple-element.87) | copy-start | bytes 1572868
  179.9 31.0 %collective-permute-start.17 = (bf16[192,1280]{1,0:T(8,128)(2,1)S(1)}, bf16[192,1280]{1,0:T(8,128)(2,1)S(1)}, u32[]{:S(2)}, u32[]{:S(2)}) collective-permute-start(bf16[192,1280]{1,0:T(8,128)(2,1)S(1)} %copy-done.34), channel_id=1, source_target_pairs={{0,1},{1,0},{2,3},{3,2},{4,5},{5,4},{6,7},{7,6},{8,9},{9,8},{10,11... | collective-permute-start | bytes 1474568 | tf_op jit(solution)/shard_map/ppermute | solution.py:17
  183.1 27.7 %collective-permute-start.18 = (bf16[192,1280]{1,0:T(8,128)(2,1)S(1)}, bf16[192,1280]{1,0:T(8,128)(2,1)S(1)}, u32[]{:S(2)}, u32[]{:S(2)}) collective-permute-start(bf16[192,1280]{1,0:T(8,128)(2,1)S(1)} %copy-done.32), channel_id=1, source_target_pairs={{0,2},{1,3},{2,0},{3,1},{4,6},{5,7},{6,4},{7,5},{8,10},{9,11},{10,... | collective-permute-start | bytes 1474568 | tf_op jit(solution)/shard_map/ppermute | solution.py:17
  187.9 31.6 %collective-permute-start.30 = (bf16[16,2,32,256]{3,2,0,1:T(8,128)(2,1)}, bf16[16,2,32,256]{3,2,0,1:T(8,128)(2,1)}, u32[]{:S(2)}, u32[]{:S(2)}) collective-permute-start(bf16[16,2,32,256]{3,2,0,1:T(8,128)(2,1)} %pad_maximum_fusion.7), channel_id=1, source_target_pairs={{0,8},{4,12},{8,0},{12,4},{16,24},{20,28},{24,16},{28,20},{1,9},{5... | collective-permute-start | bytes 1572872 | tf_op jit(solution)/shard_map/ppermute | solution.py:17
  191.9 16.3 %copy-start.52 = (bf16[2,16,32,256]{3,2,1,0:T(8,128)(2,1)}, bf16[2,16,32,256]{3,2,1,0:T(8,128)(2,1)S(1)}, u32[]{:S(2)}) copy-start(bf16[2,16,32,256]{3,2,1,0:T(8,128)(2,1)S(1)} %get-tuple-element.91) | copy-start | bytes 1572868
  210.9 7.5 %copy-start.40 = (f32[6,16,32,128]{3,2,1,0:T(8,128)S(1)}, f32[6,16,32,128]{3,2,1,0:T(8,128)}, u32[]{:S(2)}) copy-start(f32[6,16,32,128]{3,2,1,0:T(8,128)} %copy-done.39) | copy-start | bytes 4718596
  211.8 9.5 %collective-permute-start.25 = (bf16[2,2,16,32,128]{4,3,2,1,0:T(8,128)(2,1)}, bf16[2,2,16,32,128]{4,3,2,1,0:T(8,128)(2,1)S(1)}, u32[]{:S(2)}, u32[]{:S(2)}) collective-permute-start(bf16[2,2,16,32,128]{4,3,2,1,0:T(8,128)(2,1)} %pad_maximum_fusion.5), channel_id=1, source_target_pairs={{0,8},{4,12},{8,0},{12,4},{16,24},{20,28},{24,16},{28,20},{1,9},{5... | collective-permute-start | bytes 1572872 | tf_op jit(solution)/shard_map/ppermute | solution.py:17
  212.8 14.9 %collective-permute-start.19 = (bf16[192,1024]{1,0:T(8,128)(2,1)S(1)}, bf16[192,1024]{1,0:T(8,128)(2,1)S(1)}, u32[]{:S(2)}, u32[]{:S(2)}) collective-permute-start(bf16[192,1024]{1,0:T(8,128)(2,1)S(1)} %copy-done.38), channel_id=1, source_target_pairs={{0,1},{1,0},{2,3},{3,2},{4,5},{5,4},{6,7},{7,6},{8,9},{9,8},{10,11... | collective-permute-start | bytes 1179656 | tf_op jit(solution)/shard_map/ppermute | solution.py:17
  214.7 15.5 %collective-permute-start.20 = (bf16[192,1024]{1,0:T(8,128)(2,1)S(1)}, bf16[192,1024]{1,0:T(8,128)(2,1)S(1)}, u32[]{:S(2)}, u32[]{:S(2)}) collective-permute-start(bf16[192,1024]{1,0:T(8,128)(2,1)S(1)} %copy-done.36), channel_id=1, source_target_pairs={{0,2},{1,3},{2,0},{3,1},{4,6},{5,7},{6,4},{7,5},{8,10},{9,11},{10,... | collective-permute-start | bytes 1179656 | tf_op jit(solution)/shard_map/ppermute | solution.py:17
  219.5 10.7 %copy-start.62 = (bf16[192,1792]{1,0:T(8,128)(2,1)S(1)}, bf16[192,1792]{1,0:T(8,128)(2,1)}, u32[]{:S(2)}) copy-start(bf16[192,1792]{1,0:T(8,128)(2,1)} %copy-done.61) | copy-start | bytes 2064388
  219.5 10.7 %copy-start.66 = (bf16[192,1280]{1,0:T(8,128)(2,1)S(1)}, bf16[192,1280]{1,0:T(8,128)(2,1)}, u32[]{:S(2)}) copy-start(bf16[192,1280]{1,0:T(8,128)(2,1)} %copy-done.65) | copy-start | bytes 1474564
  219.5 10.6 %copy-start.68 = (bf16[192,1280]{1,0:T(8,128)(2,1)S(1)}, bf16[192,1280]{1,0:T(8,128)(2,1)}, u32[]{:S(2)}) copy-start(bf16[192,1280]{1,0:T(8,128)(2,1)} %copy-done.67) | copy-start | bytes 1474564
  220.8 9.4 %copy-start.16 = (f32[192,4096]{1,0:T(8,128)S(1)}, f32[192,4096]{1,0:T(8,128)}, u32[]{:S(2)}) copy-start(f32[192,4096]{1,0:T(8,128)} %copy-done.15) | copy-start | bytes 9437188
  220.9 9.3 %copy-start.60 = (bf16[192,1792]{1,0:T(8,128)(2,1)S(1)}, bf16[192,1792]{1,0:T(8,128)(2,1)}, u32[]{:S(2)}) copy-start(bf16[192,1792]{1,0:T(8,128)(2,1)} %copy-done.59) | copy-start | bytes 2064388
  220.9 18.2 %collective-permute-start.31 = (bf16[16,2,2,32,256]{4,3,0,1,2:T(8,128)(2,1)S(1)}, bf16[16,2,2,32,256]{4,3,0,1,2:T(8,128)(2,1)S(1)}, u32[]{:S(2)}, u32[]{:S(2)}) collective-permute-start(bf16[16,2,2,32,256]{4,3,0,1,2:T(8,128)(2,1)S(1)} %pad_maximum_fusion.4), channel_id=1, source_target_pairs={{0,4},{4,0},{8,12},{12,8},{16,20},{20,16},{24,28},{28,24},{1,5},{5... | collective-permute-start | bytes 3145736 | tf_op jit(solution)/shard_map/ppermute | solution.py:17
  221.4 10.3 %copy-start.63 = (bf16[2,2,16,32,128]{4,3,2,1,0:T(8,128)(2,1)}, bf16[2,2,16,32,128]{4,3,2,1,0:T(8,128)(2,1)S(1)}, u32[]{:S(2)}) copy-start(bf16[2,2,16,32,128]{4,3,2,1,0:T(8,128)(2,1)S(1)} %collective-permute-done.25) | copy-start | bytes 1572868
  222.2 14.9 %collective-permute-start.27 = (bf16[2,2,16,32,128]{4,3,2,1,0:T(8,128)(2,1)S(1)}, bf16[2,2,16,32,128]{4,3,2,1,0:T(8,128)(2,1)S(1)}, u32[]{:S(2)}, u32[]{:S(2)}) collective-permute-start(bf16[2,2,16,32,128]{4,3,2,1,0:T(8,128)(2,1)S(1)} %pad_maximum_fusion.6), channel_id=1, source_target_pairs={{0,16},{4,20},{8,24},{12,28},{16,0},{20,4},{24,8},{28,12},{1,17},{... | collective-permute-start | bytes 1572872 | tf_op jit(solution)/shard_map/ppermute | solution.py:17
  231.7 11.9 %collective-permute-start.26 = (bf16[1,2,16,32,128]{4,3,2,1,0:T(8,128)(2,1)S(1)}, bf16[1,2,16,32,128]{4,3,2,1,0:T(8,128)(2,1)}, u32[]{:S(2)}, u32[]{:S(2)}) collective-permute-start(bf16[1,2,16,32,128]{4,3,2,1,0:T(8,128)(2,1)S(1)} %get-tuple-element.105), channel_id=1, source_target_pairs={{0,16},{4,20},{8,24},{12,28},{16,0},{20,4},{24,8},{28,12},{1,17},{... | collective-permute-start | bytes 786440 | tf_op jit(solution)/shard_map/ppermute | solution.py:17
  238.0 6.7 %collective-permute-start.28 = (bf16[1,2,16,32,128]{4,3,2,1,0:T(8,128)(2,1)}, bf16[1,2,16,32,128]{4,3,2,1,0:T(8,128)(2,1)}, u32[]{:S(2)}, u32[]{:S(2)}) collective-permute-start(bf16[1,2,16,32,128]{4,3,2,1,0:T(8,128)(2,1)} %fusion.13), channel_id=1, source_target_pairs={{0,8},{4,12},{8,0},{12,4},{16,24},{20,28},{24,16},{28,20},{1,9},{5... | collective-permute-start | bytes 786440 | tf_op jit(solution)/shard_map/ppermute | solution.py:17
  (53 other events, 164.4 us)

commit v3 on v2

--- a/solution.py
+++ b/solution.py
@@ -48,48 +48,49 @@
     return joined
 
 
-def grads_kernel(levels, parts, shards, scale, pos_ref, cot_ref, *refs):
-    joined = len(parts[0][1])
-    sources = join(pl.program_id(0), parts, refs[: len(refs) - 3 - joined], refs[len(refs) - joined :])
-    keep_ref, send_ref, tmp_ref = refs[len(refs) - 3 - joined : len(refs) - joined]
-    block = cot_ref.shape[1]
-    rows = block // shards
-    j = pl.program_id(0)
+def grads_kernel(n_parts, n_levels, shards, scale, pos_ref, *refs):
+    cots, sources = refs[:n_parts], refs[n_parts:-3]
+    keep_ref, send_ref, tmp_ref = refs[-3:]
+    rows = cots[0].shape[1] // shards
     pos = pos_ref[0]
-    cot = cot_ref[...]
-    for k in range(levels):
-        values = sources[k][:, aligned(j, block)]
-        tmp_ref[k] = lax.dot_general(values, cot, TN, preferred_element_type=F32) * scale
-        for m in range(shards):
-            part = tmp_ref[k, aligned(pos ^ m, rows), :].astype(BF16)
-            (send_ref if m & 1 else keep_ref)[m >> 1, k, 0] = part
+    for p, cot_ref in enumerate(cots):
+        for k in range(n_levels):
+            values = sources[p * n_levels + k][...]
+            term = lax.dot_general(values, cot_ref[...], TN, preferred_element_type=F32)
+            tmp_ref[p, k] = term * scale
+            for m in range(shards):
+                part = tmp_ref[p, k, aligned(pos ^ m, rows), :].astype(BF16)
+                (send_ref if m & 1 else keep_ref)[m >> 1, k, p, 0] = part
 
 
 def block_grads(pos, cot, parts, n_blocks, shards, scale):
     tok, ff = cot.shape
     block = ff // n_blocks
     rows = block // shards
-    n_levels = len(parts[0][1])
-    sources = [value for _, part in parts for value in part]
-    part = jax.ShapeDtypeStruct((shards // 2, n_levels, n_blocks, rows, block), BF16)
+    n_parts, n_levels = len(parts), len(parts[0][1])
+    steps = n_blocks // n_parts
+    part = jax.ShapeDtypeStruct((shards // 2, n_levels, n_parts, steps, rows, block), BF16)
     part_spec = pl.BlockSpec(
-        (shards // 2, n_levels, 1, rows, block), lambda j, *_: (0, 0, j, 0, 0)
-    )
-    return pl.pallas_call(
-        functools.partial(grads_kernel, n_levels, parts, shards, scale),
+        (shards // 2, n_levels, n_parts, 1, rows, block), lambda j, *_: (0, 0, 0, j, 0, 0)
+    )
+    outs = pl.pallas_call(
+        functools.partial(grads_kernel, n_parts, n_levels, shards, scale),
         grid_spec=pltpu.PrefetchScalarGridSpec(
             num_scalar_prefetch=1,
-            grid=(n_blocks,),
-            in_specs=[pl.BlockSpec((tok, block), lambda j, *_: (0, j))]
-            + [pl.BlockSpec(s.shape, lambda j, *_: (0, 0)) for s in sources],
+            grid=(steps,),
+            in_specs=[
+                pl.BlockSpec((tok, block), lambda j, *_, p=p: (0, p * steps + j))
+                for p in range(n_parts)
+            ]
+            + [pl.BlockSpec((tok, block), lambda j, *_: (0, j))] * (n_parts * n_levels),
             out_specs=[part_spec, part_spec],
-            scratch_shapes=[pltpu.VMEM((n_levels, block, block), F32)]
-            + [pltpu.VMEM((tok, ff), BF16)] * n_levels,
+            scratch_shapes=[pltpu.VMEM((n_parts, n_levels, block, block), F32)],
         ),
         out_shape=[part, part],
         compiler_params=params(),
         cost_estimate=COST,
-    )(pos, cot, *sources)
+    )(pos, *[cot] * n_parts, *[value for _, part in parts for value in part])
+    return [o.reshape(o.shape[:2] + (n_blocks,) + o.shape[4:]) for o in outs]
 
 
 def pair_kernel(distances, shards, scale, pos_ref, *refs):
@@ -296,10 +297,10 @@
     return pieces, [value for mask in far for _, value in far[mask]]
 
 
-def with_pair(pieces, tie):
+def with_pair(pieces, *ties):
     return pieces + [
         ([mask | 1 for mask in masks], swap(after(value, *tie), "dp", 1))
-        for masks, value in pieces
+        for (masks, value), tie in zip(pieces, ties)
     ]
 
 
@@ -325,6 +326,78 @@
     return totals, received
 
 
+def scatter_and_gather(parts, rows, tie, last_tie):
+    half = parts[0].shape[-1] // 2
+    columns = slice(0, half), slice(half, None)
+    shape = parts[0].shape[1:-1] + (half,)
+    halves = jnp.stack([rows[..., c] for c in columns])
+
+    def split(parts):
+        return [[[part[q][..., c] for part in parts] for q in range(4)] for c in columns]
+
+    terms = split(parts)
+
+    def total(values):
+        return sum(v.astype(F32) for v in values).astype(BF16)
+
+    got = []
+    for way in range(2):
+        going = jnp.concatenate([total(terms[way][q]) for q in (1 + way, 3)] + [halves])
+        got.append(swap(after(going, *tie), "dp", 2 << way))
+    levels = shape[0]
+    terms = split([after(part, *got) for part in parts])
+    far, totals = [], []
+    for way in range(2):
+        mine, ours = got[way][:levels], got[way][levels : 2 * levels]
+        passed = got[way][2 * levels :][way : way + 1]
+        going = jnp.concatenate([total(terms[way][2 - way] + [ours]), passed])
+        last = swap(after(going, *got, *last_tie), "dp", 4 >> way)
+        totals.append(sum(v.astype(F32) for v in terms[way][0] + [mine, last[:levels]]))
+        far.append(last[levels])
+    near = [jnp.concatenate([g[2 * levels], g[2 * levels + 1]], axis=-1) for g in got]
+    held = jnp.stack([rows, *near, jnp.concatenate(far, axis=-1)])[:, None]
+    return totals, [([0, 2, 4, 6], held), ([1, 3, 5, 7], swap(held, "dp", 1))]
+
+
+def low_kernel(pieces, pos_ref, *refs):
+    w_refs, (left_ref, right_ref, w_ref) = refs[: len(pieces)], refs[len(pieces) :]
+    shards, rows, block = w_ref.shape[1:]
+    rank = left_ref.shape[1]
+    for b in range(w_ref.shape[0]):
+        for (masks, _), ref in zip(pieces, w_refs):
+            for i, m in enumerate(masks):
+                w_ref[b, pos_ref[0] ^ m] = ref[i, 0, b]
+        values = w_ref[b].reshape(shards * rows, block).astype(F32)
+        there = pl.ds(b * block, block)
+        left_ref[there, :] = values[:, :rank]
+        right_ref[:, there] = values[:, rank:].T
+
+
+def low_grads(pos, pieces, shards, rank):
+    n_blocks, rows, block = pieces[0][1].shape[2:]
+    width = min(4, n_blocks)
+    ff = n_blocks * block
+    return pl.pallas_call(
+        functools.partial(low_kernel, pieces),
+        grid_spec=pltpu.PrefetchScalarGridSpec(
+            num_scalar_prefetch=1,
+            grid=(n_blocks // width,),
+            in_specs=[
+                pl.BlockSpec((p.shape[0], 1, width, rows, block), lambda j, *_: (0, 0, j, 0, 0))
+                for _, p in pieces
+            ],
+            out_specs=[
+                pl.BlockSpec((width * block, rank), lambda j, *_: (j, 0)),
+                pl.BlockSpec((rank, width * block), lambda j, *_: (0, j)),
+            ],
+            scratch_shapes=[pltpu.VMEM((width, shards, rows, block), BF16)],
+        ),
+        out_shape=[jax.ShapeDtypeStruct((ff, rank), F32), jax.ShapeDtypeStruct((rank, ff), F32)],
+        compiler_params=params(),
+        cost_estimate=COST,
+    )(pos, *[p for _, p in pieces])
+
+
 def gather_rows(value, shards):
     pos = lax.axis_index("dp")
     for bit in range(shards.bit_length() - 1)[::-1]:
@@ -357,8 +430,8 @@
     def add(value, other):
         return (value.astype(F32) + other.astype(F32)).astype(BF16)
 
-    cuts = [0, max(1, n_blocks // 4) * block, max(2, n_blocks // 2) * block, ff]
-    both = swap(jnp.stack([hidden, cotangent]), "dp", 1)
+    cuts = [ff * quarter // 4 for quarter in range(5)]
+    both = swap(after(jnp.stack([hidden, cotangent]), factors), "dp", 1)
     remote, ready = [], []
     for number, (start, stop) in enumerate(zip(cuts, cuts[1:])):
         part = after(hidden[:, start:stop], *ready, *([both] if ready else []))
@@ -387,12 +460,12 @@
         shards, scale,
     )
 
-    pieces = with_pair(pieces, [their_factors])
+    pieces = with_pair(pieces, [their_factors], remote[2][1] + [kept])
     cuts = [0, max(1, n_blocks * 7 // 16), max(2, n_blocks * 3 // 4), n_blocks]
     sent, returned, ready = [], [], remote[-1][1]
     for number, (start, stop) in enumerate(zip(cuts, cuts[1:])):
         terms = back_terms(
-            pos, after(cotangent, *(returned[0] if number > 1 else ())), pieces, n_local,
+            pos, cotangent, pieces, n_local,
             cross_bits, shards, start, stop - start,
         )
         ready = [swap(after(t, *ready), "tensor", 1 << bit) for bit, t in enumerate(terms)]
@@ -401,20 +474,22 @@
     keep, send = block_grads(pos, after(cotangent, *sent[0]), remote, n_blocks, shards, scale)
     crossed = swap(send, "dp", 1)
     grads_local, received = scatter_sum(
-        [kept], shards, gathered + remote[2][1], returned[0] + sent[1] + [keep]
+        [kept], shards, gathered + remote[3][1] + sent[0], returned[0] + sent[1] + [keep]
     )
     mixed_rows, grad_in = rows_terms(
-        pos, hidden, after(cotangent, crossed), factor, back, low_left, low_right, remote,
+        pos, hidden, after(cotangent, *returned[0], crossed), factor, back, low_left, low_right, remote,
         pieces, distances, n_blocks, shards,
     )
 
     low = jnp.concatenate([part[n_local] for part in grads_local], axis=-1).astype(BF16)
-    low = gather_rows(low, shards).reshape(ff, 2 * rank).astype(F32)
-    grad_left, grad_right = low[:, :rank], low[:, rank:].T
-
-    grads_cross, _ = scatter_sum(
-        [keep, crossed], shards, received + returned[1] + sent[2] + [mixed_rows]
-    )
+    tie = received + returned[1] + sent[2] + [mixed_rows]
+    if shards == 8:
+        grads_cross, low_pieces = scatter_and_gather([keep, crossed], low, tie, returned[2])
+        grad_left, grad_right = low_grads(pos, low_pieces, shards, rank)
+    else:
+        grads_cross, _ = scatter_sum([keep, crossed], shards, tie)
+        low = gather_rows(low, shards).reshape(ff, 2 * rank).astype(F32)
+        grad_left, grad_right = low[:, :rank], low[:, rank:].T
     grad_blocks = jnp.concatenate(
         [
             jnp.concatenate([a[:n_local], b], axis=0)

time: 250 us -> 223 us (0.89)
  local copies, waits for them, and re-layouts: 34 us -> 18.1 us
  waiting for transfers between devices: 101 us -> 95.7 us
  other arithmetic: 22.5 us -> 19.4 us
    unnamed x139 -> x48, local copies, waits for them, and re-layouts: 17.9 us -> 10.2 us
    ppermute x32, waiting for transfers between devices: 101 us -> 95.7 us  [swap(): lax.ppermute(value, axis, [(i, i ^ mask) for i in range(lax.axis_size(axi...]
    squeeze x3 -> x1, local copies, waits for them, and re-layouts: 6.33 us -> 2.11 us  [scatter_sum(): part[q][..., columns]]
    slice x2, local copies, waits for them, and re-layouts: 3.7 us -> 0.19 us  [per_device(): a[:n_local]]
    add x2 -> x1, other arithmetic: 4.77 us -> 1.75 us  [scatter_sum(): totals.append(sum((t.astype(F32) for t in terms[0])))]
    pallas_call x1 -> x2, Pallas kernels: 8.51 us -> 7.15 us  [the longest x1 4.45 us: block_grads(): pl.pallas_call(functools.partial(grads_kernel, n_parts, n_levels, shards,...]
  transfers between devices with their start and end apart: 32 -> 32, of which waited for: 13 -> 14; matrix products, arithmetic and copies ran while one was open for 14% -> 12% of each run, Pallas kernels for 20% -> 19%
where the time goes in v3:
time: 223 us; the launch traced here: 222 us
  waiting for transfers between devices  95.7 us (43%)
  Pallas kernels  49 us (22%)
  starting transfers between devices  37.7 us (17%)
  other arithmetic  19.4 us (9%)
  local copies, waits for them, and re-layouts  18.1 us (8%)
    ppermute x32, waiting for transfers between devices, swap(): lax.ppermute(value, axis, [(i, i ^ mask) for i in range(lax.axis_size(axi...  95.7 us
    ppermute x32, starting transfers between devices, swap(): lax.ppermute(value, axis, [(i, i ^ mask) for i in range(lax.axis_size(axi...  37.7 us
    pallas_call x1, Pallas kernels, rows_terms(): pl.pallas_call(functools.partial(rows_kernel, pieces, distances, parts),...  16.4 us
    pallas_call x1, Pallas kernels, pair_grads(): pl.pallas_call(functools.partial(pair_kernel, distances, shards, scale),...  13.6 us
    pallas_call x3, Pallas kernels, back_terms(): pl.pallas_call(functools.partial(back_kernel, pieces, n_levels), grid_spe...  11.9 us
    unnamed x48, local copies, waits for them, and re-layouts  10.2 us
  transfers between devices with their start and end apart: 32, of which 14 were waited for; matrix products, arithmetic and copies ran while one was open for 12% of the time, Pallas kernels for 19%

profile of v3, /device:TPU:0, one launch (start us, length us, event | category | flops | bytes accessed | tf_op | source)
XLA Modules:
  0.0 222.2 jit_solution(7215051482748675626)
XLA Ops:
  0.7 2.3 %pad_maximum_fusion.1 = bf16[2,192,4096]{2,1,0:T(8,128)(2,1)S(1)} fusion(bf16[1,192,4096]{2,1,0:T(8,128)(2,1)} %bitcast.99, bf16[1,192,4096]{2,1,0:T(8,128)(2,1)} %bitcast.100), kind=kLoop, calls=%fused_computation.2 | loop fusion | flops 1572864 | bytes 6291456 | tf_op jit(solution)/shard_map/stack | solution.py:434
  3.5 2.6 %collective-permute-start.1 = (bf16[7,16,32,256]{3,2,1,0:T(8,128)(2,1)S(1)}, bf16[7,16,32,256]{3,2,1,0:T(8,128)(2,1)S(1)}, u32[]{:S(2)}, u32[]{:S(2)}) collective-permute-start(bf16[7,16,32,256]{3,2,1,0:T(8,128)(2,1)S(1)} %copy-done.20), channel_id=1, source_target_pairs={{0,16},{4,20},{8,24},{12,28},{16,0},{20,4},{24,8},{28,12},{1,17},{... | collective-permute-start | bytes 5505032 | tf_op jit(solution)/shard_map/ppermute | solution.py:17
  6.1 1.5 collective-permute-start
  7.6 1.0 fusion.7
  10.5 1.6 collective-permute-start.2
  12.1 2.6 %collective-permute-start.3 = (bf16[192,1024]{1,0:T(8,128)(2,1)S(1)}, bf16[192,1024]{1,0:T(8,128)(2,1)S(1)}, u32[]{:S(2)}, u32[]{:S(2)}) collective-permute-start(bf16[192,1024]{1,0:T(8,128)(2,1)S(1)} %get-tuple-element.106), channel_id=1, source_target_pairs={{0,2},{1,3},{2,0},{3,1},{4,6},{5,7},{6,4},{7,5},{8,10},{9,11},{10,... | collective-permute-start | bytes 1179656 | tf_op jit(solution)/shard_map/ppermute | solution.py:17
  14.7 17.3 %collective-permute-done.2.refs_4_.refs_0_ = bf16[192,1280]{1,0:T(8,128)(2,1)S(1)} collective-permute-done((bf16[192,1280]{1,0:T(8,128)(2,1)S(1)}, bf16[192,1280]{1,0:T(8,128)(2,1)S(1)}, u32[]{:S(2)}, u32[]{:S(2)}) %collective-permute-start.2) | collective-permute-done | bytes 491552 | tf_op jit(solution)/shard_map/ppermute | solution.py:17
  32.8 1.7 copy-done.2
  34.5 1.8 collective-permute-start.6
  36.2 2.5 %collective-permute-start.5 = (bf16[192,1024]{1,0:T(8,128)(2,1)S(1)}, bf16[192,1024]{1,0:T(8,128)(2,1)S(1)}, u32[]{:S(2)}, u32[]{:S(2)}) collective-permute-start(bf16[192,1024]{1,0:T(8,128)(2,1)S(1)} %get-tuple-element.45), channel_id=1, source_target_pairs={{0,1},{1,0},{2,3},{3,2},{4,5},{5,4},{6,7},{7,6},{8,9},{9,8},{10,11... | collective-permute-start | bytes 1179656 | tf_op jit(solution)/shard_map/ppermute | solution.py:17
  38.7 19.4 %collective-permute-done.6.refs_7_.refs_3_ = bf16[192,1280]{1,0:T(8,128)(2,1)S(1)} collective-permute-done((bf16[192,1280]{1,0:T(8,128)(2,1)S(1)}, bf16[192,1280]{1,0:T(8,128)(2,1)S(1)}, u32[]{:S(2)}, u32[]{:S(2)}) %collective-permute-start.6) | collective-permute-done | bytes 491552 | tf_op jit(solution)/shard_map/ppermute | solution.py:17
  60.3 3.0 %pad_maximum_fusion.refs_0_.refs_8_ = bf16[3,7,16,32,256]{4,3,2,1,0:T(8,128)(2,1)} fusion(bf16[1,7,16,32,256]{4,3,2,1,0:T(8,128)(2,1)S(1)} %bitcast.103, bf16[1,7,16,32,256]{4,3,2,1,0:T(8,128)(2,1)S(1)} %bitcast.104, bf16[1,7,16,32,256]{4,3,2,1,0:T(8,128)(2,1)S(1)} %bitcast.106), kind=kLoop, calls=%fused_computation | loop fusion | flops 5505024 | bytes 11010048 | tf_op jit(solution)/shard_map/stack | solution.py:293
  63.9 1.1 slice.301
  65.0 1.1 slice.299
  67.3 3.0 %collective-permute-start.12 = (bf16[192,1024]{1,0:T(8,128)(2,1)}, bf16[192,1024]{1,0:T(8,128)(2,1)}, u32[]{:S(2)}, u32[]{:S(2)}) collective-permute-start(bf16[192,1024]{1,0:T(8,128)(2,1)} %get-tuple-element.50), channel_id=1, source_target_pairs={{0,2},{1,3},{2,0},{3,1},{4,6},{5,7},{6,4},{7,5},{8,10},{9,11},{10,... | collective-permute-start | bytes 1179656 | tf_op jit(solution)/shard_map/ppermute | solution.py:17
  70.3 1.9 copy-done.3
  72.2 0.9 copy-done.15
  74.0 13.6 %shard_map.92 = bf16[4,6,16,32,256]{4,3,2,1,0:T(8,128)(2,1)S(1)} custom-call(s32[1]{0:T(128)} %bitcast.pos_ref, bf16[192,4096]{1,0:T(8,128)(2,1)S(1)} %copy-done.1, bf16[192,4096]{1,0:T(8,128)(2,1)S(1)} %copy-done, bf16[192,256]{1,0:T(8,128)(2,1)S(1)} %copy-done.15, bf16[2,192,4096]{2,1,0:T(8,128)(2,1)S(1)} %copy-done.3, ...), custom_call_target="tpu_custom_call" | custom-call | flops 1 | bytes 1 | tf_op jit(solution)/shard_map/pallas_call | solution.py:132
  87.6 1.1 collective-permute-done.8
  88.9 1.8 maximum_bitcast_fusion.refs_1_.refs_9_
  90.8 2.1 slice_bitcast_fusion.2
  93.1 3.2 %collective-permute-start.15 = (bf16[192,1024]{1,0:T(8,128)(2,1)S(1)}, bf16[192,1024]{1,0:T(8,128)(2,1)S(1)}, u32[]{:S(2)}, u32[]{:S(2)}) collective-permute-start(bf16[192,1024]{1,0:T(8,128)(2,1)S(1)} %copy-done.23), channel_id=1, source_target_pairs={{0,2},{1,3},{2,0},{3,1},{4,6},{5,7},{6,4},{7,5},{8,10},{9,11},{10,... | collective-permute-start | bytes 1179656 | tf_op jit(solution)/shard_map/ppermute | solution.py:17
  96.9 5.1 %shard_map.93 = (bf16[192,1792]{1,0:T(8,128)(2,1)S(1)}, bf16[192,1792]{1,0:T(8,128)(2,1)S(1)}) custom-call(s32[1]{0:T(128)} %bitcast.pos_ref, bf16[192,4096]{1,0:T(8,128)(2,1)S(1)} %copy-done, bf16[3,7,16,32,256]{4,3,2,1,0:T(8,128)(2,1)} %pad_maximum_fusion.refs_0_.refs_8_, bf16[1,7,16,32,256]{4,3,2,1,0:T(8,128)(2,1)S(1)} %maximum_bitcast_fusion.refs_1_.refs_9_, ...), custom_call_target="tpu_custom_call" | custom-call | flops 1 | bytes 1 | tf_op jit(solution)/shard_map/pallas_call | solution.py:254
  102.0 10.8 %collective-permute-done.14.refs_10_.refs_6_ = bf16[192,1024]{1,0:T(8,128)(2,1)S(1)} collective-permute-done((bf16[192,1024]{1,0:T(8,128)(2,1)S(1)}, bf16[192,1024]{1,0:T(8,128)(2,1)S(1)}, u32[]{:S(2)}, u32[]{:S(2)}) %collective-permute-start.14) | collective-permute-done | bytes 393248 | tf_op jit(solution)/shard_map/ppermute | solution.py:17
  112.8 1.4 collective-permute-done.15.refs_11_.refs_7_
  114.3 4.5 %shard_map.94 = (bf16[4,2,4,4,32,256]{5,4,3,2,1,0:T(8,128)(2,1)S(1)}, bf16[4,2,4,4,32,256]{5,4,3,2,1,0:T(8,128)(2,1)S(1)}) custom-call(s32[1]{0:T(128)} %bitcast.pos_ref, bf16[192,4096]{1,0:T(8,128)(2,1)S(1)} %copy-done, bf16[192,4096]{1,0:T(8,128)(2,1)S(1)} %copy-done, bf16[192,4096]{1,0:T(8,128)(2,1)S(1)} %copy-done, bf16[192,4096]{1,0:T(8,128)(2,1)S(1)} %copy-done, ...), custom_call_target="tpu_custom_call" | custom-call | flops 1 | bytes 1 | tf_op jit(solution)/shard_map/pallas_call | solution.py:76
  118.8 1.3 pad_maximum_fusion.2
  120.2 1.6 collective-permute-start.23
  122.6 2.7 %collective-permute-start.17 = (bf16[192,1792]{1,0:T(8,128)(2,1)S(1)}, bf16[192,1792]{1,0:T(8,128)(2,1)}, u32[]{:S(2)}, u32[]{:S(2)}) collective-permute-start(bf16[192,1792]{1,0:T(8,128)(2,1)S(1)} %get-tuple-element.56), channel_id=1, source_target_pairs={{0,2},{1,3},{2,0},{3,1},{4,6},{5,7},{6,4},{7,5},{8,10},{9,11},{10,... | collective-permute-start | bytes 2064392 | tf_op jit(solution)/shard_map/ppermute | solution.py:17
  125.3 2.9 %shard_map.97 = (bf16[192,1024]{1,0:T(8,128)(2,1)S(1)}, bf16[192,1024]{1,0:T(8,128)(2,1)S(1)}) custom-call(s32[1]{0:T(128)} %bitcast.pos_ref, bf16[192,4096]{1,0:T(8,128)(2,1)S(1)} %copy-done, bf16[3,7,16,32,256]{4,3,2,1,0:T(8,128)(2,1)} %pad_maximum_fusion.refs_0_.refs_8_, bf16[1,7,16,32,256]{4,3,2,1,0:T(8,128)(2,1)S(1)} %maximum_bitcast_fusion.refs_1_.refs_9_, ...), custom_call_target="tpu_custom_call" | custom-call | flops 1 | bytes 1 | tf_op jit(solution)/shard_map/pallas_call | solution.py:254
  128.2 3.8 %shard_map.96 = (bf16[192,1280]{1,0:T(8,128)(2,1)S(1)}, bf16[192,1280]{1,0:T(8,128)(2,1)S(1)}) custom-call(s32[1]{0:T(128)} %bitcast.pos_ref, bf16[192,4096]{1,0:T(8,128)(2,1)S(1)} %copy-done, bf16[3,7,16,32,256]{4,3,2,1,0:T(8,128)(2,1)} %pad_maximum_fusion.refs_0_.refs_8_, bf16[1,7,16,32,256]{4,3,2,1,0:T(8,128)(2,1)S(1)} %maximum_bitcast_fusion.refs_1_.refs_9_, ...), custom_call_target="tpu_custom_call" | custom-call | flops 1 | bytes 1 | tf_op jit(solution)/shard_map/pallas_call | solution.py:254
  132.1 1.2 fusion.6
  133.2 21.0 %collective-permute-done.16 = bf16[192,1792]{1,0:T(8,128)(2,1)} collective-permute-done((bf16[192,1792]{1,0:T(8,128)(2,1)S(1)}, bf16[192,1792]{1,0:T(8,128)(2,1)}, u32[]{:S(2)}, u32[]{:S(2)}) %collective-permute-start.16) | collective-permute-done | bytes 688160 | tf_op jit(solution)/shard_map/ppermute | solution.py:17
  154.2 1.3 collective-permute-done.17
  155.8 2.6 %collective-permute-start.20 = (bf16[192,1280]{1,0:T(8,128)(2,1)S(1)}, bf16[192,1280]{1,0:T(8,128)(2,1)}, u32[]{:S(2)}, u32[]{:S(2)}) collective-permute-start(bf16[192,1280]{1,0:T(8,128)(2,1)S(1)} %get-tuple-element.66), channel_id=1, source_target_pairs={{0,2},{1,3},{2,0},{3,1},{4,6},{5,7},{6,4},{7,5},{8,10},{9,11},{10,... | collective-permute-start | bytes 1474568 | tf_op jit(solution)/shard_map/ppermute | solution.py:17
  158.4 2.7 %fusion.4 = (bf16[1,6,16,32,128]{4,3,2,1,0:T(8,128)(2,1)}, bf16[1,6,16,32,128]{4,3,2,1,0:T(8,128)(2,1)}) fusion(bf16[2,6,16,32,128]{4,3,2,1,0:T(8,128)(2,1)S(1)} %collective-permute-done.23, bf16[6,16,32,256]{3,2,1,0:T(8,128)(2,1)S(1)} %get-tuple-element.84, bf16[2,6,16,32,128]{4,3,2,1,0:T(8,128)(2,1)} %collective-permute-done.25, ...), kind=kLoop, calls=%fused_computation.26 | loop fusion | flops 3145728 | bytes 4718592 | tf_op jit(solution)/shard_map/stack | solution.py:317
  161.1 1.5 collective-permute-start.24
  163.2 16.4 %shard_map.95 = (bf16[192,4096]{1,0:T(8,128)(2,1)}, f32[192,4096]{1,0:T(8,128)S(1)}) custom-call(s32[1]{0:T(128)} %bitcast.pos_ref, bf16[192,4096]{1,0:T(8,128)(2,1)S(1)} %copy-done.1, bf16[192,4096]{1,0:T(8,128)(2,1)S(1)} %copy-done, bf16[192,128]{1,0:T(8,128)(2,1)S(1)} %get-tuple-element.120.fac_ref, bf16[192,128]{1,0:T(8,128)(2,1)S(1)} %get-tuple-element.119.back_ref, ...), custom_call_target="tpu_custom_call" | custom-call | flops 1 | bytes 1 | tf_op jit(solution)/shard_map/pallas_call | solution.py:217
  181.3 1.7 fusion.3
  183.4 1.5 collective-permute-start.27
  185.8 2.7 %collective-permute-start.22 = (bf16[192,1024]{1,0:T(8,128)(2,1)S(1)}, bf16[192,1024]{1,0:T(8,128)(2,1)S(1)}, u32[]{:S(2)}, u32[]{:S(2)}) collective-permute-start(bf16[192,1024]{1,0:T(8,128)(2,1)S(1)} %get-tuple-element.69), channel_id=1, source_target_pairs={{0,2},{1,3},{2,0},{3,1},{4,6},{5,7},{6,4},{7,5},{8,10},{9,11},{10,... | collective-permute-start | bytes 1179656 | tf_op jit(solution)/shard_map/ppermute | solution.py:17
  188.5 12.5 %collective-permute-done.27 = bf16[6,16,32,128]{3,2,1,0:T(8,128)(2,1)S(1)} collective-permute-done((bf16[6,16,32,128]{3,2,1,0:T(8,128)(2,1)S(1)}, bf16[6,16,32,128]{3,2,1,0:T(8,128)(2,1)S(1)}, u32[]{:S(2)}, u32[]{:S(2)}) %collective-permute-start.27) | collective-permute-done | bytes 786464 | tf_op jit(solution)/shard_map/ppermute | solution.py:17
  201.0 1.1 collective-permute-done.28
  203.1 1.3 collective-permute-done.22
  205.9 7.1 %collective-permute-done.30 = bf16[3,16,32,128]{3,2,1,0:T(8,128)(2,1)S(1)} collective-permute-done((bf16[3,16,32,128]{3,2,1,0:T(8,128)(2,1)S(1)}, bf16[3,16,32,128]{3,2,1,0:T(8,128)(2,1)S(1)}, u32[]{:S(2)}, u32[]{:S(2)}) %collective-permute-start.30) | collective-permute-done | bytes 393248 | tf_op jit(solution)/shard_map/ppermute | solution.py:17
  214.0 2.8 %add_convert_fusion = bf16[192,4096]{1,0:T(8,128)(2,1)} fusion(f32[192,4096]{1,0:T(8,128)S(1)} %get-tuple-element.61, bf16[192,1024]{1,0:T(8,128)(2,1)S(1)} %collective-permute-done.21, bf16[192,1280]{1,0:T(8,128)(2,1)} %collective-permute-done.19, bf16[192,1792]{1,0:T(8,128)(2,1)} %collective-permute-done.16, ...), kind=kLoop, calls=%fused_computation.3 | loop fusion | flops 11796480 | bytes 7864320 | tf_op jit(solution)/shard_map/convert_element_type | solution.py:502
  217.3 2.2 %maximum_maximum_fusion = f32[7,16,32,256]{3,2,1,0:T(8,128)} fusion(f32[2,16,32,128]{3,2,1,0:T(8,128)S(1)} %get-tuple-element.108, f32[5,16,32,128]{3,2,1,0:T(8,128)S(1)} %slice.343, f32[2,16,32,128]{3,2,1,0:T(8,128)S(1)} %get-tuple-element.107, f32[5,16,32,128]{3,2,1,0:T(8,128)S(1)} %slice.315), kind=kLoop, calls=%fused_computation.1 | loop fusion | flops 2752512 | bytes 7340032 | tf_op jit(solution)/shard_map/concatenate | solution.py:493
  219.5 2.7 %shard_map.98 = (f32[4096,128]{1,0:T(8,128)}, f32[128,4096]{1,0:T(8,128)}) custom-call(s32[1]{0:T(128)} %bitcast.pos_ref, bf16[4,1,16,32,256]{4,3,2,1,0:T(8,128)(2,1)S(1)} %maximum_bitcast_fusion.1.refs_0_, bf16[4,1,16,32,256]{4,3,2,1,0:T(8,128)(2,1)S(1)} %collective-permute-done.31.refs_1_), custom_call_target="tpu_custom_call" | custom-call | flops 1 | bytes 1 | tf_op jit(solution)/shard_map/pallas_call | solution.py:380
  (118 shorter events, 17.8 us)
Async XLA Ops:
  0.6 2.9 %copy-start.20 = (bf16[7,16,32,256]{3,2,1,0:T(8,128)(2,1)S(1)}, bf16[7,16,32,256]{3,2,1,0:T(8,128)(2,1)}, u32[]{:S(2)}) copy-start(bf16[7,16,32,256]{3,2,1,0:T(8,128)(2,1)} %param.7) | copy-start | bytes 5505028
  0.6 7.0 %copy-start.1 = (bf16[192,4096]{1,0:T(8,128)(2,1)S(1)}, bf16[192,4096]{1,0:T(8,128)(2,1)}, u32[]{:S(2)}) copy-start(bf16[192,4096]{1,0:T(8,128)(2,1)} %hid_ref.1) | copy-start | bytes 4718596
  3.0 5.7 %copy-start = (bf16[192,4096]{1,0:T(8,128)(2,1)S(1)}, bf16[192,4096]{1,0:T(8,128)(2,1)}, u32[]{:S(2)}) copy-start(bf16[192,4096]{1,0:T(8,128)(2,1)} %cot_ref.6) | copy-start | bytes 4718596
  3.0 5.7 %copy-start.4 = (bf16[128,4096]{1,0:T(8,128)(2,1)S(1)}, bf16[128,4096]{1,0:T(8,128)(2,1)}, u32[]{:S(2)}) copy-start(bf16[128,4096]{1,0:T(8,128)(2,1)} %right_ref.1) | copy-start | bytes 3145732
  3.0 29.8 %collective-permute-start.4 = (bf16[2,192,4096]{2,1,0:T(8,128)(2,1)S(1)}, bf16[2,192,4096]{2,1,0:T(8,128)(2,1)S(1)}, u32[]{:S(2)}, u32[]{:S(2)}) collective-permute-start(bf16[2,192,4096]{2,1,0:T(8,128)(2,1)S(1)} %pad_maximum_fusion.1), channel_id=1, source_target_pairs={{0,4},{4,0},{8,12},{12,8},{16,20},{20,16},{24,28},{28,24},{1,5},{5... | collective-permute-start | bytes 9437192 | tf_op jit(solution)/shard_map/ppermute | solution.py:17
  3.5 55.4 %collective-permute-start.1 = (bf16[7,16,32,256]{3,2,1,0:T(8,128)(2,1)S(1)}, bf16[7,16,32,256]{3,2,1,0:T(8,128)(2,1)S(1)}, u32[]{:S(2)}, u32[]{:S(2)}) collective-permute-start(bf16[7,16,32,256]{3,2,1,0:T(8,128)(2,1)S(1)} %copy-done.20), channel_id=1, source_target_pairs={{0,16},{4,20},{8,24},{12,28},{16,0},{20,4},{24,8},{28,12},{1,17},{... | collective-permute-start | bytes 5505032 | tf_op jit(solution)/shard_map/ppermute | solution.py:17
  6.1 52.8 %collective-permute-start = (bf16[7,16,32,256]{3,2,1,0:T(8,128)(2,1)S(1)}, bf16[7,16,32,256]{3,2,1,0:T(8,128)(2,1)S(1)}, u32[]{:S(2)}, u32[]{:S(2)}) collective-permute-start(bf16[7,16,32,256]{3,2,1,0:T(8,128)(2,1)S(1)} %copy-done.20), channel_id=1, source_target_pairs={{0,8},{4,12},{8,0},{12,4},{16,24},{20,28},{24,16},{28,20},{1,9},{5... | collective-permute-start | bytes 5505032 | tf_op jit(solution)/shard_map/ppermute | solution.py:17
  8.6 1.2 copy-start.6
  10.5 21.5 %collective-permute-start.2 = (bf16[192,1280]{1,0:T(8,128)(2,1)S(1)}, bf16[192,1280]{1,0:T(8,128)(2,1)S(1)}, u32[]{:S(2)}, u32[]{:S(2)}) collective-permute-start(bf16[192,1280]{1,0:T(8,128)(2,1)S(1)} %pad_maximum_fusion.8), channel_id=1, source_target_pairs={{0,1},{1,0},{2,3},{3,2},{4,5},{5,4},{6,7},{7,6},{8,9},{9,8},{10,11... | collective-permute-start | bytes 1474568 | tf_op jit(solution)/shard_map/ppermute | solution.py:17
  12.1 20.7 %collective-permute-start.3 = (bf16[192,1024]{1,0:T(8,128)(2,1)S(1)}, bf16[192,1024]{1,0:T(8,128)(2,1)S(1)}, u32[]{:S(2)}, u32[]{:S(2)}) collective-permute-start(bf16[192,1024]{1,0:T(8,128)(2,1)S(1)} %get-tuple-element.106), channel_id=1, source_target_pairs={{0,2},{1,3},{2,0},{3,1},{4,6},{5,7},{6,4},{7,5},{8,10},{9,11},{10,... | collective-permute-start | bytes 1179656 | tf_op jit(solution)/shard_map/ppermute | solution.py:17
  32.8 1.7 copy-start.2
  34.5 23.6 %collective-permute-start.6 = (bf16[192,1280]{1,0:T(8,128)(2,1)S(1)}, bf16[192,1280]{1,0:T(8,128)(2,1)S(1)}, u32[]{:S(2)}, u32[]{:S(2)}) collective-permute-start(bf16[192,1280]{1,0:T(8,128)(2,1)S(1)} %pad_maximum_fusion.9), channel_id=1, source_target_pairs={{0,2},{1,3},{2,0},{3,1},{4,6},{5,7},{6,4},{7,5},{8,10},{9,11},{10,... | collective-permute-start | bytes 1474568 | tf_op jit(solution)/shard_map/ppermute | solution.py:17
  36.2 22.7 %collective-permute-start.5 = (bf16[192,1024]{1,0:T(8,128)(2,1)S(1)}, bf16[192,1024]{1,0:T(8,128)(2,1)S(1)}, u32[]{:S(2)}, u32[]{:S(2)}) collective-permute-start(bf16[192,1024]{1,0:T(8,128)(2,1)S(1)} %get-tuple-element.45), channel_id=1, source_target_pairs={{0,1},{1,0},{2,3},{3,2},{4,5},{5,4},{6,7},{7,6},{8,9},{9,8},{10,11... | collective-permute-start | bytes 1179656 | tf_op jit(solution)/shard_map/ppermute | solution.py:17
  59.7 3.6 %collective-permute-start.9 = (bf16[192,256]{1,0:T(8,128)(2,1)S(1)}, bf16[192,256]{1,0:T(8,128)(2,1)S(1)}, u32[]{:S(2)}, u32[]{:S(2)}) collective-permute-start(bf16[192,256]{1,0:T(8,128)(2,1)S(1)} %add_convert_fusion.7.refs_2_), channel_id=1, source_target_pairs={{0,4},{4,0},{8,12},{12,8},{16,20},{20,16},{24,28},{28,24},{1,5},{5... | collective-permute-start | bytes 294920 | tf_op jit(solution)/shard_map/ppermute | solution.py:17
  63.3 2.7 %copy-start.17 = (bf16[192,256]{1,0:T(8,128)(2,1)}, bf16[192,256]{1,0:T(8,128)(2,1)S(1)}, u32[]{:S(2)}) copy-start(bf16[192,256]{1,0:T(8,128)(2,1)S(1)} %collective-permute-done.9.refs_5_) | copy-start | bytes 294916
  63.3 33.5 %collective-permute-start.10 = (bf16[3,7,16,32,256]{4,3,2,1,0:T(8,128)(2,1)}, bf16[3,7,16,32,256]{4,3,2,1,0:T(8,128)(2,1)}, u32[]{:S(2)}, u32[]{:S(2)}) collective-permute-start(bf16[3,7,16,32,256]{4,3,2,1,0:T(8,128)(2,1)} %pad_maximum_fusion.refs_0_.refs_8_), channel_id=1, source_target_pairs={{0,4},{4,0},{8,12},{12,8},{16,20},{20,16},{24,28},{28,24},{1,5},{5... | collective-permute-start | bytes 16515080 | tf_op jit(solution)/shard_map/ppermute | solution.py:17
  66.1 22.6 %collective-permute-start.8 = (bf16[7,16,32,128]{3,2,1,0:T(8,128)(2,1)}, bf16[7,16,32,128]{3,2,1,0:T(8,128)(2,1)}, u32[]{:S(2)}, u32[]{:S(2)}) collective-permute-start(bf16[7,16,32,128]{3,2,1,0:T(8,128)(2,1)} %slice.301), channel_id=1, source_target_pairs={{0,8},{4,12},{8,0},{12,4},{16,24},{20,28},{24,16},{28,20},{1,9},{5... | collective-permute-start | bytes 2752520 | tf_op jit(solution)/shard_map/ppermute | solution.py:17
  66.6 22.3 %collective-permute-start.7 = (bf16[7,16,32,128]{3,2,1,0:T(8,128)(2,1)}, bf16[7,16,32,128]{3,2,1,0:T(8,128)(2,1)}, u32[]{:S(2)}, u32[]{:S(2)}) collective-permute-start(bf16[7,16,32,128]{3,2,1,0:T(8,128)(2,1)} %slice.299), channel_id=1, source_target_pairs={{0,16},{4,20},{8,24},{12,28},{16,0},{20,4},{24,8},{28,12},{1,17},{... | collective-permute-start | bytes 2752520 | tf_op jit(solution)/shard_map/ppermute | solution.py:17
  67.3 23.4 %collective-permute-start.11 = (bf16[192,1024]{1,0:T(8,128)(2,1)}, bf16[192,1024]{1,0:T(8,128)(2,1)}, u32[]{:S(2)}, u32[]{:S(2)}) collective-permute-start(bf16[192,1024]{1,0:T(8,128)(2,1)} %get-tuple-element.50), channel_id=1, source_target_pairs={{0,1},{1,0},{2,3},{3,2},{4,5},{5,4},{6,7},{7,6},{8,9},{9,8},{10,11... | collective-permute-start | bytes 1179656 | tf_op jit(solution)/shard_map/ppermute | solution.py:17
  67.3 23.4 %collective-permute-start.12 = (bf16[192,1024]{1,0:T(8,128)(2,1)}, bf16[192,1024]{1,0:T(8,128)(2,1)}, u32[]{:S(2)}, u32[]{:S(2)}) collective-permute-start(bf16[192,1024]{1,0:T(8,128)(2,1)} %get-tuple-element.50), channel_id=1, source_target_pairs={{0,2},{1,3},{2,0},{3,1},{4,6},{5,7},{6,4},{7,5},{8,10},{9,11},{10,... | collective-permute-start | bytes 1179656 | tf_op jit(solution)/shard_map/ppermute | solution.py:17
  70.3 1.9 copy-start.3
  90.7 2.4 %copy-start.23 = (bf16[192,1024]{1,0:T(8,128)(2,1)S(1)}, bf16[192,1024]{1,0:T(8,128)(2,1)}, u32[]{:S(2)}) copy-start(bf16[192,1024]{1,0:T(8,128)(2,1)} %get-tuple-element.53) | copy-start | bytes 1179652
  90.7 6.2 %collective-permute-start.13 = (bf16[1,7,16,32,256]{4,3,2,1,0:T(8,128)(2,1)S(1)}, bf16[1,7,16,32,256]{4,3,2,1,0:T(8,128)(2,1)S(1)}, u32[]{:S(2)}, u32[]{:S(2)}) collective-permute-start(bf16[1,7,16,32,256]{4,3,2,1,0:T(8,128)(2,1)S(1)} %maximum_bitcast_fusion.refs_1_.refs_9_), channel_id=1, source_target_pairs={{0,4},{4,0},{8,12},{12,8},{16,20},{20,16},{24,28},{28,24},{1,5},{5... | collective-permute-start | bytes 5505032 | tf_op jit(solution)/shard_map/ppermute | solution.py:17
  93.1 19.8 %collective-permute-start.14 = (bf16[192,1024]{1,0:T(8,128)(2,1)S(1)}, bf16[192,1024]{1,0:T(8,128)(2,1)S(1)}, u32[]{:S(2)}, u32[]{:S(2)}) collective-permute-start(bf16[192,1024]{1,0:T(8,128)(2,1)S(1)} %copy-done.23), channel_id=1, source_target_pairs={{0,1},{1,0},{2,3},{3,2},{4,5},{5,4},{6,7},{7,6},{8,9},{9,8},{10,11... | collective-permute-start | bytes 1179656 | tf_op jit(solution)/shard_map/ppermute | solution.py:17
  93.1 21.1 %collective-permute-start.15 = (bf16[192,1024]{1,0:T(8,128)(2,1)S(1)}, bf16[192,1024]{1,0:T(8,128)(2,1)S(1)}, u32[]{:S(2)}, u32[]{:S(2)}) collective-permute-start(bf16[192,1024]{1,0:T(8,128)(2,1)S(1)} %copy-done.23), channel_id=1, source_target_pairs={{0,2},{1,3},{2,0},{3,1},{4,6},{5,7},{6,4},{7,5},{8,10},{9,11},{10,... | collective-permute-start | bytes 1179656 | tf_op jit(solution)/shard_map/ppermute | solution.py:17
  96.8 17.4 %copy-start.9 = (bf16[192,1280]{1,0:T(8,128)(2,1)S(1)}, bf16[192,1280]{1,0:T(8,128)(2,1)}, u32[]{:S(2)}) copy-start(bf16[192,1280]{1,0:T(8,128)(2,1)} %copy-done.8) | copy-start | bytes 1474564
  96.8 17.4 %copy-start.11 = (bf16[192,1280]{1,0:T(8,128)(2,1)S(1)}, bf16[192,1280]{1,0:T(8,128)(2,1)}, u32[]{:S(2)}) copy-start(bf16[192,1280]{1,0:T(8,128)(2,1)} %copy-done.10) | copy-start | bytes 1474564
  96.8 17.4 %copy-start.13 = (bf16[192,1024]{1,0:T(8,128)(2,1)S(1)}, bf16[192,1024]{1,0:T(8,128)(2,1)}, u32[]{:S(2)}) copy-start(bf16[192,1024]{1,0:T(8,128)(2,1)} %copy-done.12) | copy-start | bytes 1179652
  118.7 44.4 %collective-permute-start.18 = (bf16[4,2,16,32,256]{4,3,2,1,0:T(8,128)(2,1)S(1)}, bf16[4,2,16,32,256]{4,3,2,1,0:T(8,128)(2,1)S(1)}, u32[]{:S(2)}, u32[]{:S(2)}) collective-permute-start(bf16[4,2,16,32,256]{4,3,2,1,0:T(8,128)(2,1)S(1)} %bitcast.102), channel_id=1, source_target_pairs={{0,4},{4,0},{8,12},{12,8},{16,20},{20,16},{24,28},{28,24},{1,5},{5... | collective-permute-start | bytes 6291464 | tf_op jit(solution)/shard_map/ppermute | solution.py:17
  120.1 5.2 %copy-start.16 = (bf16[192,256]{1,0:T(8,128)(2,1)S(1)}, bf16[192,256]{1,0:T(8,128)(2,1)}, u32[]{:S(2)}) copy-start(bf16[192,256]{1,0:T(8,128)(2,1)} %copy-done.14) | copy-start | bytes 294916
  120.2 38.2 %collective-permute-start.23 = (bf16[2,6,16,32,128]{4,3,2,1,0:T(8,128)(2,1)}, bf16[2,6,16,32,128]{4,3,2,1,0:T(8,128)(2,1)S(1)}, u32[]{:S(2)}, u32[]{:S(2)}) collective-permute-start(bf16[2,6,16,32,128]{4,3,2,1,0:T(8,128)(2,1)} %pad_maximum_fusion.2), channel_id=1, source_target_pairs={{0,8},{4,12},{8,0},{12,4},{16,24},{20,28},{24,16},{28,20},{1,9},{5... | collective-permute-start | bytes 4718600 | tf_op jit(solution)/shard_map/ppermute | solution.py:17
  121.8 36.6 %collective-permute-start.25 = (bf16[2,6,16,32,128]{4,3,2,1,0:T(8,128)(2,1)S(1)}, bf16[2,6,16,32,128]{4,3,2,1,0:T(8,128)(2,1)}, u32[]{:S(2)}, u32[]{:S(2)}) collective-permute-start(bf16[2,6,16,32,128]{4,3,2,1,0:T(8,128)(2,1)S(1)} %pad_maximum_fusion.3), channel_id=1, source_target_pairs={{0,16},{4,20},{8,24},{12,28},{16,0},{20,4},{24,8},{28,12},{1,17},{... | collective-permute-start | bytes 4718600 | tf_op jit(solution)/shard_map/ppermute | solution.py:17
  122.3 31.9 %collective-permute-start.16 = (bf16[192,1792]{1,0:T(8,128)(2,1)S(1)}, bf16[192,1792]{1,0:T(8,128)(2,1)}, u32[]{:S(2)}, u32[]{:S(2)}) collective-permute-start(bf16[192,1792]{1,0:T(8,128)(2,1)S(1)} %get-tuple-element.54), channel_id=1, source_target_pairs={{0,1},{1,0},{2,3},{3,2},{4,5},{5,4},{6,7},{7,6},{8,9},{9,8},{10,11... | collective-permute-start | bytes 2064392 | tf_op jit(solution)/shard_map/ppermute | solution.py:17
  122.6 32.8 %collective-permute-start.17 = (bf16[192,1792]{1,0:T(8,128)(2,1)S(1)}, bf16[192,1792]{1,0:T(8,128)(2,1)}, u32[]{:S(2)}, u32[]{:S(2)}) collective-permute-start(bf16[192,1792]{1,0:T(8,128)(2,1)S(1)} %get-tuple-element.56), channel_id=1, source_target_pairs={{0,2},{1,3},{2,0},{3,1},{4,6},{5,7},{6,4},{7,5},{8,10},{9,11},{10,... | collective-permute-start | bytes 2064392 | tf_op jit(solution)/shard_map/ppermute | solution.py:17
  155.5 27.9 %collective-permute-start.19 = (bf16[192,1280]{1,0:T(8,128)(2,1)S(1)}, bf16[192,1280]{1,0:T(8,128)(2,1)}, u32[]{:S(2)}, u32[]{:S(2)}) collective-permute-start(bf16[192,1280]{1,0:T(8,128)(2,1)S(1)} %get-tuple-element.63), channel_id=1, source_target_pairs={{0,1},{1,0},{2,3},{3,2},{4,5},{5,4},{6,7},{7,6},{8,9},{9,8},{10,11... | collective-permute-start | bytes 1474568 | tf_op jit(solution)/shard_map/ppermute | solution.py:17
  155.8 7.4 %copy-start.5 = (bf16[128,4096]{1,0:T(8,128)(2,1)S(1)}, bf16[128,4096]{1,0:T(8,128)(2,1)}, u32[]{:S(2)}) copy-start(bf16[128,4096]{1,0:T(8,128)(2,1)} %right_ref.1) | copy-start | bytes 3145732
  155.8 7.4 %copy-start.7 = (bf16[4096,128]{1,0:T(8,128)(2,1)S(1)}, bf16[4096,128]{1,0:T(8,128)(2,1)}, u32[]{:S(2)}) copy-start(bf16[4096,128]{1,0:T(8,128)(2,1)} %left_ref.1) | copy-start | bytes 3145732
  155.8 27.6 %collective-permute-start.20 = (bf16[192,1280]{1,0:T(8,128)(2,1)S(1)}, bf16[192,1280]{1,0:T(8,128)(2,1)}, u32[]{:S(2)}, u32[]{:S(2)}) collective-permute-start(bf16[192,1280]{1,0:T(8,128)(2,1)S(1)} %get-tuple-element.66), channel_id=1, source_target_pairs={{0,2},{1,3},{2,0},{3,1},{4,6},{5,7},{6,4},{7,5},{8,10},{9,11},{10,... | collective-permute-start | bytes 1474568 | tf_op jit(solution)/shard_map/ppermute | solution.py:17
  161.1 19.8 %collective-permute-start.24 = (bf16[1,6,16,32,128]{4,3,2,1,0:T(8,128)(2,1)}, bf16[1,6,16,32,128]{4,3,2,1,0:T(8,128)(2,1)S(1)}, u32[]{:S(2)}, u32[]{:S(2)}) collective-permute-start(bf16[1,6,16,32,128]{4,3,2,1,0:T(8,128)(2,1)} %get-tuple-element.72), channel_id=1, source_target_pairs={{0,16},{4,20},{8,24},{12,28},{16,0},{20,4},{24,8},{28,12},{1,17},{... | collective-permute-start | bytes 2359304 | tf_op jit(solution)/shard_map/ppermute | solution.py:17
  162.6 18.3 %collective-permute-start.26 = (bf16[1,6,16,32,128]{4,3,2,1,0:T(8,128)(2,1)}, bf16[1,6,16,32,128]{4,3,2,1,0:T(8,128)(2,1)S(1)}, u32[]{:S(2)}, u32[]{:S(2)}) collective-permute-start(bf16[1,6,16,32,128]{4,3,2,1,0:T(8,128)(2,1)} %get-tuple-element.74), channel_id=1, source_target_pairs={{0,8},{4,12},{8,0},{12,4},{16,24},{20,28},{24,16},{28,20},{1,9},{5... | collective-permute-start | bytes 2359304 | tf_op jit(solution)/shard_map/ppermute | solution.py:17
  179.7 1.6 copy-start.19
  183.4 17.6 %collective-permute-start.27 = (bf16[6,16,32,128]{3,2,1,0:T(8,128)(2,1)S(1)}, bf16[6,16,32,128]{3,2,1,0:T(8,128)(2,1)S(1)}, u32[]{:S(2)}, u32[]{:S(2)}) collective-permute-start(bf16[6,16,32,128]{3,2,1,0:T(8,128)(2,1)S(1)} %get-tuple-element.75), channel_id=1, source_target_pairs={{0,8},{4,12},{8,0},{12,4},{16,24},{20,28},{24,16},{28,20},{1,9},{5... | collective-permute-start | bytes 2359304 | tf_op jit(solution)/shard_map/ppermute | solution.py:17
  185.0 17.2 %collective-permute-start.28 = (bf16[6,16,32,128]{3,2,1,0:T(8,128)(2,1)S(1)}, bf16[6,16,32,128]{3,2,1,0:T(8,128)(2,1)S(1)}, u32[]{:S(2)}, u32[]{:S(2)}) collective-permute-start(bf16[6,16,32,128]{3,2,1,0:T(8,128)(2,1)S(1)} %get-tuple-element.76), channel_id=1, source_target_pairs={{0,16},{4,20},{8,24},{12,28},{16,0},{20,4},{24,8},{28,12},{1,17},{... | collective-permute-start | bytes 2359304 | tf_op jit(solution)/shard_map/ppermute | solution.py:17
  185.5 17.6 %collective-permute-start.21 = (bf16[192,1024]{1,0:T(8,128)(2,1)S(1)}, bf16[192,1024]{1,0:T(8,128)(2,1)S(1)}, u32[]{:S(2)}, u32[]{:S(2)}) collective-permute-start(bf16[192,1024]{1,0:T(8,128)(2,1)S(1)} %get-tuple-element.67), channel_id=1, source_target_pairs={{0,1},{1,0},{2,3},{3,2},{4,5},{5,4},{6,7},{7,6},{8,9},{9,8},{10,11... | collective-permute-start | bytes 1179656 | tf_op jit(solution)/shard_map/ppermute | solution.py:17
  185.8 18.5 %collective-permute-start.22 = (bf16[192,1024]{1,0:T(8,128)(2,1)S(1)}, bf16[192,1024]{1,0:T(8,128)(2,1)S(1)}, u32[]{:S(2)}, u32[]{:S(2)}) collective-permute-start(bf16[192,1024]{1,0:T(8,128)(2,1)S(1)} %get-tuple-element.69), channel_id=1, source_target_pairs={{0,2},{1,3},{2,0},{3,1},{4,6},{5,7},{6,4},{7,5},{8,10},{9,11},{10,... | collective-permute-start | bytes 1179656 | tf_op jit(solution)/shard_map/ppermute | solution.py:17
  204.3 8.7 %collective-permute-start.30 = (bf16[3,16,32,128]{3,2,1,0:T(8,128)(2,1)S(1)}, bf16[3,16,32,128]{3,2,1,0:T(8,128)(2,1)S(1)}, u32[]{:S(2)}, u32[]{:S(2)}) collective-permute-start(bf16[3,16,32,128]{3,2,1,0:T(8,128)(2,1)S(1)} %pad_maximum_fusion.11), channel_id=1, source_target_pairs={{0,8},{4,12},{8,0},{12,4},{16,24},{20,28},{24,16},{28,20},{1,9},{5... | collective-permute-start | bytes 1179656 | tf_op jit(solution)/shard_map/ppermute | solution.py:17
  205.3 8.5 %collective-permute-start.29 = (bf16[3,16,32,128]{3,2,1,0:T(8,128)(2,1)S(1)}, bf16[3,16,32,128]{3,2,1,0:T(8,128)(2,1)S(1)}, u32[]{:S(2)}, u32[]{:S(2)}) collective-permute-start(bf16[3,16,32,128]{3,2,1,0:T(8,128)(2,1)S(1)} %pad_maximum_fusion.10), channel_id=1, source_target_pairs={{0,16},{4,20},{8,24},{12,28},{16,0},{20,4},{24,8},{28,12},{1,17},{... | collective-permute-start | bytes 1179656 | tf_op jit(solution)/shard_map/ppermute | solution.py:17
  214.0 5.6 %collective-permute-start.31 = (bf16[4,1,16,32,256]{4,3,2,1,0:T(8,128)(2,1)S(1)}, bf16[4,1,16,32,256]{4,3,2,1,0:T(8,128)(2,1)S(1)}, u32[]{:S(2)}, u32[]{:S(2)}) collective-permute-start(bf16[4,1,16,32,256]{4,3,2,1,0:T(8,128)(2,1)S(1)} %maximum_bitcast_fusion.1.refs_0_), channel_id=1, source_target_pairs={{0,4},{4,0},{8,12},{12,8},{16,20},{20,16},{24,28},{28,24},{1,5},{5... | collective-permute-start | bytes 3145736 | tf_op jit(solution)/shard_map/ppermute | solution.py:17
  (8 other events, 7.0 us)

commit v4 on v3

--- a/solution.py
+++ b/solution.py
@@ -10,7 +10,7 @@
 F32 = jnp.float32
 BF16 = jnp.bfloat16
 COST = pl.CostEstimate(flops=1, bytes_accessed=1, transcendentals=0)
-VMEM_LIMIT = 28 * 1024 * 1024
+VMEM_LIMIT = 20 * 1024 * 1024
 
 
 def swap(value, axis, mask):
@@ -274,7 +274,7 @@
 def gather_pieces(own, shards, tie):
     half = own.shape[-1] // 2
     low, high, full = slice(0, half), slice(half, None), slice(None)
-    far = {0: [(full, own)]}
+    far, cut = {0: [(full, own)]}, []
     for mask in range(2, shards, 2):
         last_a, last_b = highest(mask), mask & -mask
         if last_a == last_b:
@@ -287,10 +287,12 @@
                     value = value[..., columns]
                 elif held != columns:
                     continue
-                far[mask].append((columns, swap(after(value, *tie), "dp", last)))
+                value = after(value, *tie)
+                cut.append(value)
+                far[mask].append((columns, swap(value, "dp", last)))
     near = [mask for mask in far if len(far[mask]) == 1]
     rest = [mask for mask in far if mask not in near]
-    pieces = [(near, jnp.stack([far[mask][0][1] for mask in near]))]
+    pieces = [(near, jnp.stack([after(far[mask][0][1], *cut) for mask in near]))]
     if rest:
         joined = [jnp.concatenate([value for _, value in far[mask]], axis=-1) for mask in rest]
         pieces.append((rest, jnp.stack(joined)))

time: 223 us -> 212 us (0.951)
  other arithmetic: 19.4 us -> 14.5 us
  local copies, waits for them, and re-layouts: 18.1 us -> 14.3 us
    another operation x3, other arithmetic: 4.14 us -> 0.73 us  [scatter_sum(): jnp.stack([sum((t.astype(F32) for t in terms[q])).astype(BF16) for q in g...]
    unnamed x48 -> x54, local copies, waits for them, and re-layouts: 10.2 us -> 8.25 us
  transfers between devices with their start and end apart: 32 -> 32, of which waited for: 14 -> 17; matrix products, arithmetic and copies ran while one was open for 12% -> 9% of each run, Pallas kernels for 19% -> 20%
where the time goes in v4:
time: 212 us; the launch traced here: 211 us
  waiting for transfers between devices  93.6 us (44%)
  Pallas kernels  49.1 us (23%)
  starting transfers between devices  37.5 us (18%)
  other arithmetic  14.5 us (7%)
  local copies, waits for them, and re-layouts  14.3 us (7%)
    ppermute x32, waiting for transfers between devices, swap(): lax.ppermute(value, axis, [(i, i ^ mask) for i in range(lax.axis_size(axi...  93.6 us
    ppermute x32, starting transfers between devices, swap(): lax.ppermute(value, axis, [(i, i ^ mask) for i in range(lax.axis_size(axi...  37.5 us
    pallas_call x1, Pallas kernels, rows_terms(): pl.pallas_call(functools.partial(rows_kernel, pieces, distances, parts),...  16.4 us
    pallas_call x1, Pallas kernels, pair_grads(): pl.pallas_call(functools.partial(pair_kernel, distances, shards, scale),...  13.6 us
    pallas_call x3, Pallas kernels, back_terms(): pl.pallas_call(functools.partial(back_kernel, pieces, n_levels), grid_spe...  11.9 us
    unnamed x54, local copies, waits for them, and re-layouts  8.25 us
    pallas_call x1, Pallas kernels, block_grads(): pl.pallas_call(functools.partial(grads_kernel, n_parts, n_levels, shards,...  4.45 us
  transfers between devices with their start and end apart: 32, of which 17 were waited for; matrix products, arithmetic and copies ran while one was open for 9% of the time, Pallas kernels for 20%

profile of v4, /device:TPU:0, one launch (start us, length us, event | category | flops | bytes accessed | tf_op | source)
XLA Modules:
  0.0 211.3 jit_solution(351843369948220728)
XLA Ops:
  0.7 2.3 %pad_maximum_fusion.1 = bf16[2,192,4096]{2,1,0:T(8,128)(2,1)S(1)} fusion(bf16[1,192,4096]{2,1,0:T(8,128)(2,1)} %bitcast.99, bf16[1,192,4096]{2,1,0:T(8,128)(2,1)} %bitcast.100), kind=kLoop, calls=%fused_computation.2 | loop fusion | flops 1572864 | bytes 6291456 | tf_op jit(solution)/shard_map/stack | solution.py:436
  3.5 2.6 %collective-permute-start.6 = (bf16[7,16,32,256]{3,2,1,0:T(8,128)(2,1)S(1)}, bf16[7,16,32,256]{3,2,1,0:T(8,128)(2,1)S(1)}, u32[]{:S(2)}, u32[]{:S(2)}) collective-permute-start(bf16[7,16,32,256]{3,2,1,0:T(8,128)(2,1)S(1)} %copy-done.19), channel_id=1, source_target_pairs={{0,16},{4,20},{8,24},{12,28},{16,0},{20,4},{24,8},{28,12},{1,17},{... | collective-permute-start | bytes 5505032 | tf_op jit(solution)/shard_map/ppermute | solution.py:17
  6.1 1.5 collective-permute-start
  8.8 1.0 fusion.7
  9.9 1.6 collective-permute-start.1
  11.5 2.6 %collective-permute-start.2 = (bf16[192,1024]{1,0:T(8,128)(2,1)S(1)}, bf16[192,1024]{1,0:T(8,128)(2,1)S(1)}, u32[]{:S(2)}, u32[]{:S(2)}) collective-permute-start(bf16[192,1024]{1,0:T(8,128)(2,1)S(1)} %get-tuple-element.112), channel_id=1, source_target_pairs={{0,2},{1,3},{2,0},{3,1},{4,6},{5,7},{6,4},{7,5},{8,10},{9,11},{10,... | collective-permute-start | bytes 1179656 | tf_op jit(solution)/shard_map/ppermute | solution.py:17
  14.1 17.3 %collective-permute-done.1.refs_4_.refs_0_ = bf16[192,1280]{1,0:T(8,128)(2,1)S(1)} collective-permute-done((bf16[192,1280]{1,0:T(8,128)(2,1)S(1)}, bf16[192,1280]{1,0:T(8,128)(2,1)S(1)}, u32[]{:S(2)}, u32[]{:S(2)}) %collective-permute-start.1) | collective-permute-done | bytes 491552 | tf_op jit(solution)/shard_map/ppermute | solution.py:17
  31.4 0.8 copy-done.8
  32.2 1.7 collective-permute-start.5
  34.0 2.5 %collective-permute-start.4 = (bf16[192,1024]{1,0:T(8,128)(2,1)S(1)}, bf16[192,1024]{1,0:T(8,128)(2,1)S(1)}, u32[]{:S(2)}, u32[]{:S(2)}) collective-permute-start(bf16[192,1024]{1,0:T(8,128)(2,1)S(1)} %get-tuple-element.48), channel_id=1, source_target_pairs={{0,1},{1,0},{2,3},{3,2},{4,5},{5,4},{6,7},{7,6},{8,9},{9,8},{10,11... | collective-permute-start | bytes 1179656 | tf_op jit(solution)/shard_map/ppermute | solution.py:17
  36.4 11.8 %collective-permute-done = bf16[7,16,32,256]{3,2,1,0:T(8,128)(2,1)S(1)} collective-permute-done((bf16[7,16,32,256]{3,2,1,0:T(8,128)(2,1)S(1)}, bf16[7,16,32,256]{3,2,1,0:T(8,128)(2,1)S(1)}, u32[]{:S(2)}, u32[]{:S(2)}) %collective-permute-start) | collective-permute-done | bytes 1835040 | tf_op jit(solution)/shard_map/ppermute | solution.py:17
  48.2 1.1 slice.299
  49.3 1.1 slice.301
  50.4 1.7 collective-permute-done.4.refs_6_.refs_2_
  52.8 3.0 %collective-permute-done.5.refs_7_.refs_3_ = bf16[192,1280]{1,0:T(8,128)(2,1)S(1)} collective-permute-done((bf16[192,1280]{1,0:T(8,128)(2,1)S(1)}, bf16[192,1280]{1,0:T(8,128)(2,1)S(1)}, u32[]{:S(2)}, u32[]{:S(2)}) %collective-permute-start.5) | collective-permute-done | bytes 491552 | tf_op jit(solution)/shard_map/ppermute | solution.py:17
  56.7 3.0 %pad_maximum_fusion.refs_0_.refs_8_ = bf16[3,7,16,32,256]{4,3,2,1,0:T(8,128)(2,1)} fusion(bf16[1,7,16,32,256]{4,3,2,1,0:T(8,128)(2,1)S(1)} %bitcast.103, bf16[1,7,16,32,256]{4,3,2,1,0:T(8,128)(2,1)S(1)} %bitcast.104, bf16[1,7,16,32,256]{4,3,2,1,0:T(8,128)(2,1)S(1)} %bitcast.106), kind=kLoop, calls=%fused_computation | loop fusion | flops 5505024 | bytes 11010048 | tf_op jit(solution)/shard_map/stack | solution.py:295
  61.8 3.2 %collective-permute-start.12 = (bf16[192,1024]{1,0:T(8,128)(2,1)}, bf16[192,1024]{1,0:T(8,128)(2,1)}, u32[]{:S(2)}, u32[]{:S(2)}) collective-permute-start(bf16[192,1024]{1,0:T(8,128)(2,1)} %get-tuple-element.56), channel_id=1, source_target_pairs={{0,2},{1,3},{2,0},{3,1},{4,6},{5,7},{6,4},{7,5},{8,10},{9,11},{10,... | collective-permute-start | bytes 1179656 | tf_op jit(solution)/shard_map/ppermute | solution.py:17
  65.0 1.9 copy-done.3
  66.9 0.9 copy-done.15
  67.8 0.9 copy-done.18
  68.7 13.6 %shard_map.92 = bf16[4,6,16,32,256]{4,3,2,1,0:T(8,128)(2,1)S(1)} custom-call(s32[1]{0:T(128)} %bitcast.pos_ref, bf16[192,4096]{1,0:T(8,128)(2,1)S(1)} %copy-done.1, bf16[192,4096]{1,0:T(8,128)(2,1)S(1)} %copy-done, bf16[192,256]{1,0:T(8,128)(2,1)S(1)} %copy-done.15, bf16[2,192,4096]{2,1,0:T(8,128)(2,1)S(1)} %copy-done.3, ...), custom_call_target="tpu_custom_call" | custom-call | flops 1 | bytes 1 | tf_op jit(solution)/shard_map/pallas_call | solution.py:132
  82.3 1.1 collective-permute-done.8
  83.6 1.8 maximum_bitcast_fusion.refs_1_.refs_9_
  85.5 1.0 slice_bitcast_fusion.2
  86.8 3.2 %collective-permute-start.15 = (bf16[192,1024]{1,0:T(8,128)(2,1)S(1)}, bf16[192,1024]{1,0:T(8,128)(2,1)S(1)}, u32[]{:S(2)}, u32[]{:S(2)}) collective-permute-start(bf16[192,1024]{1,0:T(8,128)(2,1)S(1)} %copy-done.26), channel_id=1, source_target_pairs={{0,2},{1,3},{2,0},{3,1},{4,6},{5,7},{6,4},{7,5},{8,10},{9,11},{10,... | collective-permute-start | bytes 1179656 | tf_op jit(solution)/shard_map/ppermute | solution.py:17
  90.5 5.2 %shard_map.93 = (bf16[192,1792]{1,0:T(8,128)(2,1)S(1)}, bf16[192,1792]{1,0:T(8,128)(2,1)S(1)}) custom-call(s32[1]{0:T(128)} %bitcast.pos_ref, bf16[192,4096]{1,0:T(8,128)(2,1)S(1)} %copy-done, bf16[3,7,16,32,256]{4,3,2,1,0:T(8,128)(2,1)} %pad_maximum_fusion.refs_0_.refs_8_, bf16[1,7,16,32,256]{4,3,2,1,0:T(8,128)(2,1)S(1)} %maximum_bitcast_fusion.refs_1_.refs_9_, ...), custom_call_target="tpu_custom_call" | custom-call | flops 1 | bytes 1 | tf_op jit(solution)/shard_map/pallas_call | solution.py:254
  95.7 10.8 %collective-permute-done.14.refs_10_.refs_6_ = bf16[192,1024]{1,0:T(8,128)(2,1)S(1)} collective-permute-done((bf16[192,1024]{1,0:T(8,128)(2,1)S(1)}, bf16[192,1024]{1,0:T(8,128)(2,1)S(1)}, u32[]{:S(2)}, u32[]{:S(2)}) %collective-permute-start.14) | collective-permute-done | bytes 393248 | tf_op jit(solution)/shard_map/ppermute | solution.py:17
  106.5 1.4 collective-permute-done.15.refs_11_.refs_7_
  107.9 4.5 %shard_map.94 = (bf16[4,2,4,4,32,256]{5,4,3,2,1,0:T(8,128)(2,1)S(1)}, bf16[4,2,4,4,32,256]{5,4,3,2,1,0:T(8,128)(2,1)S(1)}) custom-call(s32[1]{0:T(128)} %bitcast.pos_ref, bf16[192,4096]{1,0:T(8,128)(2,1)S(1)} %copy-done, bf16[192,4096]{1,0:T(8,128)(2,1)S(1)} %copy-done, bf16[192,4096]{1,0:T(8,128)(2,1)S(1)} %copy-done, bf16[192,4096]{1,0:T(8,128)(2,1)S(1)} %copy-done, ...), custom_call_target="tpu_custom_call" | custom-call | flops 1 | bytes 1 | tf_op jit(solution)/shard_map/pallas_call | solution.py:76
  112.7 1.6 collective-permute-start.23
  115.1 2.7 %collective-permute-start.17 = (bf16[192,1792]{1,0:T(8,128)(2,1)S(1)}, bf16[192,1792]{1,0:T(8,128)(2,1)S(1)}, u32[]{:S(2)}, u32[]{:S(2)}) collective-permute-start(bf16[192,1792]{1,0:T(8,128)(2,1)S(1)} %get-tuple-element.62), channel_id=1, source_target_pairs={{0,2},{1,3},{2,0},{3,1},{4,6},{5,7},{6,4},{7,5},{8,10},{9,11},{10,... | collective-permute-start | bytes 2064392 | tf_op jit(solution)/shard_map/ppermute | solution.py:17
  117.8 2.9 %shard_map.97 = (bf16[192,1024]{1,0:T(8,128)(2,1)S(1)}, bf16[192,1024]{1,0:T(8,128)(2,1)S(1)}) custom-call(s32[1]{0:T(128)} %bitcast.pos_ref, bf16[192,4096]{1,0:T(8,128)(2,1)S(1)} %copy-done, bf16[3,7,16,32,256]{4,3,2,1,0:T(8,128)(2,1)} %pad_maximum_fusion.refs_0_.refs_8_, bf16[1,7,16,32,256]{4,3,2,1,0:T(8,128)(2,1)S(1)} %maximum_bitcast_fusion.refs_1_.refs_9_, ...), custom_call_target="tpu_custom_call" | custom-call | flops 1 | bytes 1 | tf_op jit(solution)/shard_map/pallas_call | solution.py:254
  120.7 3.8 %shard_map.96 = (bf16[192,1280]{1,0:T(8,128)(2,1)S(1)}, bf16[192,1280]{1,0:T(8,128)(2,1)S(1)}) custom-call(s32[1]{0:T(128)} %bitcast.pos_ref, bf16[192,4096]{1,0:T(8,128)(2,1)S(1)} %copy-done, bf16[3,7,16,32,256]{4,3,2,1,0:T(8,128)(2,1)} %pad_maximum_fusion.refs_0_.refs_8_, bf16[1,7,16,32,256]{4,3,2,1,0:T(8,128)(2,1)S(1)} %maximum_bitcast_fusion.refs_1_.refs_9_, ...), custom_call_target="tpu_custom_call" | custom-call | flops 1 | bytes 1 | tf_op jit(solution)/shard_map/pallas_call | solution.py:254
  124.8 21.8 %collective-permute-done.16 = bf16[192,1792]{1,0:T(8,128)(2,1)S(1)} collective-permute-done((bf16[192,1792]{1,0:T(8,128)(2,1)S(1)}, bf16[192,1792]{1,0:T(8,128)(2,1)S(1)}, u32[]{:S(2)}, u32[]{:S(2)}) %collective-permute-start.16) | collective-permute-done | bytes 688160 | tf_op jit(solution)/shard_map/ppermute | solution.py:17
  146.6 1.3 collective-permute-done.17
  148.2 2.6 %collective-permute-start.20 = (bf16[192,1280]{1,0:T(8,128)(2,1)S(1)}, bf16[192,1280]{1,0:T(8,128)(2,1)}, u32[]{:S(2)}, u32[]{:S(2)}) collective-permute-start(bf16[192,1280]{1,0:T(8,128)(2,1)S(1)} %get-tuple-element.72), channel_id=1, source_target_pairs={{0,2},{1,3},{2,0},{3,1},{4,6},{5,7},{6,4},{7,5},{8,10},{9,11},{10,... | collective-permute-start | bytes 1474568 | tf_op jit(solution)/shard_map/ppermute | solution.py:17
  151.9 1.5 collective-permute-start.24
  154.0 16.4 %shard_map.95 = (bf16[192,4096]{1,0:T(8,128)(2,1)}, f32[192,4096]{1,0:T(8,128)S(1)}) custom-call(s32[1]{0:T(128)} %bitcast.pos_ref, bf16[192,4096]{1,0:T(8,128)(2,1)S(1)} %copy-done.1, bf16[192,4096]{1,0:T(8,128)(2,1)S(1)} %copy-done, bf16[192,128]{1,0:T(8,128)(2,1)S(1)} %get-tuple-element.126.fac_ref, bf16[192,128]{1,0:T(8,128)(2,1)S(1)} %get-tuple-element.125.back_ref, ...), custom_call_target="tpu_custom_call" | custom-call | flops 1 | bytes 1 | tf_op jit(solution)/shard_map/pallas_call | solution.py:217
  171.2 0.9 copy-done.21
  173.0 1.6 collective-permute-start.27
  175.4 2.7 %collective-permute-start.22 = (bf16[192,1024]{1,0:T(8,128)(2,1)S(1)}, bf16[192,1024]{1,0:T(8,128)(2,1)S(1)}, u32[]{:S(2)}, u32[]{:S(2)}) collective-permute-start(bf16[192,1024]{1,0:T(8,128)(2,1)S(1)} %get-tuple-element.75), channel_id=1, source_target_pairs={{0,2},{1,3},{2,0},{3,1},{4,6},{5,7},{6,4},{7,5},{8,10},{9,11},{10,... | collective-permute-start | bytes 1179656 | tf_op jit(solution)/shard_map/ppermute | solution.py:17
  178.1 12.4 %collective-permute-done.27 = bf16[6,16,32,128]{3,2,1,0:T(8,128)(2,1)S(1)} collective-permute-done((bf16[6,16,32,128]{3,2,1,0:T(8,128)(2,1)S(1)}, bf16[6,16,32,128]{3,2,1,0:T(8,128)(2,1)S(1)}, u32[]{:S(2)}, u32[]{:S(2)}) %collective-permute-start.27) | collective-permute-done | bytes 786464 | tf_op jit(solution)/shard_map/ppermute | solution.py:17
  190.5 1.2 collective-permute-done.28
  192.6 1.2 collective-permute-done.22
  195.4 7.2 %collective-permute-done.30 = bf16[3,16,32,128]{3,2,1,0:T(8,128)(2,1)S(1)} collective-permute-done((bf16[3,16,32,128]{3,2,1,0:T(8,128)(2,1)S(1)}, bf16[3,16,32,128]{3,2,1,0:T(8,128)(2,1)S(1)}, u32[]{:S(2)}, u32[]{:S(2)}) %collective-permute-start.30) | collective-permute-done | bytes 393248 | tf_op jit(solution)/shard_map/ppermute | solution.py:17
  203.4 2.5 %add_convert_fusion = bf16[192,4096]{1,0:T(8,128)(2,1)} fusion(f32[192,4096]{1,0:T(8,128)S(1)} %get-tuple-element.67, bf16[192,1024]{1,0:T(8,128)(2,1)S(1)} %collective-permute-done.21, bf16[192,1280]{1,0:T(8,128)(2,1)} %collective-permute-done.19, bf16[192,1792]{1,0:T(8,128)(2,1)S(1)} %copy-done.23, bf16[192,1024]{1,0:T(8,128)(2,1)S(1)} %collective-permute-done.22, ...), kind=kLoop, calls=%fused_computation.3 | loop fusion | flops 11796480 | bytes 7864320 | tf_op jit(solution)/shard_map/convert_element_type | solution.py:504
  206.4 2.2 %maximum_maximum_fusion = f32[7,16,32,256]{3,2,1,0:T(8,128)} fusion(f32[2,16,32,128]{3,2,1,0:T(8,128)S(1)} %get-tuple-element.114, f32[5,16,32,128]{3,2,1,0:T(8,128)S(1)} %slice.343, f32[2,16,32,128]{3,2,1,0:T(8,128)S(1)} %get-tuple-element.113, f32[5,16,32,128]{3,2,1,0:T(8,128)S(1)} %slice.315), kind=kLoop, calls=%fused_computation.1 | loop fusion | flops 2752512 | bytes 7340032 | tf_op jit(solution)/shard_map/concatenate | solution.py:495
  208.6 2.7 %shard_map.98 = (f32[4096,128]{1,0:T(8,128)}, f32[128,4096]{1,0:T(8,128)}) custom-call(s32[1]{0:T(128)} %bitcast.pos_ref, bf16[4,1,16,32,256]{4,3,2,1,0:T(8,128)(2,1)S(1)} %maximum_bitcast_fusion.1.refs_0_, bf16[4,1,16,32,256]{4,3,2,1,0:T(8,128)(2,1)S(1)} %collective-permute-done.31.refs_1_), custom_call_target="tpu_custom_call" | custom-call | flops 1 | bytes 1 | tf_op jit(solution)/shard_map/pallas_call | solution.py:382
  (124 shorter events, 16.1 us)
Async XLA Ops:
  0.6 7.0 %copy-start = (bf16[192,4096]{1,0:T(8,128)(2,1)S(1)}, bf16[192,4096]{1,0:T(8,128)(2,1)}, u32[]{:S(2)}) copy-start(bf16[192,4096]{1,0:T(8,128)(2,1)} %cot_ref.6) | copy-start | bytes 4718596
  0.7 7.0 %copy-start.4 = (bf16[128,4096]{1,0:T(8,128)(2,1)S(1)}, bf16[128,4096]{1,0:T(8,128)(2,1)}, u32[]{:S(2)}) copy-start(bf16[128,4096]{1,0:T(8,128)(2,1)} %right_ref.1) | copy-start | bytes 3145732
  3.0 5.2 %copy-start.1 = (bf16[192,4096]{1,0:T(8,128)(2,1)S(1)}, bf16[192,4096]{1,0:T(8,128)(2,1)}, u32[]{:S(2)}) copy-start(bf16[192,4096]{1,0:T(8,128)(2,1)} %hid_ref.1) | copy-start | bytes 4718596
  3.0 5.2 %copy-start.6 = (bf16[4096,128]{1,0:T(8,128)(2,1)S(1)}, bf16[4096,128]{1,0:T(8,128)(2,1)}, u32[]{:S(2)}) copy-start(bf16[4096,128]{1,0:T(8,128)(2,1)} %left_ref.1) | copy-start | bytes 3145732
  3.0 29.2 %collective-permute-start.3 = (bf16[2,192,4096]{2,1,0:T(8,128)(2,1)S(1)}, bf16[2,192,4096]{2,1,0:T(8,128)(2,1)S(1)}, u32[]{:S(2)}, u32[]{:S(2)}) collective-permute-start(bf16[2,192,4096]{2,1,0:T(8,128)(2,1)S(1)} %pad_maximum_fusion.1), channel_id=1, source_target_pairs={{0,4},{4,0},{8,12},{12,8},{16,20},{20,16},{24,28},{28,24},{1,5},{5... | collective-permute-start | bytes 9437192 | tf_op jit(solution)/shard_map/ppermute | solution.py:17
  3.5 45.8 %collective-permute-start.6 = (bf16[7,16,32,256]{3,2,1,0:T(8,128)(2,1)S(1)}, bf16[7,16,32,256]{3,2,1,0:T(8,128)(2,1)S(1)}, u32[]{:S(2)}, u32[]{:S(2)}) collective-permute-start(bf16[7,16,32,256]{3,2,1,0:T(8,128)(2,1)S(1)} %copy-done.19), channel_id=1, source_target_pairs={{0,16},{4,20},{8,24},{12,28},{16,0},{20,4},{24,8},{28,12},{1,17},{... | collective-permute-start | bytes 5505032 | tf_op jit(solution)/shard_map/ppermute | solution.py:17
  6.1 42.1 %collective-permute-start = (bf16[7,16,32,256]{3,2,1,0:T(8,128)(2,1)S(1)}, bf16[7,16,32,256]{3,2,1,0:T(8,128)(2,1)S(1)}, u32[]{:S(2)}, u32[]{:S(2)}) collective-permute-start(bf16[7,16,32,256]{3,2,1,0:T(8,128)(2,1)S(1)} %copy-done.19), channel_id=1, source_target_pairs={{0,8},{4,12},{8,0},{12,4},{16,24},{20,28},{24,16},{28,20},{1,9},{5... | collective-permute-start | bytes 5505032 | tf_op jit(solution)/shard_map/ppermute | solution.py:17
  9.9 21.5 %collective-permute-start.1 = (bf16[192,1280]{1,0:T(8,128)(2,1)S(1)}, bf16[192,1280]{1,0:T(8,128)(2,1)S(1)}, u32[]{:S(2)}, u32[]{:S(2)}) collective-permute-start(bf16[192,1280]{1,0:T(8,128)(2,1)S(1)} %pad_maximum_fusion.8), channel_id=1, source_target_pairs={{0,1},{1,0},{2,3},{3,2},{4,5},{5,4},{6,7},{7,6},{8,9},{9,8},{10,11... | collective-permute-start | bytes 1474568 | tf_op jit(solution)/shard_map/ppermute | solution.py:17
  11.5 20.7 %collective-permute-start.2 = (bf16[192,1024]{1,0:T(8,128)(2,1)S(1)}, bf16[192,1024]{1,0:T(8,128)(2,1)S(1)}, u32[]{:S(2)}, u32[]{:S(2)}) collective-permute-start(bf16[192,1024]{1,0:T(8,128)(2,1)S(1)} %get-tuple-element.112), channel_id=1, source_target_pairs={{0,2},{1,3},{2,0},{3,1},{4,6},{5,7},{6,4},{7,5},{8,10},{9,11},{10,... | collective-permute-start | bytes 1179656 | tf_op jit(solution)/shard_map/ppermute | solution.py:17
  32.2 18.3 %copy-start.2 = (bf16[2,192,4096]{2,1,0:T(8,128)(2,1)}, bf16[2,192,4096]{2,1,0:T(8,128)(2,1)S(1)}, u32[]{:S(2)}) copy-start(bf16[2,192,4096]{2,1,0:T(8,128)(2,1)S(1)} %collective-permute-done.3.refs_3_.refs_4_) | copy-start | bytes 9437188
  32.2 23.6 %collective-permute-start.5 = (bf16[192,1280]{1,0:T(8,128)(2,1)S(1)}, bf16[192,1280]{1,0:T(8,128)(2,1)S(1)}, u32[]{:S(2)}, u32[]{:S(2)}) collective-permute-start(bf16[192,1280]{1,0:T(8,128)(2,1)S(1)} %pad_maximum_fusion.9), channel_id=1, source_target_pairs={{0,2},{1,3},{2,0},{3,1},{4,6},{5,7},{6,4},{7,5},{8,10},{9,11},{10,... | collective-permute-start | bytes 1474568 | tf_op jit(solution)/shard_map/ppermute | solution.py:17
  34.0 18.1 %collective-permute-start.4 = (bf16[192,1024]{1,0:T(8,128)(2,1)S(1)}, bf16[192,1024]{1,0:T(8,128)(2,1)S(1)}, u32[]{:S(2)}, u32[]{:S(2)}) collective-permute-start(bf16[192,1024]{1,0:T(8,128)(2,1)S(1)} %get-tuple-element.48), channel_id=1, source_target_pairs={{0,1},{1,0},{2,3},{3,2},{4,5},{5,4},{6,7},{7,6},{8,9},{9,8},{10,11... | collective-permute-start | bytes 1179656 | tf_op jit(solution)/shard_map/ppermute | solution.py:17
  56.7 3.0 %copy-start.14 = (bf16[192,256]{1,0:T(8,128)(2,1)}, bf16[192,256]{1,0:T(8,128)(2,1)S(1)}, u32[]{:S(2)}) copy-start(bf16[192,256]{1,0:T(8,128)(2,1)S(1)} %add_convert_fusion.7.refs_2_) | copy-start | bytes 294916
  56.7 3.0 %collective-permute-start.9 = (bf16[192,256]{1,0:T(8,128)(2,1)S(1)}, bf16[192,256]{1,0:T(8,128)(2,1)S(1)}, u32[]{:S(2)}, u32[]{:S(2)}) collective-permute-start(bf16[192,256]{1,0:T(8,128)(2,1)S(1)} %add_convert_fusion.7.refs_2_), channel_id=1, source_target_pairs={{0,4},{4,0},{8,12},{12,8},{16,20},{20,16},{24,28},{28,24},{1,5},{5... | collective-permute-start | bytes 294920 | tf_op jit(solution)/shard_map/ppermute | solution.py:17
  60.3 30.2 %collective-permute-start.10 = (bf16[3,7,16,32,256]{4,3,2,1,0:T(8,128)(2,1)}, bf16[3,7,16,32,256]{4,3,2,1,0:T(8,128)(2,1)}, u32[]{:S(2)}, u32[]{:S(2)}) collective-permute-start(bf16[3,7,16,32,256]{4,3,2,1,0:T(8,128)(2,1)} %pad_maximum_fusion.refs_0_.refs_8_), channel_id=1, source_target_pairs={{0,4},{4,0},{8,12},{12,8},{16,20},{20,16},{24,28},{28,24},{1,5},{5... | collective-permute-start | bytes 16515080 | tf_op jit(solution)/shard_map/ppermute | solution.py:17
  60.8 22.6 %collective-permute-start.8 = (bf16[7,16,32,128]{3,2,1,0:T(8,128)(2,1)}, bf16[7,16,32,128]{3,2,1,0:T(8,128)(2,1)}, u32[]{:S(2)}, u32[]{:S(2)}) collective-permute-start(bf16[7,16,32,128]{3,2,1,0:T(8,128)(2,1)} %slice.301), channel_id=1, source_target_pairs={{0,8},{4,12},{8,0},{12,4},{16,24},{20,28},{24,16},{28,20},{1,9},{5... | collective-permute-start | bytes 2752520 | tf_op jit(solution)/shard_map/ppermute | solution.py:17
  61.3 22.3 %collective-permute-start.7 = (bf16[7,16,32,128]{3,2,1,0:T(8,128)(2,1)}, bf16[7,16,32,128]{3,2,1,0:T(8,128)(2,1)}, u32[]{:S(2)}, u32[]{:S(2)}) collective-permute-start(bf16[7,16,32,128]{3,2,1,0:T(8,128)(2,1)} %slice.299), channel_id=1, source_target_pairs={{0,16},{4,20},{8,24},{12,28},{16,0},{20,4},{24,8},{28,12},{1,17},{... | collective-permute-start | bytes 2752520 | tf_op jit(solution)/shard_map/ppermute | solution.py:17
  61.8 23.6 %collective-permute-start.11 = (bf16[192,1024]{1,0:T(8,128)(2,1)}, bf16[192,1024]{1,0:T(8,128)(2,1)}, u32[]{:S(2)}, u32[]{:S(2)}) collective-permute-start(bf16[192,1024]{1,0:T(8,128)(2,1)} %get-tuple-element.56), channel_id=1, source_target_pairs={{0,1},{1,0},{2,3},{3,2},{4,5},{5,4},{6,7},{7,6},{8,9},{9,8},{10,11... | collective-permute-start | bytes 1179656 | tf_op jit(solution)/shard_map/ppermute | solution.py:17
  61.8 23.6 %collective-permute-start.12 = (bf16[192,1024]{1,0:T(8,128)(2,1)}, bf16[192,1024]{1,0:T(8,128)(2,1)}, u32[]{:S(2)}, u32[]{:S(2)}) collective-permute-start(bf16[192,1024]{1,0:T(8,128)(2,1)} %get-tuple-element.56), channel_id=1, source_target_pairs={{0,2},{1,3},{2,0},{3,1},{4,6},{5,7},{6,4},{7,5},{8,10},{9,11},{10,... | collective-permute-start | bytes 1179656 | tf_op jit(solution)/shard_map/ppermute | solution.py:17
  85.4 5.1 %collective-permute-start.13 = (bf16[1,7,16,32,256]{4,3,2,1,0:T(8,128)(2,1)S(1)}, bf16[1,7,16,32,256]{4,3,2,1,0:T(8,128)(2,1)S(1)}, u32[]{:S(2)}, u32[]{:S(2)}) collective-permute-start(bf16[1,7,16,32,256]{4,3,2,1,0:T(8,128)(2,1)S(1)} %maximum_bitcast_fusion.refs_1_.refs_9_), channel_id=1, source_target_pairs={{0,4},{4,0},{8,12},{12,8},{16,20},{20,16},{24,28},{28,24},{1,5},{5... | collective-permute-start | bytes 5505032 | tf_op jit(solution)/shard_map/ppermute | solution.py:17
  86.7 19.8 %collective-permute-start.14 = (bf16[192,1024]{1,0:T(8,128)(2,1)S(1)}, bf16[192,1024]{1,0:T(8,128)(2,1)S(1)}, u32[]{:S(2)}, u32[]{:S(2)}) collective-permute-start(bf16[192,1024]{1,0:T(8,128)(2,1)S(1)} %copy-done.26), channel_id=1, source_target_pairs={{0,1},{1,0},{2,3},{3,2},{4,5},{5,4},{6,7},{7,6},{8,9},{9,8},{10,11... | collective-permute-start | bytes 1179656 | tf_op jit(solution)/shard_map/ppermute | solution.py:17
  86.8 21.1 %collective-permute-start.15 = (bf16[192,1024]{1,0:T(8,128)(2,1)S(1)}, bf16[192,1024]{1,0:T(8,128)(2,1)S(1)}, u32[]{:S(2)}, u32[]{:S(2)}) collective-permute-start(bf16[192,1024]{1,0:T(8,128)(2,1)S(1)} %copy-done.26), channel_id=1, source_target_pairs={{0,2},{1,3},{2,0},{3,1},{4,6},{5,7},{6,4},{7,5},{8,10},{9,11},{10,... | collective-permute-start | bytes 1179656 | tf_op jit(solution)/shard_map/ppermute | solution.py:17
  90.4 17.4 %copy-start.9 = (bf16[192,1280]{1,0:T(8,128)(2,1)S(1)}, bf16[192,1280]{1,0:T(8,128)(2,1)}, u32[]{:S(2)}) copy-start(bf16[192,1280]{1,0:T(8,128)(2,1)} %copy-done.8) | copy-start | bytes 1474564
  90.5 17.4 %copy-start.11 = (bf16[192,1280]{1,0:T(8,128)(2,1)S(1)}, bf16[192,1280]{1,0:T(8,128)(2,1)}, u32[]{:S(2)}) copy-start(bf16[192,1280]{1,0:T(8,128)(2,1)} %copy-done.10) | copy-start | bytes 1474564
  90.5 17.4 %copy-start.13 = (bf16[192,1024]{1,0:T(8,128)(2,1)S(1)}, bf16[192,1024]{1,0:T(8,128)(2,1)}, u32[]{:S(2)}) copy-start(bf16[192,1024]{1,0:T(8,128)(2,1)} %copy-done.12) | copy-start | bytes 1179652
  112.3 41.6 %collective-permute-start.18 = (bf16[4,2,16,32,256]{4,3,2,1,0:T(8,128)(2,1)S(1)}, bf16[4,2,16,32,256]{4,3,2,1,0:T(8,128)(2,1)S(1)}, u32[]{:S(2)}, u32[]{:S(2)}) collective-permute-start(bf16[4,2,16,32,256]{4,3,2,1,0:T(8,128)(2,1)S(1)} %bitcast.102), channel_id=1, source_target_pairs={{0,4},{4,0},{8,12},{12,8},{16,20},{20,16},{24,28},{28,24},{1,5},{5... | collective-permute-start | bytes 6291464 | tf_op jit(solution)/shard_map/ppermute | solution.py:17
  112.6 5.2 %copy-start.16 = (bf16[192,256]{1,0:T(8,128)(2,1)S(1)}, bf16[192,256]{1,0:T(8,128)(2,1)}, u32[]{:S(2)}) copy-start(bf16[192,256]{1,0:T(8,128)(2,1)} %copy-done.14) | copy-start | bytes 294916
  112.7 38.0 %collective-permute-start.23 = (bf16[2,6,16,32,128]{4,3,2,1,0:T(8,128)(2,1)S(1)}, bf16[2,6,16,32,128]{4,3,2,1,0:T(8,128)(2,1)S(1)}, u32[]{:S(2)}, u32[]{:S(2)}) collective-permute-start(bf16[2,6,16,32,128]{4,3,2,1,0:T(8,128)(2,1)S(1)} %pad_maximum_fusion.2), channel_id=1, source_target_pairs={{0,8},{4,12},{8,0},{12,4},{16,24},{20,28},{24,16},{28,20},{1,9},{5... | collective-permute-start | bytes 4718600 | tf_op jit(solution)/shard_map/ppermute | solution.py:17
  114.3 36.5 %collective-permute-start.25 = (bf16[2,6,16,32,128]{4,3,2,1,0:T(8,128)(2,1)S(1)}, bf16[2,6,16,32,128]{4,3,2,1,0:T(8,128)(2,1)S(1)}, u32[]{:S(2)}, u32[]{:S(2)}) collective-permute-start(bf16[2,6,16,32,128]{4,3,2,1,0:T(8,128)(2,1)S(1)} %pad_maximum_fusion.3), channel_id=1, source_target_pairs={{0,16},{4,20},{8,24},{12,28},{16,0},{20,4},{24,8},{28,12},{1,17},{... | collective-permute-start | bytes 4718600 | tf_op jit(solution)/shard_map/ppermute | solution.py:17
  114.8 31.8 %collective-permute-start.16 = (bf16[192,1792]{1,0:T(8,128)(2,1)S(1)}, bf16[192,1792]{1,0:T(8,128)(2,1)S(1)}, u32[]{:S(2)}, u32[]{:S(2)}) collective-permute-start(bf16[192,1792]{1,0:T(8,128)(2,1)S(1)} %get-tuple-element.60), channel_id=1, source_target_pairs={{0,1},{1,0},{2,3},{3,2},{4,5},{5,4},{6,7},{7,6},{8,9},{9,8},{10,11... | collective-permute-start | bytes 2064392 | tf_op jit(solution)/shard_map/ppermute | solution.py:17
  115.1 32.7 %collective-permute-start.17 = (bf16[192,1792]{1,0:T(8,128)(2,1)S(1)}, bf16[192,1792]{1,0:T(8,128)(2,1)S(1)}, u32[]{:S(2)}, u32[]{:S(2)}) collective-permute-start(bf16[192,1792]{1,0:T(8,128)(2,1)S(1)} %get-tuple-element.62), channel_id=1, source_target_pairs={{0,2},{1,3},{2,0},{3,1},{4,6},{5,7},{6,4},{7,5},{8,10},{9,11},{10,... | collective-permute-start | bytes 2064392 | tf_op jit(solution)/shard_map/ppermute | solution.py:17
  146.6 4.2 %copy-start.22 = (bf16[192,1792]{1,0:T(8,128)(2,1)}, bf16[192,1792]{1,0:T(8,128)(2,1)S(1)}, u32[]{:S(2)}) copy-start(bf16[192,1792]{1,0:T(8,128)(2,1)S(1)} %collective-permute-done.16) | copy-start | bytes 2064388
  147.8 3.4 %copy-start.24 = (bf16[192,1792]{1,0:T(8,128)(2,1)}, bf16[192,1792]{1,0:T(8,128)(2,1)S(1)}, u32[]{:S(2)}) copy-start(bf16[192,1792]{1,0:T(8,128)(2,1)S(1)} %collective-permute-done.17) | copy-start | bytes 2064388
  147.8 25.1 %collective-permute-start.19 = (bf16[192,1280]{1,0:T(8,128)(2,1)S(1)}, bf16[192,1280]{1,0:T(8,128)(2,1)}, u32[]{:S(2)}, u32[]{:S(2)}) collective-permute-start(bf16[192,1280]{1,0:T(8,128)(2,1)S(1)} %get-tuple-element.69), channel_id=1, source_target_pairs={{0,1},{1,0},{2,3},{3,2},{4,5},{5,4},{6,7},{7,6},{8,9},{9,8},{10,11... | collective-permute-start | bytes 1474568 | tf_op jit(solution)/shard_map/ppermute | solution.py:17
  148.2 5.8 %copy-start.5 = (bf16[128,4096]{1,0:T(8,128)(2,1)S(1)}, bf16[128,4096]{1,0:T(8,128)(2,1)}, u32[]{:S(2)}) copy-start(bf16[128,4096]{1,0:T(8,128)(2,1)} %right_ref.1) | copy-start | bytes 3145732
  148.2 5.8 %copy-start.7 = (bf16[4096,128]{1,0:T(8,128)(2,1)S(1)}, bf16[4096,128]{1,0:T(8,128)(2,1)}, u32[]{:S(2)}) copy-start(bf16[4096,128]{1,0:T(8,128)(2,1)} %left_ref.1) | copy-start | bytes 3145732
  148.2 24.8 %collective-permute-start.20 = (bf16[192,1280]{1,0:T(8,128)(2,1)S(1)}, bf16[192,1280]{1,0:T(8,128)(2,1)}, u32[]{:S(2)}, u32[]{:S(2)}) collective-permute-start(bf16[192,1280]{1,0:T(8,128)(2,1)S(1)} %get-tuple-element.72), channel_id=1, source_target_pairs={{0,2},{1,3},{2,0},{3,1},{4,6},{5,7},{6,4},{7,5},{8,10},{9,11},{10,... | collective-permute-start | bytes 1474568 | tf_op jit(solution)/shard_map/ppermute | solution.py:17
  151.9 19.0 %collective-permute-start.24 = (bf16[1,6,16,32,128]{4,3,2,1,0:T(8,128)(2,1)S(1)}, bf16[1,6,16,32,128]{4,3,2,1,0:T(8,128)(2,1)S(1)}, u32[]{:S(2)}, u32[]{:S(2)}) collective-permute-start(bf16[1,6,16,32,128]{4,3,2,1,0:T(8,128)(2,1)S(1)} %get-tuple-element.78), channel_id=1, source_target_pairs={{0,16},{4,20},{8,24},{12,28},{16,0},{20,4},{24,8},{28,12},{1,17},{... | collective-permute-start | bytes 2359304 | tf_op jit(solution)/shard_map/ppermute | solution.py:17
  153.4 17.7 %collective-permute-start.26 = (bf16[1,6,16,32,128]{4,3,2,1,0:T(8,128)(2,1)S(1)}, bf16[1,6,16,32,128]{4,3,2,1,0:T(8,128)(2,1)S(1)}, u32[]{:S(2)}, u32[]{:S(2)}) collective-permute-start(bf16[1,6,16,32,128]{4,3,2,1,0:T(8,128)(2,1)S(1)} %get-tuple-element.80), channel_id=1, source_target_pairs={{0,8},{4,12},{8,0},{12,4},{16,24},{20,28},{24,16},{28,20},{1,9},{5... | collective-permute-start | bytes 2359304 | tf_op jit(solution)/shard_map/ppermute | solution.py:17
  173.0 17.5 %collective-permute-start.27 = (bf16[6,16,32,128]{3,2,1,0:T(8,128)(2,1)S(1)}, bf16[6,16,32,128]{3,2,1,0:T(8,128)(2,1)S(1)}, u32[]{:S(2)}, u32[]{:S(2)}) collective-permute-start(bf16[6,16,32,128]{3,2,1,0:T(8,128)(2,1)S(1)} %get-tuple-element.81), channel_id=1, source_target_pairs={{0,8},{4,12},{8,0},{12,4},{16,24},{20,28},{24,16},{28,20},{1,9},{5... | collective-permute-start | bytes 2359304 | tf_op jit(solution)/shard_map/ppermute | solution.py:17
  174.5 17.2 %collective-permute-start.28 = (bf16[6,16,32,128]{3,2,1,0:T(8,128)(2,1)S(1)}, bf16[6,16,32,128]{3,2,1,0:T(8,128)(2,1)S(1)}, u32[]{:S(2)}, u32[]{:S(2)}) collective-permute-start(bf16[6,16,32,128]{3,2,1,0:T(8,128)(2,1)S(1)} %get-tuple-element.82), channel_id=1, source_target_pairs={{0,16},{4,20},{8,24},{12,28},{16,0},{20,4},{24,8},{28,12},{1,17},{... | collective-permute-start | bytes 2359304 | tf_op jit(solution)/shard_map/ppermute | solution.py:17
  175.1 17.5 %collective-permute-start.21 = (bf16[192,1024]{1,0:T(8,128)(2,1)S(1)}, bf16[192,1024]{1,0:T(8,128)(2,1)S(1)}, u32[]{:S(2)}, u32[]{:S(2)}) collective-permute-start(bf16[192,1024]{1,0:T(8,128)(2,1)S(1)} %get-tuple-element.73), channel_id=1, source_target_pairs={{0,1},{1,0},{2,3},{3,2},{4,5},{5,4},{6,7},{7,6},{8,9},{9,8},{10,11... | collective-permute-start | bytes 1179656 | tf_op jit(solution)/shard_map/ppermute | solution.py:17
  175.4 18.5 %collective-permute-start.22 = (bf16[192,1024]{1,0:T(8,128)(2,1)S(1)}, bf16[192,1024]{1,0:T(8,128)(2,1)S(1)}, u32[]{:S(2)}, u32[]{:S(2)}) collective-permute-start(bf16[192,1024]{1,0:T(8,128)(2,1)S(1)} %get-tuple-element.75), channel_id=1, source_target_pairs={{0,2},{1,3},{2,0},{3,1},{4,6},{5,7},{6,4},{7,5},{8,10},{9,11},{10,... | collective-permute-start | bytes 1179656 | tf_op jit(solution)/shard_map/ppermute | solution.py:17
  193.9 8.8 %collective-permute-start.30 = (bf16[3,16,32,128]{3,2,1,0:T(8,128)(2,1)S(1)}, bf16[3,16,32,128]{3,2,1,0:T(8,128)(2,1)S(1)}, u32[]{:S(2)}, u32[]{:S(2)}) collective-permute-start(bf16[3,16,32,128]{3,2,1,0:T(8,128)(2,1)S(1)} %pad_maximum_fusion.11), channel_id=1, source_target_pairs={{0,8},{4,12},{8,0},{12,4},{16,24},{20,28},{24,16},{28,20},{1,9},{5... | collective-permute-start | bytes 1179656 | tf_op jit(solution)/shard_map/ppermute | solution.py:17
  194.7 8.5 %collective-permute-start.29 = (bf16[3,16,32,128]{3,2,1,0:T(8,128)(2,1)S(1)}, bf16[3,16,32,128]{3,2,1,0:T(8,128)(2,1)S(1)}, u32[]{:S(2)}, u32[]{:S(2)}) collective-permute-start(bf16[3,16,32,128]{3,2,1,0:T(8,128)(2,1)S(1)} %pad_maximum_fusion.10), channel_id=1, source_target_pairs={{0,16},{4,20},{8,24},{12,28},{16,0},{20,4},{24,8},{28,12},{1,17},{... | collective-permute-start | bytes 1179656 | tf_op jit(solution)/shard_map/ppermute | solution.py:17
  195.3 8.1 %copy-start.23 = (bf16[192,1792]{1,0:T(8,128)(2,1)S(1)}, bf16[192,1792]{1,0:T(8,128)(2,1)}, u32[]{:S(2)}) copy-start(bf16[192,1792]{1,0:T(8,128)(2,1)} %copy-done.22) | copy-start | bytes 2064388
  195.3 8.1 %copy-start.25 = (bf16[192,1792]{1,0:T(8,128)(2,1)S(1)}, bf16[192,1792]{1,0:T(8,128)(2,1)}, u32[]{:S(2)}) copy-start(bf16[192,1792]{1,0:T(8,128)(2,1)} %copy-done.24) | copy-start | bytes 2064388
  203.3 5.3 %collective-permute-start.31 = (bf16[4,1,16,32,256]{4,3,2,1,0:T(8,128)(2,1)S(1)}, bf16[4,1,16,32,256]{4,3,2,1,0:T(8,128)(2,1)S(1)}, u32[]{:S(2)}, u32[]{:S(2)}) collective-permute-start(bf16[4,1,16,32,256]{4,3,2,1,0:T(8,128)(2,1)S(1)} %maximum_bitcast_fusion.1.refs_0_), channel_id=1, source_target_pairs={{0,4},{4,0},{8,12},{12,8},{16,20},{20,16},{24,28},{28,24},{1,5},{5... | collective-permute-start | bytes 3145736 | tf_op jit(solution)/shard_map/ppermute | solution.py:17
  (11 other events, 13.3 us)

commit v5 on v4

--- a/solution.py
+++ b/solution.py
@@ -10,7 +10,7 @@
 F32 = jnp.float32
 BF16 = jnp.bfloat16
 COST = pl.CostEstimate(flops=1, bytes_accessed=1, transcendentals=0)
-VMEM_LIMIT = 20 * 1024 * 1024
+VMEM_LIMIT = 16 * 1024 * 1024
 
 
 def swap(value, axis, mask):
@@ -220,14 +220,17 @@
             num_scalar_prefetch=1,
             grid=(n_blocks,),
             in_specs=[
-                whole,
+                pl.BlockSpec((tok, ff), lambda j, *_: (0, 0), pipeline_mode=pl.Buffered(1)),
                 column,
                 low,
                 low,
                 pl.BlockSpec((block, rank), lambda j, *_: (j, 0)),
                 pl.BlockSpec((rank, block), lambda j, *_: (0, j)),
             ]
-            + [pl.BlockSpec(s.shape, lambda j, *_: (0, 0)) for s in sources]
+            + [
+                pl.BlockSpec(s.shape, lambda j, *_: (0, 0), pipeline_mode=pl.Buffered(1))
+                for s in sources
+            ]
             + piece_specs(pieces, 0, n_levels),
             out_specs=[column, whole],
             scratch_shapes=[w_scratch(pieces, n_levels, shards)]
@@ -433,7 +436,7 @@
         return (value.astype(F32) + other.astype(F32)).astype(BF16)
 
     cuts = [ff * quarter // 4 for quarter in range(5)]
-    both = swap(after(jnp.stack([hidden, cotangent]), factors), "dp", 1)
+    both = swap(jnp.stack([after(hidden, factors), cotangent]), "dp", 1)
     remote, ready = [], []
     for number, (start, stop) in enumerate(zip(cuts, cuts[1:])):
         part = after(hidden[:, start:stop], *ready, *([both] if ready else []))
@@ -476,7 +479,7 @@
     keep, send = block_grads(pos, after(cotangent, *sent[0]), remote, n_blocks, shards, scale)
     crossed = swap(send, "dp", 1)
     grads_local, received = scatter_sum(
-        [kept], shards, gathered + remote[3][1] + sent[0], returned[0] + sent[1] + [keep]
+        [kept], shards, gathered + remote[2][1] + sent[0], returned[0] + sent[1] + [keep]
     )
     mixed_rows, grad_in = rows_terms(
         pos, hidden, after(cotangent, *returned[0], crossed), factor, back, low_left, low_right, remote,

time: 212 us -> 211 us (level)
    unnamed x54 -> x50, local copies, waits for them, and re-layouts: 8.25 us -> 6.69 us
  transfers between devices with their start and end apart: 32 -> 32, of which waited for: 17 -> 18; matrix products, arithmetic and copies ran while one was open for 9% -> 9% of each run, Pallas kernels for 20% -> 20%
where the time goes in v5:
time: 211 us; the launch traced here: 210 us
  waiting for transfers between devices  93.3 us (44%)
  Pallas kernels  49.1 us (23%)
  starting transfers between devices  38 us (18%)
  other arithmetic  14.5 us (7%)
  local copies, waits for them, and re-layouts  12.6 us (6%)
    ppermute x32, waiting for transfers between devices, swap(): lax.ppermute(value, axis, [(i, i ^ mask) for i in range(lax.axis_size(axi...  93.3 us
    ppermute x32, starting transfers between devices, swap(): lax.ppermute(value, axis, [(i, i ^ mask) for i in range(lax.axis_size(axi...  38 us
    pallas_call x1, Pallas kernels, rows_terms(): pl.pallas_call(functools.partial(rows_kernel, pieces, distances, parts),...  16.4 us
    pallas_call x1, Pallas kernels, pair_grads(): pl.pallas_call(functools.partial(pair_kernel, distances, shards, scale),...  13.6 us
    pallas_call x3, Pallas kernels, back_terms(): pl.pallas_call(functools.partial(back_kernel, pieces, n_levels), grid_spe...  11.9 us
    unnamed x50, local copies, waits for them, and re-layouts  6.69 us
    pallas_call x1, Pallas kernels, block_grads(): pl.pallas_call(functools.partial(grads_kernel, n_parts, n_levels, shards,...  4.45 us
  transfers between devices with their start and end apart: 32, of which 18 were waited for; matrix products, arithmetic and copies ran while one was open for 9% of the time, Pallas kernels for 20%

profile of v5, /device:TPU:0, one launch (start us, length us, event | category | flops | bytes accessed | tf_op | source)
XLA Modules:
  0.0 210.0 jit_solution(9822586807189975193)
XLA Ops:
  0.7 2.3 %pad_maximum_fusion.1 = bf16[2,192,4096]{2,1,0:T(8,128)(2,1)S(1)} fusion(bf16[1,192,4096]{2,1,0:T(8,128)(2,1)} %bitcast.99, bf16[1,192,4096]{2,1,0:T(8,128)(2,1)} %bitcast.100), kind=kLoop, calls=%fused_computation.2 | loop fusion | flops 1572864 | bytes 6291456 | tf_op jit(solution)/shard_map/stack | solution.py:439
  3.5 2.6 %collective-permute-start.6 = (bf16[7,16,32,256]{3,2,1,0:T(8,128)(2,1)S(1)}, bf16[7,16,32,256]{3,2,1,0:T(8,128)(2,1)S(1)}, u32[]{:S(2)}, u32[]{:S(2)}) collective-permute-start(bf16[7,16,32,256]{3,2,1,0:T(8,128)(2,1)S(1)} %copy-done.19), channel_id=1, source_target_pairs={{0,16},{4,20},{8,24},{12,28},{16,0},{20,4},{24,8},{28,12},{1,17},{... | collective-permute-start | bytes 5505032 | tf_op jit(solution)/shard_map/ppermute | solution.py:17
  6.1 1.5 collective-permute-start
  8.9 1.0 fusion.7
  9.9 1.6 collective-permute-start.1
  11.6 2.6 %collective-permute-start.2 = (bf16[192,1024]{1,0:T(8,128)(2,1)S(1)}, bf16[192,1024]{1,0:T(8,128)(2,1)S(1)}, u32[]{:S(2)}, u32[]{:S(2)}) collective-permute-start(bf16[192,1024]{1,0:T(8,128)(2,1)S(1)} %get-tuple-element.112), channel_id=1, source_target_pairs={{0,2},{1,3},{2,0},{3,1},{4,6},{5,7},{6,4},{7,5},{8,10},{9,11},{10,... | collective-permute-start | bytes 1179656 | tf_op jit(solution)/shard_map/ppermute | solution.py:17
  14.2 17.3 %collective-permute-done.1.refs_4_.refs_0_ = bf16[192,1280]{1,0:T(8,128)(2,1)S(1)} collective-permute-done((bf16[192,1280]{1,0:T(8,128)(2,1)S(1)}, bf16[192,1280]{1,0:T(8,128)(2,1)S(1)}, u32[]{:S(2)}, u32[]{:S(2)}) %collective-permute-start.1) | collective-permute-done | bytes 491552 | tf_op jit(solution)/shard_map/ppermute | solution.py:17
  32.3 1.8 collective-permute-start.5
  34.1 2.5 %collective-permute-start.4 = (bf16[192,1024]{1,0:T(8,128)(2,1)S(1)}, bf16[192,1024]{1,0:T(8,128)(2,1)S(1)}, u32[]{:S(2)}, u32[]{:S(2)}) collective-permute-start(bf16[192,1024]{1,0:T(8,128)(2,1)S(1)} %get-tuple-element.48), channel_id=1, source_target_pairs={{0,1},{1,0},{2,3},{3,2},{4,5},{5,4},{6,7},{7,6},{8,9},{9,8},{10,11... | collective-permute-start | bytes 1179656 | tf_op jit(solution)/shard_map/ppermute | solution.py:17
  36.5 11.7 %collective-permute-done = bf16[7,16,32,256]{3,2,1,0:T(8,128)(2,1)S(1)} collective-permute-done((bf16[7,16,32,256]{3,2,1,0:T(8,128)(2,1)S(1)}, bf16[7,16,32,256]{3,2,1,0:T(8,128)(2,1)S(1)}, u32[]{:S(2)}, u32[]{:S(2)}) %collective-permute-start) | collective-permute-done | bytes 1835040 | tf_op jit(solution)/shard_map/ppermute | solution.py:17
  48.2 1.1 slice.299
  49.3 1.1 slice.301
  50.4 1.8 collective-permute-done.4.refs_6_.refs_2_
  53.0 3.0 %collective-permute-done.5.refs_7_.refs_3_ = bf16[192,1280]{1,0:T(8,128)(2,1)S(1)} collective-permute-done((bf16[192,1280]{1,0:T(8,128)(2,1)S(1)}, bf16[192,1280]{1,0:T(8,128)(2,1)S(1)}, u32[]{:S(2)}, u32[]{:S(2)}) %collective-permute-start.5) | collective-permute-done | bytes 491552 | tf_op jit(solution)/shard_map/ppermute | solution.py:17
  56.8 3.0 %pad_maximum_fusion.refs_0_.refs_8_ = bf16[3,7,16,32,256]{4,3,2,1,0:T(8,128)(2,1)} fusion(bf16[1,7,16,32,256]{4,3,2,1,0:T(8,128)(2,1)S(1)} %bitcast.103, bf16[1,7,16,32,256]{4,3,2,1,0:T(8,128)(2,1)S(1)} %bitcast.104, bf16[1,7,16,32,256]{4,3,2,1,0:T(8,128)(2,1)S(1)} %bitcast.106), kind=kLoop, calls=%fused_computation | loop fusion | flops 5505024 | bytes 11010048 | tf_op jit(solution)/shard_map/stack | solution.py:298
  61.8 3.2 %collective-permute-start.12 = (bf16[192,1024]{1,0:T(8,128)(2,1)}, bf16[192,1024]{1,0:T(8,128)(2,1)}, u32[]{:S(2)}, u32[]{:S(2)}) collective-permute-start(bf16[192,1024]{1,0:T(8,128)(2,1)} %get-tuple-element.56), channel_id=1, source_target_pairs={{0,2},{1,3},{2,0},{3,1},{4,6},{5,7},{6,4},{7,5},{8,10},{9,11},{10,... | collective-permute-start | bytes 1179656 | tf_op jit(solution)/shard_map/ppermute | solution.py:17
  65.1 1.9 copy-done.3
  67.0 0.9 copy-done.15
  67.9 0.9 copy-done.18
  68.8 13.6 %shard_map.92 = bf16[4,6,16,32,256]{4,3,2,1,0:T(8,128)(2,1)S(1)} custom-call(s32[1]{0:T(128)} %bitcast.pos_ref, bf16[192,4096]{1,0:T(8,128)(2,1)S(1)} %copy-done.1, bf16[192,4096]{1,0:T(8,128)(2,1)S(1)} %copy-done, bf16[192,256]{1,0:T(8,128)(2,1)S(1)} %copy-done.15, bf16[2,192,4096]{2,1,0:T(8,128)(2,1)S(1)} %copy-done.3, ...), custom_call_target="tpu_custom_call" | custom-call | flops 1 | bytes 1 | tf_op jit(solution)/shard_map/pallas_call | solution.py:132
  82.4 1.1 collective-permute-done.8
  83.7 1.8 maximum_bitcast_fusion.refs_1_.refs_9_
  85.6 1.1 slice_bitcast_fusion.2
  86.9 3.2 %collective-permute-start.15 = (bf16[192,1024]{1,0:T(8,128)(2,1)S(1)}, bf16[192,1024]{1,0:T(8,128)(2,1)S(1)}, u32[]{:S(2)}, u32[]{:S(2)}) collective-permute-start(bf16[192,1024]{1,0:T(8,128)(2,1)S(1)} %copy-done.24), channel_id=1, source_target_pairs={{0,2},{1,3},{2,0},{3,1},{4,6},{5,7},{6,4},{7,5},{8,10},{9,11},{10,... | collective-permute-start | bytes 1179656 | tf_op jit(solution)/shard_map/ppermute | solution.py:17
  90.6 5.1 %shard_map.93 = (bf16[192,1792]{1,0:T(8,128)(2,1)S(1)}, bf16[192,1792]{1,0:T(8,128)(2,1)S(1)}) custom-call(s32[1]{0:T(128)} %bitcast.pos_ref, bf16[192,4096]{1,0:T(8,128)(2,1)S(1)} %copy-done, bf16[3,7,16,32,256]{4,3,2,1,0:T(8,128)(2,1)} %pad_maximum_fusion.refs_0_.refs_8_, bf16[1,7,16,32,256]{4,3,2,1,0:T(8,128)(2,1)S(1)} %maximum_bitcast_fusion.refs_1_.refs_9_, ...), custom_call_target="tpu_custom_call" | custom-call | flops 1 | bytes 1 | tf_op jit(solution)/shard_map/pallas_call | solution.py:257
  95.8 10.9 %collective-permute-done.14.refs_10_.refs_6_ = bf16[192,1024]{1,0:T(8,128)(2,1)S(1)} collective-permute-done((bf16[192,1024]{1,0:T(8,128)(2,1)S(1)}, bf16[192,1024]{1,0:T(8,128)(2,1)S(1)}, u32[]{:S(2)}, u32[]{:S(2)}) %collective-permute-start.14) | collective-permute-done | bytes 393248 | tf_op jit(solution)/shard_map/ppermute | solution.py:17
  106.6 1.4 collective-permute-done.15.refs_11_.refs_7_
  108.1 4.5 %shard_map.94 = (bf16[4,2,4,4,32,256]{5,4,3,2,1,0:T(8,128)(2,1)S(1)}, bf16[4,2,4,4,32,256]{5,4,3,2,1,0:T(8,128)(2,1)S(1)}) custom-call(s32[1]{0:T(128)} %bitcast.pos_ref, bf16[192,4096]{1,0:T(8,128)(2,1)S(1)} %copy-done, bf16[192,4096]{1,0:T(8,128)(2,1)S(1)} %copy-done, bf16[192,4096]{1,0:T(8,128)(2,1)S(1)} %copy-done, bf16[192,4096]{1,0:T(8,128)(2,1)S(1)} %copy-done, ...), custom_call_target="tpu_custom_call" | custom-call | flops 1 | bytes 1 | tf_op jit(solution)/shard_map/pallas_call | solution.py:76
  112.9 1.6 collective-permute-start.23
  115.3 2.7 %collective-permute-start.17 = (bf16[192,1792]{1,0:T(8,128)(2,1)S(1)}, bf16[192,1792]{1,0:T(8,128)(2,1)S(1)}, u32[]{:S(2)}, u32[]{:S(2)}) collective-permute-start(bf16[192,1792]{1,0:T(8,128)(2,1)S(1)} %get-tuple-element.62), channel_id=1, source_target_pairs={{0,2},{1,3},{2,0},{3,1},{4,6},{5,7},{6,4},{7,5},{8,10},{9,11},{10,... | collective-permute-start | bytes 2064392 | tf_op jit(solution)/shard_map/ppermute | solution.py:17
  118.0 2.9 %shard_map.97 = (bf16[192,1024]{1,0:T(8,128)(2,1)S(1)}, bf16[192,1024]{1,0:T(8,128)(2,1)S(1)}) custom-call(s32[1]{0:T(128)} %bitcast.pos_ref, bf16[192,4096]{1,0:T(8,128)(2,1)S(1)} %copy-done, bf16[3,7,16,32,256]{4,3,2,1,0:T(8,128)(2,1)} %pad_maximum_fusion.refs_0_.refs_8_, bf16[1,7,16,32,256]{4,3,2,1,0:T(8,128)(2,1)S(1)} %maximum_bitcast_fusion.refs_1_.refs_9_, ...), custom_call_target="tpu_custom_call" | custom-call | flops 1 | bytes 1 | tf_op jit(solution)/shard_map/pallas_call | solution.py:257
  120.9 3.8 %shard_map.96 = (bf16[192,1280]{1,0:T(8,128)(2,1)S(1)}, bf16[192,1280]{1,0:T(8,128)(2,1)S(1)}) custom-call(s32[1]{0:T(128)} %bitcast.pos_ref, bf16[192,4096]{1,0:T(8,128)(2,1)S(1)} %copy-done, bf16[3,7,16,32,256]{4,3,2,1,0:T(8,128)(2,1)} %pad_maximum_fusion.refs_0_.refs_8_, bf16[1,7,16,32,256]{4,3,2,1,0:T(8,128)(2,1)S(1)} %maximum_bitcast_fusion.refs_1_.refs_9_, ...), custom_call_target="tpu_custom_call" | custom-call | flops 1 | bytes 1 | tf_op jit(solution)/shard_map/pallas_call | solution.py:257
  124.9 21.9 %collective-permute-done.16 = bf16[192,1792]{1,0:T(8,128)(2,1)S(1)} collective-permute-done((bf16[192,1792]{1,0:T(8,128)(2,1)S(1)}, bf16[192,1792]{1,0:T(8,128)(2,1)S(1)}, u32[]{:S(2)}, u32[]{:S(2)}) %collective-permute-start.16) | collective-permute-done | bytes 688160 | tf_op jit(solution)/shard_map/ppermute | solution.py:17
  146.8 1.2 collective-permute-done.17
  148.4 2.6 %collective-permute-start.20 = (bf16[192,1280]{1,0:T(8,128)(2,1)S(1)}, bf16[192,1280]{1,0:T(8,128)(2,1)}, u32[]{:S(2)}, u32[]{:S(2)}) collective-permute-start(bf16[192,1280]{1,0:T(8,128)(2,1)S(1)} %get-tuple-element.72), channel_id=1, source_target_pairs={{0,2},{1,3},{2,0},{3,1},{4,6},{5,7},{6,4},{7,5},{8,10},{9,11},{10,... | collective-permute-start | bytes 1474568 | tf_op jit(solution)/shard_map/ppermute | solution.py:17
  151.4 1.6 collective-permute-start.24
  153.6 16.4 %shard_map.95 = (bf16[192,4096]{1,0:T(8,128)(2,1)}, f32[192,4096]{1,0:T(8,128)S(1)}) custom-call(s32[1]{0:T(128)} %bitcast.pos_ref, bf16[192,4096]{1,0:T(8,128)(2,1)S(1)} %copy-done.1, bf16[192,4096]{1,0:T(8,128)(2,1)S(1)} %copy-done, bf16[192,128]{1,0:T(8,128)(2,1)S(1)} %get-tuple-element.126.fac_ref, bf16[192,128]{1,0:T(8,128)(2,1)S(1)} %get-tuple-element.125.back_ref, ...), custom_call_target="tpu_custom_call" | custom-call | flops 1 | bytes 1 | tf_op jit(solution)/shard_map/pallas_call | solution.py:217
  172.2 0.9 collective-permute-start.27
  173.0 1.1 collective-permute-start.28
  174.3 2.7 %collective-permute-start.22 = (bf16[192,1024]{1,0:T(8,128)(2,1)S(1)}, bf16[192,1024]{1,0:T(8,128)(2,1)S(1)}, u32[]{:S(2)}, u32[]{:S(2)}) collective-permute-start(bf16[192,1024]{1,0:T(8,128)(2,1)S(1)} %get-tuple-element.75), channel_id=1, source_target_pairs={{0,2},{1,3},{2,0},{3,1},{4,6},{5,7},{6,4},{7,5},{8,10},{9,11},{10,... | collective-permute-start | bytes 1179656 | tf_op jit(solution)/shard_map/ppermute | solution.py:17
  176.9 12.5 %collective-permute-done.27 = bf16[6,16,32,128]{3,2,1,0:T(8,128)(2,1)S(1)} collective-permute-done((bf16[6,16,32,128]{3,2,1,0:T(8,128)(2,1)S(1)}, bf16[6,16,32,128]{3,2,1,0:T(8,128)(2,1)S(1)}, u32[]{:S(2)}, u32[]{:S(2)}) %collective-permute-start.27) | collective-permute-done | bytes 786464 | tf_op jit(solution)/shard_map/ppermute | solution.py:17
  189.4 0.8 collective-permute-done.28
  191.1 1.3 collective-permute-done.22
  192.4 1.4 collective-permute-start.30
  194.6 6.5 %collective-permute-done.30 = bf16[3,16,32,128]{3,2,1,0:T(8,128)(2,1)S(1)} collective-permute-done((bf16[3,16,32,128]{3,2,1,0:T(8,128)(2,1)S(1)}, bf16[3,16,32,128]{3,2,1,0:T(8,128)(2,1)S(1)}, u32[]{:S(2)}, u32[]{:S(2)}) %collective-permute-start.30) | collective-permute-done | bytes 393248 | tf_op jit(solution)/shard_map/ppermute | solution.py:17
  202.0 2.5 %add_convert_fusion = bf16[192,4096]{1,0:T(8,128)(2,1)} fusion(f32[192,4096]{1,0:T(8,128)S(1)} %get-tuple-element.67, bf16[192,1024]{1,0:T(8,128)(2,1)S(1)} %collective-permute-done.21, bf16[192,1280]{1,0:T(8,128)(2,1)} %collective-permute-done.19, bf16[192,1792]{1,0:T(8,128)(2,1)S(1)} %copy-done.21, bf16[192,1024]{1,0:T(8,128)(2,1)S(1)} %collective-permute-done.22, ...), kind=kLoop, calls=%fused_computation.3 | loop fusion | flops 11796480 | bytes 7864320 | tf_op jit(solution)/shard_map/convert_element_type | solution.py:507
  205.1 2.2 %maximum_maximum_fusion = f32[7,16,32,256]{3,2,1,0:T(8,128)} fusion(f32[2,16,32,128]{3,2,1,0:T(8,128)S(1)} %get-tuple-element.114, f32[5,16,32,128]{3,2,1,0:T(8,128)S(1)} %slice.343, f32[2,16,32,128]{3,2,1,0:T(8,128)S(1)} %get-tuple-element.113, f32[5,16,32,128]{3,2,1,0:T(8,128)S(1)} %slice.315), kind=kLoop, calls=%fused_computation.1 | loop fusion | flops 2752512 | bytes 7340032 | tf_op jit(solution)/shard_map/concatenate | solution.py:498
  207.3 2.7 %shard_map.98 = (f32[4096,128]{1,0:T(8,128)}, f32[128,4096]{1,0:T(8,128)}) custom-call(s32[1]{0:T(128)} %bitcast.pos_ref, bf16[4,1,16,32,256]{4,3,2,1,0:T(8,128)(2,1)S(1)} %maximum_bitcast_fusion.1.refs_0_, bf16[4,1,16,32,256]{4,3,2,1,0:T(8,128)(2,1)S(1)} %collective-permute-done.31.refs_1_), custom_call_target="tpu_custom_call" | custom-call | flops 1 | bytes 1 | tf_op jit(solution)/shard_map/pallas_call | solution.py:385
  (120 shorter events, 15.4 us)
Async XLA Ops:
  0.6 7.0 %copy-start = (bf16[192,4096]{1,0:T(8,128)(2,1)S(1)}, bf16[192,4096]{1,0:T(8,128)(2,1)}, u32[]{:S(2)}) copy-start(bf16[192,4096]{1,0:T(8,128)(2,1)} %cot_ref.6) | copy-start | bytes 4718596
  0.7 7.0 %copy-start.4 = (bf16[128,4096]{1,0:T(8,128)(2,1)S(1)}, bf16[128,4096]{1,0:T(8,128)(2,1)}, u32[]{:S(2)}) copy-start(bf16[128,4096]{1,0:T(8,128)(2,1)} %right_ref.1) | copy-start | bytes 3145732
  3.0 5.3 %copy-start.1 = (bf16[192,4096]{1,0:T(8,128)(2,1)S(1)}, bf16[192,4096]{1,0:T(8,128)(2,1)}, u32[]{:S(2)}) copy-start(bf16[192,4096]{1,0:T(8,128)(2,1)} %hid_ref.1) | copy-start | bytes 4718596
  3.0 5.3 %copy-start.6 = (bf16[4096,128]{1,0:T(8,128)(2,1)S(1)}, bf16[4096,128]{1,0:T(8,128)(2,1)}, u32[]{:S(2)}) copy-start(bf16[4096,128]{1,0:T(8,128)(2,1)} %left_ref.1) | copy-start | bytes 3145732
  3.0 29.3 %collective-permute-start.3 = (bf16[2,192,4096]{2,1,0:T(8,128)(2,1)S(1)}, bf16[2,192,4096]{2,1,0:T(8,128)(2,1)S(1)}, u32[]{:S(2)}, u32[]{:S(2)}) collective-permute-start(bf16[2,192,4096]{2,1,0:T(8,128)(2,1)S(1)} %pad_maximum_fusion.1), channel_id=1, source_target_pairs={{0,4},{4,0},{8,12},{12,8},{16,20},{20,16},{24,28},{28,24},{1,5},{5... | collective-permute-start | bytes 9437192 | tf_op jit(solution)/shard_map/ppermute | solution.py:17
  3.5 45.8 %collective-permute-start.6 = (bf16[7,16,32,256]{3,2,1,0:T(8,128)(2,1)S(1)}, bf16[7,16,32,256]{3,2,1,0:T(8,128)(2,1)S(1)}, u32[]{:S(2)}, u32[]{:S(2)}) collective-permute-start(bf16[7,16,32,256]{3,2,1,0:T(8,128)(2,1)S(1)} %copy-done.19), channel_id=1, source_target_pairs={{0,16},{4,20},{8,24},{12,28},{16,0},{20,4},{24,8},{28,12},{1,17},{... | collective-permute-start | bytes 5505032 | tf_op jit(solution)/shard_map/ppermute | solution.py:17
  6.1 42.1 %collective-permute-start = (bf16[7,16,32,256]{3,2,1,0:T(8,128)(2,1)S(1)}, bf16[7,16,32,256]{3,2,1,0:T(8,128)(2,1)S(1)}, u32[]{:S(2)}, u32[]{:S(2)}) collective-permute-start(bf16[7,16,32,256]{3,2,1,0:T(8,128)(2,1)S(1)} %copy-done.19), channel_id=1, source_target_pairs={{0,8},{4,12},{8,0},{12,4},{16,24},{20,28},{24,16},{28,20},{1,9},{5... | collective-permute-start | bytes 5505032 | tf_op jit(solution)/shard_map/ppermute | solution.py:17
  9.9 21.5 %collective-permute-start.1 = (bf16[192,1280]{1,0:T(8,128)(2,1)S(1)}, bf16[192,1280]{1,0:T(8,128)(2,1)S(1)}, u32[]{:S(2)}, u32[]{:S(2)}) collective-permute-start(bf16[192,1280]{1,0:T(8,128)(2,1)S(1)} %pad_maximum_fusion.8), channel_id=1, source_target_pairs={{0,1},{1,0},{2,3},{3,2},{4,5},{5,4},{6,7},{7,6},{8,9},{9,8},{10,11... | collective-permute-start | bytes 1474568 | tf_op jit(solution)/shard_map/ppermute | solution.py:17
  11.6 20.7 %collective-permute-start.2 = (bf16[192,1024]{1,0:T(8,128)(2,1)S(1)}, bf16[192,1024]{1,0:T(8,128)(2,1)S(1)}, u32[]{:S(2)}, u32[]{:S(2)}) collective-permute-start(bf16[192,1024]{1,0:T(8,128)(2,1)S(1)} %get-tuple-element.112), channel_id=1, source_target_pairs={{0,2},{1,3},{2,0},{3,1},{4,6},{5,7},{6,4},{7,5},{8,10},{9,11},{10,... | collective-permute-start | bytes 1179656 | tf_op jit(solution)/shard_map/ppermute | solution.py:17
  32.3 18.2 %copy-start.2 = (bf16[2,192,4096]{2,1,0:T(8,128)(2,1)}, bf16[2,192,4096]{2,1,0:T(8,128)(2,1)S(1)}, u32[]{:S(2)}) copy-start(bf16[2,192,4096]{2,1,0:T(8,128)(2,1)S(1)} %collective-permute-done.3.refs_3_.refs_4_) | copy-start | bytes 9437188
  32.3 23.6 %collective-permute-start.5 = (bf16[192,1280]{1,0:T(8,128)(2,1)S(1)}, bf16[192,1280]{1,0:T(8,128)(2,1)S(1)}, u32[]{:S(2)}, u32[]{:S(2)}) collective-permute-start(bf16[192,1280]{1,0:T(8,128)(2,1)S(1)} %pad_maximum_fusion.9), channel_id=1, source_target_pairs={{0,2},{1,3},{2,0},{3,1},{4,6},{5,7},{6,4},{7,5},{8,10},{9,11},{10,... | collective-permute-start | bytes 1474568 | tf_op jit(solution)/shard_map/ppermute | solution.py:17
  34.1 18.1 %collective-permute-start.4 = (bf16[192,1024]{1,0:T(8,128)(2,1)S(1)}, bf16[192,1024]{1,0:T(8,128)(2,1)S(1)}, u32[]{:S(2)}, u32[]{:S(2)}) collective-permute-start(bf16[192,1024]{1,0:T(8,128)(2,1)S(1)} %get-tuple-element.48), channel_id=1, source_target_pairs={{0,1},{1,0},{2,3},{3,2},{4,5},{5,4},{6,7},{7,6},{8,9},{9,8},{10,11... | collective-permute-start | bytes 1179656 | tf_op jit(solution)/shard_map/ppermute | solution.py:17
  56.8 3.0 %copy-start.14 = (bf16[192,256]{1,0:T(8,128)(2,1)}, bf16[192,256]{1,0:T(8,128)(2,1)S(1)}, u32[]{:S(2)}) copy-start(bf16[192,256]{1,0:T(8,128)(2,1)S(1)} %add_convert_fusion.7.refs_2_) | copy-start | bytes 294916
  56.8 3.0 %collective-permute-start.9 = (bf16[192,256]{1,0:T(8,128)(2,1)S(1)}, bf16[192,256]{1,0:T(8,128)(2,1)S(1)}, u32[]{:S(2)}, u32[]{:S(2)}) collective-permute-start(bf16[192,256]{1,0:T(8,128)(2,1)S(1)} %add_convert_fusion.7.refs_2_), channel_id=1, source_target_pairs={{0,4},{4,0},{8,12},{12,8},{16,20},{20,16},{24,28},{28,24},{1,5},{5... | collective-permute-start | bytes 294920 | tf_op jit(solution)/shard_map/ppermute | solution.py:17
  60.4 30.2 %collective-permute-start.10 = (bf16[3,7,16,32,256]{4,3,2,1,0:T(8,128)(2,1)}, bf16[3,7,16,32,256]{4,3,2,1,0:T(8,128)(2,1)}, u32[]{:S(2)}, u32[]{:S(2)}) collective-permute-start(bf16[3,7,16,32,256]{4,3,2,1,0:T(8,128)(2,1)} %pad_maximum_fusion.refs_0_.refs_8_), channel_id=1, source_target_pairs={{0,4},{4,0},{8,12},{12,8},{16,20},{20,16},{24,28},{28,24},{1,5},{5... | collective-permute-start | bytes 16515080 | tf_op jit(solution)/shard_map/ppermute | solution.py:17
  60.9 22.6 %collective-permute-start.8 = (bf16[7,16,32,128]{3,2,1,0:T(8,128)(2,1)}, bf16[7,16,32,128]{3,2,1,0:T(8,128)(2,1)}, u32[]{:S(2)}, u32[]{:S(2)}) collective-permute-start(bf16[7,16,32,128]{3,2,1,0:T(8,128)(2,1)} %slice.301), channel_id=1, source_target_pairs={{0,8},{4,12},{8,0},{12,4},{16,24},{20,28},{24,16},{28,20},{1,9},{5... | collective-permute-start | bytes 2752520 | tf_op jit(solution)/shard_map/ppermute | solution.py:17
  61.4 22.3 %collective-permute-start.7 = (bf16[7,16,32,128]{3,2,1,0:T(8,128)(2,1)}, bf16[7,16,32,128]{3,2,1,0:T(8,128)(2,1)}, u32[]{:S(2)}, u32[]{:S(2)}) collective-permute-start(bf16[7,16,32,128]{3,2,1,0:T(8,128)(2,1)} %slice.299), channel_id=1, source_target_pairs={{0,16},{4,20},{8,24},{12,28},{16,0},{20,4},{24,8},{28,12},{1,17},{... | collective-permute-start | bytes 2752520 | tf_op jit(solution)/shard_map/ppermute | solution.py:17
  61.8 23.7 %collective-permute-start.11 = (bf16[192,1024]{1,0:T(8,128)(2,1)}, bf16[192,1024]{1,0:T(8,128)(2,1)}, u32[]{:S(2)}, u32[]{:S(2)}) collective-permute-start(bf16[192,1024]{1,0:T(8,128)(2,1)} %get-tuple-element.56), channel_id=1, source_target_pairs={{0,1},{1,0},{2,3},{3,2},{4,5},{5,4},{6,7},{7,6},{8,9},{9,8},{10,11... | collective-permute-start | bytes 1179656 | tf_op jit(solution)/shard_map/ppermute | solution.py:17
  61.8 23.7 %collective-permute-start.12 = (bf16[192,1024]{1,0:T(8,128)(2,1)}, bf16[192,1024]{1,0:T(8,128)(2,1)}, u32[]{:S(2)}, u32[]{:S(2)}) collective-permute-start(bf16[192,1024]{1,0:T(8,128)(2,1)} %get-tuple-element.56), channel_id=1, source_target_pairs={{0,2},{1,3},{2,0},{3,1},{4,6},{5,7},{6,4},{7,5},{8,10},{9,11},{10,... | collective-permute-start | bytes 1179656 | tf_op jit(solution)/shard_map/ppermute | solution.py:17
  85.5 5.0 %collective-permute-start.13 = (bf16[1,7,16,32,256]{4,3,2,1,0:T(8,128)(2,1)S(1)}, bf16[1,7,16,32,256]{4,3,2,1,0:T(8,128)(2,1)S(1)}, u32[]{:S(2)}, u32[]{:S(2)}) collective-permute-start(bf16[1,7,16,32,256]{4,3,2,1,0:T(8,128)(2,1)S(1)} %maximum_bitcast_fusion.refs_1_.refs_9_), channel_id=1, source_target_pairs={{0,4},{4,0},{8,12},{12,8},{16,20},{20,16},{24,28},{28,24},{1,5},{5... | collective-permute-start | bytes 5505032 | tf_op jit(solution)/shard_map/ppermute | solution.py:17
  86.9 19.8 %collective-permute-start.14 = (bf16[192,1024]{1,0:T(8,128)(2,1)S(1)}, bf16[192,1024]{1,0:T(8,128)(2,1)S(1)}, u32[]{:S(2)}, u32[]{:S(2)}) collective-permute-start(bf16[192,1024]{1,0:T(8,128)(2,1)S(1)} %copy-done.24), channel_id=1, source_target_pairs={{0,1},{1,0},{2,3},{3,2},{4,5},{5,4},{6,7},{7,6},{8,9},{9,8},{10,11... | collective-permute-start | bytes 1179656 | tf_op jit(solution)/shard_map/ppermute | solution.py:17
  86.9 21.1 %collective-permute-start.15 = (bf16[192,1024]{1,0:T(8,128)(2,1)S(1)}, bf16[192,1024]{1,0:T(8,128)(2,1)S(1)}, u32[]{:S(2)}, u32[]{:S(2)}) collective-permute-start(bf16[192,1024]{1,0:T(8,128)(2,1)S(1)} %copy-done.24), channel_id=1, source_target_pairs={{0,2},{1,3},{2,0},{3,1},{4,6},{5,7},{6,4},{7,5},{8,10},{9,11},{10,... | collective-permute-start | bytes 1179656 | tf_op jit(solution)/shard_map/ppermute | solution.py:17
  90.5 17.5 %copy-start.9 = (bf16[192,1280]{1,0:T(8,128)(2,1)S(1)}, bf16[192,1280]{1,0:T(8,128)(2,1)}, u32[]{:S(2)}) copy-start(bf16[192,1280]{1,0:T(8,128)(2,1)} %copy-done.8) | copy-start | bytes 1474564
  90.6 17.5 %copy-start.11 = (bf16[192,1280]{1,0:T(8,128)(2,1)S(1)}, bf16[192,1280]{1,0:T(8,128)(2,1)}, u32[]{:S(2)}) copy-start(bf16[192,1280]{1,0:T(8,128)(2,1)} %copy-done.10) | copy-start | bytes 1474564
  90.6 17.5 %copy-start.13 = (bf16[192,1024]{1,0:T(8,128)(2,1)S(1)}, bf16[192,1024]{1,0:T(8,128)(2,1)}, u32[]{:S(2)}) copy-start(bf16[192,1024]{1,0:T(8,128)(2,1)} %copy-done.12) | copy-start | bytes 1179652
  112.5 41.0 %collective-permute-start.18 = (bf16[4,2,16,32,256]{4,3,2,1,0:T(8,128)(2,1)S(1)}, bf16[4,2,16,32,256]{4,3,2,1,0:T(8,128)(2,1)S(1)}, u32[]{:S(2)}, u32[]{:S(2)}) collective-permute-start(bf16[4,2,16,32,256]{4,3,2,1,0:T(8,128)(2,1)S(1)} %bitcast.102), channel_id=1, source_target_pairs={{0,4},{4,0},{8,12},{12,8},{16,20},{20,16},{24,28},{28,24},{1,5},{5... | collective-permute-start | bytes 6291464 | tf_op jit(solution)/shard_map/ppermute | solution.py:17
  112.8 5.2 %copy-start.16 = (bf16[192,256]{1,0:T(8,128)(2,1)S(1)}, bf16[192,256]{1,0:T(8,128)(2,1)}, u32[]{:S(2)}) copy-start(bf16[192,256]{1,0:T(8,128)(2,1)} %copy-done.14) | copy-start | bytes 294916
  112.9 38.1 %collective-permute-start.23 = (bf16[2,6,16,32,128]{4,3,2,1,0:T(8,128)(2,1)S(1)}, bf16[2,6,16,32,128]{4,3,2,1,0:T(8,128)(2,1)S(1)}, u32[]{:S(2)}, u32[]{:S(2)}) collective-permute-start(bf16[2,6,16,32,128]{4,3,2,1,0:T(8,128)(2,1)S(1)} %pad_maximum_fusion.2), channel_id=1, source_target_pairs={{0,8},{4,12},{8,0},{12,4},{16,24},{20,28},{24,16},{28,20},{1,9},{5... | collective-permute-start | bytes 4718600 | tf_op jit(solution)/shard_map/ppermute | solution.py:17
  114.5 36.5 %collective-permute-start.25 = (bf16[2,6,16,32,128]{4,3,2,1,0:T(8,128)(2,1)S(1)}, bf16[2,6,16,32,128]{4,3,2,1,0:T(8,128)(2,1)S(1)}, u32[]{:S(2)}, u32[]{:S(2)}) collective-permute-start(bf16[2,6,16,32,128]{4,3,2,1,0:T(8,128)(2,1)S(1)} %pad_maximum_fusion.3), channel_id=1, source_target_pairs={{0,16},{4,20},{8,24},{12,28},{16,0},{20,4},{24,8},{28,12},{1,17},{... | collective-permute-start | bytes 4718600 | tf_op jit(solution)/shard_map/ppermute | solution.py:17
  115.0 31.8 %collective-permute-start.16 = (bf16[192,1792]{1,0:T(8,128)(2,1)S(1)}, bf16[192,1792]{1,0:T(8,128)(2,1)S(1)}, u32[]{:S(2)}, u32[]{:S(2)}) collective-permute-start(bf16[192,1792]{1,0:T(8,128)(2,1)S(1)} %get-tuple-element.60), channel_id=1, source_target_pairs={{0,1},{1,0},{2,3},{3,2},{4,5},{5,4},{6,7},{7,6},{8,9},{9,8},{10,11... | collective-permute-start | bytes 2064392 | tf_op jit(solution)/shard_map/ppermute | solution.py:17
  115.3 32.7 %collective-permute-start.17 = (bf16[192,1792]{1,0:T(8,128)(2,1)S(1)}, bf16[192,1792]{1,0:T(8,128)(2,1)S(1)}, u32[]{:S(2)}, u32[]{:S(2)}) collective-permute-start(bf16[192,1792]{1,0:T(8,128)(2,1)S(1)} %get-tuple-element.62), channel_id=1, source_target_pairs={{0,2},{1,3},{2,0},{3,1},{4,6},{5,7},{6,4},{7,5},{8,10},{9,11},{10,... | collective-permute-start | bytes 2064392 | tf_op jit(solution)/shard_map/ppermute | solution.py:17
  146.8 4.2 %copy-start.20 = (bf16[192,1792]{1,0:T(8,128)(2,1)}, bf16[192,1792]{1,0:T(8,128)(2,1)S(1)}, u32[]{:S(2)}) copy-start(bf16[192,1792]{1,0:T(8,128)(2,1)S(1)} %collective-permute-done.16) | copy-start | bytes 2064388
  148.0 2.9 %copy-start.22 = (bf16[192,1792]{1,0:T(8,128)(2,1)}, bf16[192,1792]{1,0:T(8,128)(2,1)S(1)}, u32[]{:S(2)}) copy-start(bf16[192,1792]{1,0:T(8,128)(2,1)S(1)} %collective-permute-done.17) | copy-start | bytes 2064388
  148.0 23.6 %collective-permute-start.19 = (bf16[192,1280]{1,0:T(8,128)(2,1)S(1)}, bf16[192,1280]{1,0:T(8,128)(2,1)}, u32[]{:S(2)}, u32[]{:S(2)}) collective-permute-start(bf16[192,1280]{1,0:T(8,128)(2,1)S(1)} %get-tuple-element.69), channel_id=1, source_target_pairs={{0,1},{1,0},{2,3},{3,2},{4,5},{5,4},{6,7},{7,6},{8,9},{9,8},{10,11... | collective-permute-start | bytes 1474568 | tf_op jit(solution)/shard_map/ppermute | solution.py:17
  148.4 5.2 %copy-start.5 = (bf16[128,4096]{1,0:T(8,128)(2,1)S(1)}, bf16[128,4096]{1,0:T(8,128)(2,1)}, u32[]{:S(2)}) copy-start(bf16[128,4096]{1,0:T(8,128)(2,1)} %right_ref.1) | copy-start | bytes 3145732
  148.4 5.2 %copy-start.7 = (bf16[4096,128]{1,0:T(8,128)(2,1)S(1)}, bf16[4096,128]{1,0:T(8,128)(2,1)}, u32[]{:S(2)}) copy-start(bf16[4096,128]{1,0:T(8,128)(2,1)} %left_ref.1) | copy-start | bytes 3145732
  148.4 23.8 %collective-permute-start.20 = (bf16[192,1280]{1,0:T(8,128)(2,1)S(1)}, bf16[192,1280]{1,0:T(8,128)(2,1)}, u32[]{:S(2)}, u32[]{:S(2)}) collective-permute-start(bf16[192,1280]{1,0:T(8,128)(2,1)S(1)} %get-tuple-element.72), channel_id=1, source_target_pairs={{0,2},{1,3},{2,0},{3,1},{4,6},{5,7},{6,4},{7,5},{8,10},{9,11},{10,... | collective-permute-start | bytes 1474568 | tf_op jit(solution)/shard_map/ppermute | solution.py:17
  151.4 19.1 %collective-permute-start.24 = (bf16[1,6,16,32,128]{4,3,2,1,0:T(8,128)(2,1)S(1)}, bf16[1,6,16,32,128]{4,3,2,1,0:T(8,128)(2,1)S(1)}, u32[]{:S(2)}, u32[]{:S(2)}) collective-permute-start(bf16[1,6,16,32,128]{4,3,2,1,0:T(8,128)(2,1)S(1)} %get-tuple-element.78), channel_id=1, source_target_pairs={{0,16},{4,20},{8,24},{12,28},{16,0},{20,4},{24,8},{28,12},{1,17},{... | collective-permute-start | bytes 2359304 | tf_op jit(solution)/shard_map/ppermute | solution.py:17
  153.0 17.7 %collective-permute-start.26 = (bf16[1,6,16,32,128]{4,3,2,1,0:T(8,128)(2,1)S(1)}, bf16[1,6,16,32,128]{4,3,2,1,0:T(8,128)(2,1)S(1)}, u32[]{:S(2)}, u32[]{:S(2)}) collective-permute-start(bf16[1,6,16,32,128]{4,3,2,1,0:T(8,128)(2,1)S(1)} %get-tuple-element.80), channel_id=1, source_target_pairs={{0,8},{4,12},{8,0},{12,4},{16,24},{20,28},{24,16},{28,20},{1,9},{5... | collective-permute-start | bytes 2359304 | tf_op jit(solution)/shard_map/ppermute | solution.py:17
  172.2 17.2 %collective-permute-start.27 = (bf16[6,16,32,128]{3,2,1,0:T(8,128)(2,1)S(1)}, bf16[6,16,32,128]{3,2,1,0:T(8,128)(2,1)S(1)}, u32[]{:S(2)}, u32[]{:S(2)}) collective-permute-start(bf16[6,16,32,128]{3,2,1,0:T(8,128)(2,1)S(1)} %get-tuple-element.81), channel_id=1, source_target_pairs={{0,8},{4,12},{8,0},{12,4},{16,24},{20,28},{24,16},{28,20},{1,9},{5... | collective-permute-start | bytes 2359304 | tf_op jit(solution)/shard_map/ppermute | solution.py:17
  173.0 17.2 %collective-permute-start.28 = (bf16[6,16,32,128]{3,2,1,0:T(8,128)(2,1)S(1)}, bf16[6,16,32,128]{3,2,1,0:T(8,128)(2,1)S(1)}, u32[]{:S(2)}, u32[]{:S(2)}) collective-permute-start(bf16[6,16,32,128]{3,2,1,0:T(8,128)(2,1)S(1)} %get-tuple-element.82), channel_id=1, source_target_pairs={{0,16},{4,20},{8,24},{12,28},{16,0},{20,4},{24,8},{28,12},{1,17},{... | collective-permute-start | bytes 2359304 | tf_op jit(solution)/shard_map/ppermute | solution.py:17
  174.2 16.9 %collective-permute-start.21 = (bf16[192,1024]{1,0:T(8,128)(2,1)S(1)}, bf16[192,1024]{1,0:T(8,128)(2,1)S(1)}, u32[]{:S(2)}, u32[]{:S(2)}) collective-permute-start(bf16[192,1024]{1,0:T(8,128)(2,1)S(1)} %get-tuple-element.73), channel_id=1, source_target_pairs={{0,1},{1,0},{2,3},{3,2},{4,5},{5,4},{6,7},{7,6},{8,9},{9,8},{10,11... | collective-permute-start | bytes 1179656 | tf_op jit(solution)/shard_map/ppermute | solution.py:17
  174.3 18.1 %collective-permute-start.22 = (bf16[192,1024]{1,0:T(8,128)(2,1)S(1)}, bf16[192,1024]{1,0:T(8,128)(2,1)S(1)}, u32[]{:S(2)}, u32[]{:S(2)}) collective-permute-start(bf16[192,1024]{1,0:T(8,128)(2,1)S(1)} %get-tuple-element.75), channel_id=1, source_target_pairs={{0,2},{1,3},{2,0},{3,1},{4,6},{5,7},{6,4},{7,5},{8,10},{9,11},{10,... | collective-permute-start | bytes 1179656 | tf_op jit(solution)/shard_map/ppermute | solution.py:17
  192.4 8.7 %collective-permute-start.30 = (bf16[3,16,32,128]{3,2,1,0:T(8,128)(2,1)S(1)}, bf16[3,16,32,128]{3,2,1,0:T(8,128)(2,1)S(1)}, u32[]{:S(2)}, u32[]{:S(2)}) collective-permute-start(bf16[3,16,32,128]{3,2,1,0:T(8,128)(2,1)S(1)} %pad_maximum_fusion.11), channel_id=1, source_target_pairs={{0,8},{4,12},{8,0},{12,4},{16,24},{20,28},{24,16},{28,20},{1,9},{5... | collective-permute-start | bytes 1179656 | tf_op jit(solution)/shard_map/ppermute | solution.py:17
  193.9 7.8 %collective-permute-start.29 = (bf16[3,16,32,128]{3,2,1,0:T(8,128)(2,1)S(1)}, bf16[3,16,32,128]{3,2,1,0:T(8,128)(2,1)S(1)}, u32[]{:S(2)}, u32[]{:S(2)}) collective-permute-start(bf16[3,16,32,128]{3,2,1,0:T(8,128)(2,1)S(1)} %pad_maximum_fusion.10), channel_id=1, source_target_pairs={{0,16},{4,20},{8,24},{12,28},{16,0},{20,4},{24,8},{28,12},{1,17},{... | collective-permute-start | bytes 1179656 | tf_op jit(solution)/shard_map/ppermute | solution.py:17
  194.6 7.5 %copy-start.21 = (bf16[192,1792]{1,0:T(8,128)(2,1)S(1)}, bf16[192,1792]{1,0:T(8,128)(2,1)}, u32[]{:S(2)}) copy-start(bf16[192,1792]{1,0:T(8,128)(2,1)} %copy-done.20) | copy-start | bytes 2064388
  194.6 7.5 %copy-start.23 = (bf16[192,1792]{1,0:T(8,128)(2,1)S(1)}, bf16[192,1792]{1,0:T(8,128)(2,1)}, u32[]{:S(2)}) copy-start(bf16[192,1792]{1,0:T(8,128)(2,1)} %copy-done.22) | copy-start | bytes 2064388
  201.9 5.4 %collective-permute-start.31 = (bf16[4,1,16,32,256]{4,3,2,1,0:T(8,128)(2,1)S(1)}, bf16[4,1,16,32,256]{4,3,2,1,0:T(8,128)(2,1)S(1)}, u32[]{:S(2)}, u32[]{:S(2)}) collective-permute-start(bf16[4,1,16,32,256]{4,3,2,1,0:T(8,128)(2,1)S(1)} %maximum_bitcast_fusion.1.refs_0_), channel_id=1, source_target_pairs={{0,4},{4,0},{8,12},{12,8},{16,20},{20,16},{24,28},{28,24},{1,5},{5... | collective-permute-start | bytes 3145736 | tf_op jit(solution)/shard_map/ppermute | solution.py:17
  (9 other events, 10.9 us)
